TPU v7x, 512 devices: a whole 4x8x8 slice. The times are simulated.
512 devices in a mesh: tm: 128 (over z_hi, y, x), space: 4 (over z_lo, core).
Axes of the slice: x: 4, y: 8, z: 8 (z_hi: 4, z_lo: 2; z = z_hi * 2 + z_lo), core: 2. Of those that a mesh axis runs over, the one named last changes fastest.
Arguments:
- patches: bfloat16 [256, 16, 16, 256], P('tm', 'space'), may hold values from -24 to 24
- stem_weight: bfloat16 [2304, 256], P('space'), may hold values from -0.125 to 0.125
- embed_weight: bfloat16 [256, 2048], P('space'), may hold values from -0.375 to 0.375
- frame_embed: bfloat16 [256, 2048], P('tm'), may hold values from -3 to 3
- attention_gain: bfloat16 [2048], replicated, may hold values from 0.5 to 1.5
- final_gain: bfloat16 [2048], replicated, may hold values from 0.5 to 1.5
- query_weight: bfloat16 [2048, 1024], P(None, 'space'), may hold values from -0.125 to 0.125
- key_weight: bfloat16 [2048, 1024], P(None, 'space'), may hold values from -0.125 to 0.125
- value_weight: bfloat16 [2048, 1024], P(None, 'space'), may hold values from -0.125 to 0.125
- output_weight: bfloat16 [1024, 2048], P('space'), may hold values from -0.1875 to 0.1875
- unembedding: bfloat16 [32768, 2048], P(('tm', 'space')), may hold values from -0.375 to 0.375
- rating_ids: int32 [5], replicated, may hold values from 0 to 32767
- target_score: int32 [1], replicated, may hold values from 1 to 5
Outputs:
- expected_score: float32 [1], replicated
- stem_gradient: float32 [589824], P(('tm', 'space'))
All inputs are finite; a program needn't handle non-finite values.
Results may differ from a plain program's by a relative error of at most 0.008.
Values may be sent and summed in bfloat16 or wider, within the bound.
No kernel may reach another device: no remote copies, remote signals or barrier semaphores. Data moves between devices by JAX's collectives and lax.ppermute only.
A program may use at most 128 MiB of HBM per device.

v0:
```python
import math

import jax
import jax.numpy as jnp
from jax import lax
from jax.sharding import PartitionSpec as P

HEAD = 128


epsilon = 1e-05
highest = lax.Precision.HIGHEST


def neighbourhoods(frames):
    count_rows = frames.shape[1]
    count_cols = frames.shape[2]
    padded = jnp.pad(frames, ((0, 0), (1, 1), (1, 1), (0, 0)))
    pieces = [
        padded[:, row_off : row_off + count_rows, col_off : col_off + count_cols, :]
        for row_off in range(3)
        for col_off in range(3)
    ]
    return jnp.concatenate(pieces, axis=-1)


def rms_scale(values):
    return lax.rsqrt(jnp.mean(values * values, axis=-1, keepdims=True) + epsilon)


def rms_back(values, gain, upstream):
    inverse_rms = rms_scale(values)
    unit_rows = values * inverse_rms
    gained = gain * upstream
    return inverse_rms * (gained - unit_rows * jnp.mean(gained * unit_rows, axis=-1, keepdims=True))


def attend(queries, key_rows, value_rows):
    factor = 1.0 / math.sqrt(queries.shape[-1])
    scores = (
        jnp.einsum("fih,gih->ifg", queries, key_rows, preferred_element_type=jnp.float32) * factor
    )
    exact_weights = jax.nn.softmax(scores, axis=-1)
    rounded_weights = exact_weights.astype(jnp.bfloat16)
    mixture = jnp.einsum(
        "ifg,gih->fih", rounded_weights, value_rows, preferred_element_type=jnp.float32
    )
    return (exact_weights, rounded_weights, mixture.astype(jnp.bfloat16))


def attend_back(queries, key_rows, value_rows, exact_weights, rounded_weights, grad_mixture):
    factor = 1.0 / math.sqrt(queries.shape[-1])
    grad_weights = jnp.einsum(
        "ih,gih->ig", grad_mixture, value_rows.astype(jnp.float32), precision=highest
    )
    column_mass = jnp.sum(rounded_weights.astype(jnp.float32), axis=1)
    grad_values = jnp.transpose(column_mass)[:, :, None] * grad_mixture[None, :, :]
    centred = grad_weights[:, None, :] - jnp.sum(
        exact_weights * grad_weights[:, None, :], axis=-1, keepdims=True
    )
    grad_scores = exact_weights * centred * factor
    grad_queries = jnp.einsum(
        "ifg,gih->fih", grad_scores, key_rows.astype(jnp.float32), precision=highest
    )
    grad_keys = jnp.einsum(
        "ifg,fih->gih", grad_scores, queries.astype(jnp.float32), precision=highest
    )
    return (
        grad_queries.astype(jnp.bfloat16),
        grad_keys.astype(jnp.bfloat16),
        grad_values.astype(jnp.bfloat16),
    )


def head_terms(pooled_total, rating_rows, final_gain, target_score, tokens):
    pooled_raw = pooled_total / tokens
    inverse_rms = lax.rsqrt(jnp.mean(pooled_raw * pooled_raw) + epsilon)
    unit_rows = pooled_raw * inverse_rms
    gain = final_gain.astype(jnp.float32)
    pooled = unit_rows * gain
    logits = jnp.dot(rating_rows, pooled, precision=highest)
    rating_probs = jax.nn.softmax(logits)
    ladder = jnp.arange(1, rating_rows.shape[0] + 1).astype(jnp.float32)
    expected = jnp.sum(rating_probs * ladder)
    target = (jnp.arange(rating_rows.shape[0]) == target_score[0] - 1).astype(jnp.float32)
    grad_pooled = jnp.dot(rating_probs - target, rating_rows, precision=highest)
    gained = gain * grad_pooled
    grad_raw = inverse_rms * (gained - unit_rows * jnp.mean(gained * unit_rows))
    return (expected.reshape(1), grad_raw / math.sqrt(tokens))


def on_device(
    patches,
    stem_weight,
    embed_weight,
    frame_embed,
    attention_gain,
    final_gain,
    query_weight,
    key_weight,
    value_weight,
    output_weight,
    unembedding,
    rating_ids,
    target_score,
):
    full_patches, full_stem, full_embed = (
        lax.all_gather(patches, "space", axis=1, tiled=True),
        lax.all_gather(stem_weight, "space", axis=0, tiled=True),
        lax.all_gather(embed_weight, "space", axis=0, tiled=True),
    )
    frames_dev, count_rows, count_cols, channels = full_patches.shape
    rows_dev = patches.shape[1]
    positions = count_rows * count_cols
    width = full_embed.shape[1]
    inner = query_weight.shape[1]
    heads_dev = inner // HEAD
    time_devices = lax.axis_size("tm")
    slot_count = positions // time_devices
    all_frames = frames_dev * time_devices
    tokens = all_frames * positions
    items = slot_count * heads_dev
    time_index = lax.axis_index("tm")
    space_index = lax.axis_index("space")
    beside_all = neighbourhoods(full_patches).reshape(frames_dev * positions, 9 * channels)
    stem_pre = jnp.dot(beside_all, full_stem, preferred_element_type=jnp.float32)
    stem_act = jax.nn.gelu(stem_pre, approximate=True).astype(jnp.bfloat16)
    embedded = jnp.dot(stem_act, full_embed, preferred_element_type=jnp.float32).reshape(
        frames_dev, positions, width
    )
    embedded = (embedded + frame_embed.astype(jnp.float32)[:, None, :]).astype(jnp.bfloat16)
    gain = attention_gain.astype(jnp.float32)

    def project(normed, weight):
        return jnp.dot(normed, weight, preferred_element_type=jnp.float32).astype(jnp.bfloat16)

    moved = lax.all_to_all(embedded, "tm", split_axis=1, concat_axis=0, tiled=True)
    wide = moved.astype(jnp.float32)
    normed = (wide * rms_scale(wide) * gain).astype(jnp.bfloat16).reshape(-1, width)
    queries = project(normed, query_weight)
    key_rows = project(normed, key_weight)
    value_rows = project(normed, value_weight)
    item_shape = (all_frames, items, HEAD)
    queries = queries.reshape(item_shape)
    key_rows = key_rows.reshape(item_shape)
    value_rows = value_rows.reshape(item_shape)
    exact_weights, rounded_weights, mixture = attend(queries, key_rows, value_rows)
    own_rows = lax.dynamic_slice_in_dim(
        embedded.reshape(frames_dev, count_rows, count_cols, width),
        space_index * rows_dev,
        rows_dev,
        1,
    )
    embed_sum = jnp.sum(own_rows, axis=(0, 1, 2), dtype=jnp.float32)
    mixture_sum = jnp.sum(mixture, axis=0, dtype=jnp.float32).reshape(slot_count, inner).sum(axis=0)
    output_wide = output_weight.astype(jnp.float32)
    pooled_part = embed_sum + jnp.dot(mixture_sum, output_wide, precision=highest)
    vocab_dev = unembedding.shape[0]
    first_row = lax.axis_index(("tm", "space")) * vocab_dev
    picks = (rating_ids[:, None] - first_row == jnp.arange(vocab_dev)[None, :]).astype(jnp.bfloat16)
    rows_part = jnp.dot(picks, unembedding, preferred_element_type=jnp.float32)
    pooled_total, rating_rows = lax.psum((pooled_part, rows_part), ("tm", "space"))
    expected_score, cotangent = head_terms(
        pooled_total, rating_rows, final_gain, target_score, tokens
    )
    grad_heads = jnp.dot(output_wide, cotangent, precision=highest).reshape(heads_dev, HEAD)
    grad_mixture = jnp.tile(grad_heads, (slot_count, 1))
    grad_q, grad_k, grad_v = attend_back(
        queries, key_rows, value_rows, exact_weights, rounded_weights, grad_mixture
    )
    backproject_grad_q = grad_q.reshape(-1, inner)
    backproject_grad_k = grad_k.reshape(-1, inner)
    backproject_grad_v = grad_v.reshape(-1, inner)
    total = jnp.dot(backproject_grad_q, query_weight.T, preferred_element_type=jnp.float32)
    total = total + jnp.dot(backproject_grad_k, key_weight.T, preferred_element_type=jnp.float32)
    grad_normed = (
        total + jnp.dot(backproject_grad_v, value_weight.T, preferred_element_type=jnp.float32)
    ).reshape(all_frames, slot_count, width)
    slots = time_index * slot_count + jnp.arange(slot_count)
    own_tile = (slots // count_cols // rows_dev == space_index).astype(jnp.float32)[None, :, None]
    grad_embed = (
        rms_back(moved.astype(jnp.float32), gain, grad_normed) + own_tile * cotangent
    ).astype(jnp.bfloat16)
    grad_embed = lax.all_to_all(grad_embed, "tm", split_axis=0, concat_axis=1, tiled=True)
    grad_act = jnp.dot(
        grad_embed.reshape(-1, width), full_embed.T, preferred_element_type=jnp.float32
    )
    _, gelu_back = jax.vjp(lambda value: jax.nn.gelu(value, approximate=True), stem_pre)
    grad_pre = gelu_back(grad_act)[0].astype(jnp.bfloat16)
    local_grad = jnp.dot(beside_all.T, grad_pre, preferred_element_type=jnp.float32).reshape(-1)
    stem_gradient = lax.psum_scatter(local_grad, ("tm", "space"), scatter_dimension=0, tiled=True)
    return (expected_score, stem_gradient)


def solution(mesh):
    in_specs = (
        P("tm", "space", None, None),
        P("space", None),
        P("space", None),
        P("tm", None),
        P(),
        P(),
        P(None, "space"),
        P(None, "space"),
        P(None, "space"),
        P("space", None),
        P(("tm", "space"), None),
        P(),
        P(),
    )
    out_specs = (P(), P(("tm", "space")))
    return jax.shard_map(
        on_device, mesh=mesh, in_specs=in_specs, out_specs=out_specs, check_vma=False
    )
```

profile of v0, /device:TPU:1, one launch (start us, length us, event | category | flops | bytes accessed | tf_op | source)
XLA Modules:
  0.0 695.6 jit_solution(16710078804811988119)
XLA Ops:
  7.2 0.7 all-gather.3.cloned.1.call-update
  8.0 0.7 all-gather.5.cloned.1.call-update
  8.7 0.7 convert_element_type.121
  9.4 12.6 %all_gather.9 = bf16[2,16,16,256]{3,2,1,0:T(8,128)(2,1)S(1)} all-gather(bf16[2,4,16,256]{3,2,1,0:T(8,128)(2,1)} %param.13), channel_id=1, replica_groups=mesh['tm'=128,'space'=4] {'space'}, dimensions={1}, use_global_device_ids=true | all-gather | bytes 327680 | tf_op jit(solution)/shard_map/all_gather | solution.py:108
  22.6 20.5 %all-gather.3.cloned.1.call-done = bf16[2304,256]{1,0:T(8,128)(2,1)} async-done(((bf16[576,256]{1,0:T(8,128)(2,1)}), bf16[2304,256]{1,0:T(8,128)(2,1)}) %all-gather.3.cloned.1.call-update) | async-done | bytes 1179664 | tf_op jit(solution)/shard_map/all_gather | solution.py:109
  43.1 2.8 fusion.74
  45.8 26.3 %all-gather.5.cloned.1.call-done = bf16[256,2048]{1,0:T(8,128)(2,1)} async-done(((bf16[64,2048]{1,0:T(8,128)(2,1)}), bf16[256,2048]{1,0:T(8,128)(2,1)}) %all-gather.5.cloned.1.call-update) | async-done | bytes 1048592 | tf_op jit(solution)/shard_map/all_gather | solution.py:110
  72.1 2.0 fusion.26
  74.1 1.9 copy-done.1
  76.5 3.5 copy.107
  80.0 16.0 %all-to-all-start = ((bf16[2,256,2048]{2,0,1:T(2,128)(2,1)}), bf16[2,256,2048]{2,0,1:T(2,128)(2,1)S(1)}, u32[]{:S(2)}, u32[]{:S(2)}) async-start(bf16[2,256,2048]{2,0,1:T(2,128)(2,1)} %copy.107), calls=%async_computation | async-start | bytes 4194304 | tf_op jit(solution)/shard_map/all_to_all | solution.py:137
  96.9 0.6 compare_convert_fusion
  97.5 0.8 fusion.47
  98.3 1.3 convert_reduce_fusion.1
  99.7 48.8 %all-to-all-done = bf16[2,256,2048]{2,0,1:T(2,128)(2,1)S(1)} async-done(((bf16[2,256,2048]{2,0,1:T(2,128)(2,1)}), bf16[2,256,2048]{2,0,1:T(2,128)(2,1)S(1)}, u32[]{:S(2)}, u32[]{:S(2)}) %all-to-all-start) | async-done | bytes 2097184 | tf_op jit(solution)/shard_map/all_to_all | solution.py:137
  148.4 4.4 copy.138
  152.8 6.1 reshape.203
  158.9 2.2 multiply_reduce_fusion.1
  161.2 0.9 copy.136
  162.4 2.7 multiply_convert_fusion
  165.1 1.3 copy-done.2
  166.4 1.4 convolution_convert_fusion.3
  167.8 1.0 reshape.195
  168.9 0.9 copy.117
  169.7 3.3 convolution_convert_fusion.4
  173.0 1.0 reshape.194
  174.0 0.9 copy.120
  174.9 2.3 convolution_convert_fusion.5
  177.2 0.8 reshape.193
  178.0 1.1 copy.113
  179.1 3.1 fusion.70
  182.2 2.1 fusion.9
  184.3 1.3 reshape.196
  185.6 1.2 reduce_sum.119
  186.8 1.8 fusion.75
  188.6 0.6 add.102
  189.2 96.5 %all-reduce.2 = (f32[5,2048]{1,0:T(8,128)}, f32[2048]{0:T(1024)S(1)}) all-reduce(f32[5,2048]{1,0:T(8,128)} %fusion.47, f32[2048]{0:T(1024)} %add.102), channel_id=1, replica_groups=mesh['tm'=128,'space'=4] {'tm','space'}, use_global_device_ids=true, to_apply=%region_0.1 | all-reduce | flops 12288 | bytes 98304 | tf_op jit(solution)/shard_map/psum | solution.py:162
  285.7 0.6 multiply_reduce_fusion.4
  287.0 0.7 convert_multiply_fusion.1
  287.7 1.7 fusion.71
  289.4 1.3 fusion.69
  290.7 1.9 multiply_reduce_fusion.5
  292.6 1.0 fusion.51
  293.6 0.6 copy-done.12
  294.2 1.4 multiply_reduce_fusion.3
  296.3 0.8 multiply_multiply_fusion.5
  297.1 2.1 fusion.76
  299.5 1.6 convert_reduce_fusion
  301.1 1.6 fusion.11
  302.7 0.7 fusion.10
  303.4 4.4 copy.108
  307.8 1.1 copy.122
  309.1 4.0 fusion.79
  313.5 2.7 fusion.78
  316.9 7.8 %multiply_reduce_fusion = (f32[512]{0:T(512)S(1)}, f32[512,2048]{1,0:T(8,128)}) fusion(f32[512,2048]{1,0:T(8,128)} %reshape.203, f32[2048]{0:T(1024)S(1)} %convert_element_type.130, f32[512]{0:T(512)S(1)} %copy-done.15, bf16[512,256]{1,0:T(8,128)(2,1)S(1)} %convert_element_type.147, bf16[2048,256]{1,0:T(8,128)(2,1)S(1)} %copy-done, f32[512,2048]{1,0:T(8,128)} %fusion.78, ...), kind=kOutput, calls=%fused_computation.6 | convolution fusion | flops 543161856 | bytes 18100224 | tf_op jit(solution)/shard_map/dot_general | solution.py:177
  324.7 5.8 reshape.200
  330.8 6.7 fusion.5
  337.5 62.4 %all_to_all.24 = bf16[256,2,2048]{2,1,0:T(2,128)(2,1)S(1)} all-to-all(bf16[256,2,2048]{2,1,0:T(2,128)(2,1)S(1)} %fusion.5), channel_id=1, replica_groups=mesh['tm'=128,'space'=4] {'tm'}, dimensions={0} | all-to-all | bytes 4194304 | tf_op jit(solution)/shard_map/all_to_all | solution.py:184
  399.9 1.4 copy.124
  401.4 2.2 reshape.201
  403.6 5.2 convolution_bitcast_fusion
  408.9 2.6 copy.132
  411.5 276.2 %all-reduce.5.cloned.1.call-done = f32[589824]{0:T(1024)} async-done(((f32[589824]{0:T(1024)}), f32[589824]{0:T(1024)}) %all-reduce.5.cloned.1.call-update) | async-done | bytes 2359312
  687.7 1.4 dynamic-slice
  (68 shorter events, 3.3 us)
Async XLA Ops:
  7.2 167.8 %copy-start = (bf16[2048,256]{1,0:T(8,128)(2,1)S(1)}, bf16[2048,256]{1,0:T(8,128)(2,1)}, u32[]{:S(2)}) copy-start(bf16[2048,256]{1,0:T(8,128)(2,1)} %param.21) | copy-start | bytes 3145732
  7.2 35.9 %all-gather.3.cloned.1.call-start = ((), (), s32[]{:S(2)}) async-start(), calls=%async_computation.2 | async-start | bytes 1474560 | tf_op jit(solution)/shard_map/all_gather | solution.py:109
  7.9 64.2 %all-gather.5.cloned.1.call-start = ((), (), s32[]{:S(2)}) async-start(), calls=%async_computation.3 | async-start | bytes 1310720 | tf_op jit(solution)/shard_map/all_gather | solution.py:110
  22.6 20.5 %copy-start.13 = (bf16[2,16,16,2304]{3,2,1,0:T(8,128)(2,1)}, bf16[2,16,16,2304]{3,2,1,0:T(8,128)(2,1)S(1)}, u32[]{:S(2)}) copy-start(bf16[2,16,16,2304]{3,2,1,0:T(8,128)(2,1)S(1)} %fusion.35) | copy-start | bytes 7077892
  45.8 28.3 %copy-start.3 = (f32[512,256]{1,0:T(8,128)}, f32[512,256]{1,0:T(8,128)S(1)}, u32[]{:S(2)}) copy-start(f32[512,256]{1,0:T(8,128)S(1)} %fusion.74) | copy-start | bytes 1572868
  74.1 1.9 copy-start.1
  80.0 16.2 %copy-start.17 = (bf16[2048]{0:T(1024)(128)(2,1)S(1)}, bf16[2048]{0:T(1024)(128)(2,1)}, u32[]{:S(2)}) copy-start(bf16[2048]{0:T(1024)(128)(2,1)} %param.17) | copy-start | bytes 12292
  80.0 17.5 %copy-start.19 = (s32[5]{0:T(128)S(1)}, s32[5]{0:T(128)}, u32[]{:S(2)}) copy-start(s32[5]{0:T(128)} %param.24) | copy-start | bytes 64
  80.0 17.5 %copy-start.7 = (bf16[64,2048]{1,0:T(8,128)(2,1)S(1)}, bf16[64,2048]{1,0:T(8,128)(2,1)}, u32[]{:S(2)}) copy-start(bf16[64,2048]{1,0:T(8,128)(2,1)} %param.23) | copy-start | bytes 786436
  80.0 68.4 %all-to-all-start = ((bf16[2,256,2048]{2,0,1:T(2,128)(2,1)}), bf16[2,256,2048]{2,0,1:T(2,128)(2,1)S(1)}, u32[]{:S(2)}, u32[]{:S(2)}) async-start(bf16[2,256,2048]{2,0,1:T(2,128)(2,1)} %copy.107), calls=%async_computation | async-start | bytes 4194304 | tf_op jit(solution)/shard_map/all_to_all | solution.py:137
  96.0 591.7 %all-reduce.5.cloned.1.call-start = ((), (), s32[]{:S(2)}) async-start(), calls=%async_computation.4 | async-start | bytes 4718592
  162.4 2.7 copy-start.14
  162.4 4.0 copy-start.5
  165.1 1.3 copy-start.2
  293.6 0.6 copy-start.12
  296.2 4.8 copy-start.4
  296.2 4.8 copy-start.9
  296.2 4.8 copy-start.16
  297.1 2.4 copy-start.10
  301.1 1.6 copy-start.8
  309.1 4.4 copy-start.6
  313.5 3.4 copy-start.15
  324.7 6.0 copy-start.11
  324.7 6.0 copy-start.18
Sparse Core Ops, SparseCore 0:
  10.1 32.9 all-gather.2
  45.2 26.8 all-gather.4
  411.6 276.0 all-reduce.4
where the time goes:
time: 697 us; the launch traced here: 696 us
  waiting for transfers between devices  373 us (54%)
  blocking collectives  172 us (25%)
  matrix products  46.7 us (7%)
  local copies, waits for them, and re-layouts  46.5 us (7%)
  other arithmetic  25.3 us (4%)
  starting transfers between devices  16.3 us (2%)
  between operations  16.2 us (2%)
    unnamed x4, waiting for transfers between devices  278 us
    psum x1, blocking collectives, on_device(): lax.psum((pooled_part, rows_part), ('tm', 'space'))  96.5 us
    all_to_all x1, blocking collectives, on_device(): lax.all_to_all(grad_embed, 'tm', split_axis=0, concat_axis=1, tiled=True)  62.4 us
    all_to_all x1, waiting for transfers between devices, on_device(): lax.all_to_all(embedded, 'tm', split_axis=1, concat_axis=0, tiled=True)  48.8 us
    all_gather x1, waiting for transfers between devices, on_device(): lax.all_gather(embed_weight, 'space', axis=0, tiled=True)  26.3 us
    all_gather x1, waiting for transfers between devices, on_device(): lax.all_gather(stem_weight, 'space', axis=0, tiled=True)  20.5 us
    all_to_all x1, starting transfers between devices, on_device(): lax.all_to_all(embedded, 'tm', split_axis=1, concat_axis=0, tiled=True)  16 us
    convert_element_type x3, local copies, waits for them, and re-layouts, on_device(): wide = moved.astype(jnp.float32)  14.9 us
  transfers between devices with their start and end apart: 4, of which 4 were waited for; matrix products, arithmetic and copies ran while one was open for 1% of the time, Pallas kernels for 0%

commit v1 on v0

v1 whole, which is shorter than its diff:
```python
import functools
import math

import jax
import jax.numpy as jnp
from jax import lax
from jax.experimental import pallas as pl
from jax.experimental.pallas import tpu as pltpu
from jax.sharding import Mesh, PartitionSpec as P

HEAD = 128
LANES = 128
EPSILON = 1e-05
BF = jnp.bfloat16
F32 = jnp.float32
T_AXES = ("zh", "y", "x")
S_AXES = ("zl", "core")
FACTORS = {128: (4, 8, 4), 8: (2, 2, 2)}
NT = (((1,), (1,)), ((), ()))
TN = (((0,), (0,)), ((), ()))
VMEM_LIMIT = 48 * 1024 * 1024


def dot(lhs, rhs, dims=(((1,), (0,)), ((), ()))):
    return lax.dot_general(lhs, rhs, dims, preferred_element_type=F32)


def thirds(row):
    first = row.astype(BF)
    rest = row - first.astype(F32)
    second = rest.astype(BF)
    third = (rest - second.astype(F32)).astype(BF)
    zero = jnp.zeros((5, row.shape[1]), F32)
    parts = [first.astype(F32), second.astype(F32), third.astype(F32), zero]
    return jnp.concatenate(parts, axis=0).astype(BF)


def halves(values):
    first = values.astype(BF)
    return first, (values - first.astype(F32)).astype(BF)


def neighbourhoods(frames):
    count_rows = frames.shape[1]
    count_cols = frames.shape[2]
    padded = jnp.pad(frames, ((0, 0), (1, 1), (1, 1), (0, 0)))
    pieces = [
        padded[:, row_off : row_off + count_rows, col_off : col_off + count_cols, :]
        for row_off in range(3)
        for col_off in range(3)
    ]
    return jnp.concatenate(pieces, axis=-1)


def split_heads(block, heads):
    inner = heads * HEAD
    for head in range(heads):
        at = head * HEAD
        yield (
            head,
            block[:, at : at + HEAD],
            block[:, inner + at : inner + at + HEAD],
            block[:, 2 * inner + at : 2 * inner + at + HEAD],
        )


def forward_kernel(heads, qkv_ref, out_weight_ref, embed_sum_ref, weights_ref, pooled_ref):
    slots = qkv_ref.shape[0]
    factor = 1.0 / math.sqrt(HEAD)
    sums = [0.0] * heads
    for slot in range(slots):
        for head, query, key, value in split_heads(qkv_ref[slot], heads):
            scores = dot(key, query, NT) * factor
            top = jnp.max(scores, axis=0, keepdims=True)
            raised = jnp.exp(scores - top)
            weights = raised / jnp.sum(raised, axis=0, keepdims=True)
            weights_ref[slot * heads + head] = weights
            mixture = dot(weights.astype(BF), value, TN).astype(BF).astype(F32)
            sums[head] = sums[head] + jnp.sum(mixture, axis=0, keepdims=True)
    mixture_sum = thirds(jnp.concatenate(sums, axis=1))
    mixed = jnp.sum(dot(mixture_sum, out_weight_ref[...]), axis=0, keepdims=True)
    pooled_ref[...] = embed_sum_ref[...] + mixed


def backward_kernel(
    heads,
    tokens,
    ratings,
    target_ref,
    pooled_ref,
    rating_ref,
    gain_ref,
    out_weight_ref,
    own_embed_ref,
    qkv_ref,
    weights_ref,
    back_first_ref,
    back_second_ref,
    expected_ref,
    direct_ref,
    sent_ref,
    mean_ref,
):
    width = pooled_ref.shape[1]
    pooled_raw = pooled_ref[...] / tokens
    inverse_rms = lax.rsqrt(jnp.mean(pooled_raw * pooled_raw, axis=1, keepdims=True) + EPSILON)
    unit = pooled_raw * inverse_rms
    gain = gain_ref[...].astype(F32)
    rows = rating_ref[...]
    logits = jnp.sum(rows * (unit * gain), axis=1, keepdims=True)
    index = lax.broadcasted_iota(jnp.int32, logits.shape, 0)
    real = index < ratings
    logits = jnp.where(real, logits, -jnp.inf)
    raised = jnp.exp(logits - jnp.max(logits, axis=0, keepdims=True))
    probs = raised / jnp.sum(raised, axis=0, keepdims=True)
    ladder = (index + 1).astype(F32)
    expected = jnp.sum(probs * ladder, axis=0, keepdims=True)
    expected_ref[...] = jnp.broadcast_to(expected, expected_ref.shape)
    hit = (index == target_ref[0] - 1).astype(F32)
    gained = gain * jnp.sum((probs - hit) * rows, axis=0, keepdims=True)
    centre = jnp.mean(gained * unit, axis=1, keepdims=True)
    cotangent = inverse_rms * (gained - unit * centre) / math.sqrt(tokens)
    parts = thirds(cotangent)
    direct = jnp.sum(dot(own_embed_ref[...], parts, NT), axis=1, keepdims=True)
    direct_ref[...] = jnp.broadcast_to(direct, direct_ref.shape)
    grad_heads = jnp.sum(dot(parts, out_weight_ref[...], NT), axis=0, keepdims=True)
    factor = 1.0 / math.sqrt(HEAD)
    slots, frames = qkv_ref.shape[0], qkv_ref.shape[1]
    half = frames // 2
    for slot in range(slots):
        grads_q, grads_k, grads_v = [], [], []
        total = jnp.zeros((frames, 1), F32)
        for head, query, key, value in split_heads(qkv_ref[slot], heads):
            grad_mixture = grad_heads[:, head * HEAD : (head + 1) * HEAD]
            weights = weights_ref[slot * heads + head]
            wide_value = value.astype(F32)
            grad_weights = jnp.sum(wide_value * grad_mixture, axis=1, keepdims=True)
            centre = jnp.sum(weights * grad_weights, axis=0, keepdims=True)
            upper, lower = halves(weights * (grad_weights - centre) * factor)
            grad_query = dot(upper, key, TN) + dot(lower, key, TN)
            grad_key = dot(upper, query) + dot(lower, query)
            mass = jnp.sum(weights.astype(BF).astype(F32), axis=1, keepdims=True)
            grad_value = mass * grad_mixture
            total = total + jnp.sum(
                grad_query * query.astype(F32)
                + grad_key * key.astype(F32)
                + grad_value * wide_value,
                axis=1,
                keepdims=True,
            )
            grads_q.append(grad_query.astype(BF))
            grads_k.append(grad_key.astype(BF))
            grads_v.append(grad_value.astype(BF))
        grads = jnp.concatenate(grads_q + grads_k + grads_v, axis=1)
        sent = dot(grads[:half], back_first_ref[...]) + dot(grads[half:], back_second_ref[...])
        sent_ref[slot] = sent.astype(BF)
        mean_ref[slot] = jnp.broadcast_to(total / width, (frames, mean_ref.shape[2]))


def on_device(
    patches,
    stem_weight,
    embed_weight,
    frame_embed,
    attention_gain,
    final_gain,
    query_weight,
    key_weight,
    value_weight,
    output_weight,
    unembedding,
    rating_ids,
    target_score,
):
    n_t = lax.axis_size(T_AXES)
    n_s = lax.axis_size(S_AXES)
    everyone = T_AXES + S_AXES
    space_index = lax.axis_index(S_AXES)
    frames_dev, rows_dev, cols, channels = patches.shape
    own_channels = channels // n_s
    count_rows = rows_dev * n_s
    positions = count_rows * cols
    slots = positions // n_t
    width = embed_weight.shape[1]
    inner = query_weight.shape[1]
    heads = inner // HEAD
    all_frames = frames_dev * n_t
    tokens = all_frames * positions
    tokens_dev = frames_dev * positions
    assert frames_dev == 2 and slots == 2

    pair = lax.all_gather(embed_weight, "core", axis=0, tiled=True)
    other = lax.ppermute(pair, "zl", [(0, 1), (1, 0)])

    lane_blocks = channels // LANES
    patch_rows = patches.reshape(-1, channels)
    patch_part = jnp.concatenate(
        [patch_rows[:, i * LANES : (i + 1) * LANES] for i in range(lane_blocks)], axis=0
    )
    stem_rows = stem_weight.shape[0]
    stem_half = stem_rows // 2
    stem_part = stem_weight.reshape(2, stem_half, n_s, own_channels).transpose(2, 1, 0, 3)
    stem_part = stem_part.reshape(n_s, stem_half, 2 * own_channels)
    packed = jnp.concatenate(
        [jnp.broadcast_to(patch_part[None], (n_s,) + patch_part.shape), stem_part], axis=1
    )
    packed = lax.all_to_all(packed, S_AXES, 0, 0, tiled=True)
    count = patch_part.shape[0]
    got = packed[:, :count].reshape(n_s, lane_blocks, frames_dev, rows_dev, cols, LANES)
    full_patches = got.transpose(2, 0, 3, 4, 1, 5).reshape(
        frames_dev, count_rows, cols, channels
    )
    stem_cols = packed[:, count:].reshape(n_s, stem_half, 2, own_channels)
    stem_cols = stem_cols.transpose(0, 2, 1, 3).reshape(n_s * stem_rows, own_channels)

    beside = neighbourhoods(full_patches).reshape(tokens_dev, 9 * channels)
    stem_pre = dot(stem_cols, beside, (((0,), (1,)), ((), ())))
    stem_act, gelu_back = jax.vjp(lambda value: jax.nn.gelu(value, approximate=True), stem_pre)
    (gelu_slope,) = gelu_back(jnp.ones_like(stem_pre))
    act = lax.all_gather(stem_act.astype(BF), S_AXES, axis=0, tiled=True)

    lower = lax.axis_index("zl") == 0
    full_embed = jnp.concatenate(
        [jnp.where(lower, pair, other), jnp.where(lower, other, pair)], axis=0
    )
    gain = attention_gain.astype(F32)
    embedded = dot(act, full_embed, TN).reshape(frames_dev, positions, width)
    embedded = (embedded + frame_embed.astype(F32)[:, None, :]).astype(BF)
    embedded = embedded.reshape(tokens_dev, width)
    wide = embedded.astype(F32)
    scale = lax.rsqrt(jnp.mean(wide * wide, axis=-1, keepdims=True) + EPSILON)
    normed = (wide * scale * gain).astype(BF)
    qkv = jnp.concatenate(
        [dot(normed, w).astype(BF) for w in (query_weight, key_weight, value_weight)], axis=1
    )
    embed_sum = jnp.sum(wide, axis=0, keepdims=True) * (1.0 / n_s)
    scale_row = scale.reshape(1, tokens_dev)
    back_unit = dot(embed_weight, embedded, NT) * scale_row

    vocab_dev = unembedding.shape[0]
    ratings = rating_ids.shape[0]
    first_row = lax.axis_index(everyone) * vocab_dev
    picks = (rating_ids[:, None] - first_row == jnp.arange(vocab_dev)[None, :]).astype(BF)
    rows_part = dot(picks, unembedding).astype(BF)
    groups = width // n_t
    rating_part = rows_part.reshape(ratings * groups, n_t).T
    rating_part = jnp.pad(rating_part, ((0, 0), (0, LANES - ratings * groups)))
    rating_part = jnp.pad(rating_part[:, None, :], ((0, 0), (0, slots * frames_dev - 1), (0, 0)))

    qkv = qkv.reshape(frames_dev, slots, n_t, 3 * inner).transpose(2, 1, 0, 3)
    qkv = qkv.reshape(n_t, slots * frames_dev, 3 * inner)
    moved = jnp.concatenate([qkv, rating_part], axis=2)
    moved = lax.all_to_all(moved, T_AXES, 0, 0, tiled=True)
    qkv = moved[:, :, : 3 * inner].transpose(1, 0, 2).reshape(slots, all_frames, 3 * inner)
    rating_slice = jnp.sum(moved[:, 0, 3 * inner :].astype(F32), axis=0, keepdims=True)

    items = slots * heads
    whole = pl.BlockSpec(memory_space=pltpu.VMEM)
    weights, pooled_part = pl.pallas_call(
        functools.partial(forward_kernel, heads),
        name="attend",
        out_shape=(
            jax.ShapeDtypeStruct((items, all_frames, all_frames), F32),
            jax.ShapeDtypeStruct((1, width), F32),
        ),
        in_specs=[whole] * 3,
        out_specs=(whole, whole),
        compiler_params=pltpu.CompilerParams(vmem_limit_bytes=VMEM_LIMIT),
    )(qkv, output_weight, embed_sum)

    pooled_rows = pooled_part.reshape(width // LANES, LANES)
    rating_rows = rating_slice
    for axes in (("x",) + S_AXES, ("y",), ("zh",)):
        size = lax.axis_size(axes)
        packed = jnp.concatenate([pooled_rows, rating_rows], axis=0)
        packed = jnp.broadcast_to(packed[None], (size,) + packed.shape)
        packed = lax.all_to_all(packed, axes, 0, 0, tiled=True)
        pooled_rows = jnp.sum(packed[:, : width // LANES], axis=0)
        rating_rows = packed[:, width // LANES :]
        if len(axes) > 1:
            rating_rows = rating_rows.reshape(size // n_s, n_s, LANES).sum(axis=1)
        rating_rows = rating_rows.reshape(-1, LANES)
    rating_rows = rating_rows[:, : ratings * groups].T.reshape(ratings, width)
    rating_rows = jnp.pad(rating_rows, ((0, 8 - ratings), (0, 0)))

    scaled = (full_embed.astype(F32) * gain).astype(BF)
    back = jnp.concatenate(
        [
            dot(w, scaled, (((0,), (1,)), ((), ()))).astype(BF)
            for w in (query_weight, key_weight, value_weight)
        ],
        axis=0,
    ).reshape(3 * inner, n_s, own_channels)
    blank = jnp.zeros_like(back)
    sent_width = n_s * frames_dev * own_channels
    back_first = jnp.concatenate([back, blank], axis=2).reshape(3 * inner, sent_width)
    back_second = jnp.concatenate([blank, back], axis=2).reshape(3 * inner, sent_width)

    expected, direct, sent, means = pl.pallas_call(
        functools.partial(backward_kernel, heads, float(tokens), ratings),
        name="attend_back",
        out_shape=(
            jax.ShapeDtypeStruct((8, LANES), F32),
            jax.ShapeDtypeStruct((own_channels, LANES), F32),
            jax.ShapeDtypeStruct((slots, n_t, sent_width), BF),
            jax.ShapeDtypeStruct((slots, all_frames, 8), F32),
        ),
        in_specs=[pl.BlockSpec(memory_space=pltpu.SMEM)] + [whole] * 9,
        out_specs=(whole,) * 4,
        compiler_params=pltpu.CompilerParams(vmem_limit_bytes=VMEM_LIMIT),
    )(
        target_score,
        pooled_rows.reshape(1, width),
        rating_rows,
        final_gain[None, :],
        output_weight,
        embed_weight,
        qkv,
        weights,
        back_first,
        back_second,
    )

    pair_lanes = frames_dev * own_channels
    sent = sent.reshape(slots, n_t, n_s, pair_lanes).transpose(1, 2, 0, 3)
    means = means[:, :, 0].reshape(slots * frames_dev, n_t).T.astype(BF)
    means = jnp.pad(means, ((0, 0), (0, pair_lanes - slots * frames_dev)))
    means = jnp.broadcast_to(means[:, None, None, :], (n_t, n_s, 1, pair_lanes))
    sent = jnp.concatenate([sent, means], axis=2).reshape(n_t * n_s, slots + 1, pair_lanes)
    sent = lax.all_to_all(sent, everyone, 0, 0, tiled=True)
    sent = jnp.sum(sent.reshape(n_t, n_s, slots + 1, pair_lanes).astype(F32), axis=1)
    turned = sent.transpose(1, 2, 0)
    grad_unit = turned[:slots].reshape(slots, frames_dev, own_channels, n_t)
    grad_unit = grad_unit.transpose(2, 1, 0, 3).reshape(own_channels, tokens_dev)
    mean_row = turned[slots, : slots * frames_dev].reshape(slots, frames_dev, n_t)
    mean_row = mean_row.transpose(1, 0, 2).reshape(1, tokens_dev)
    grad_act = scale_row * (grad_unit - mean_row * back_unit) + direct[:, :1]
    grad_pre = (gelu_slope * grad_act).astype(BF)

    local_grad = dot(beside, grad_pre, (((0,), (1,)), ((), ())))
    lines = local_grad.reshape(n_t, -1, LANES).astype(BF)
    step = lines.shape[1] // n_s
    window = -(-lines.shape[1] // n_s)
    lines = jnp.stack([lines[:, step * s : step * s + window] for s in range(n_s)], axis=1)
    lines = lines.reshape(n_t * n_s, window, LANES)
    lines = lax.all_to_all(lines, everyone, 0, 0, tiled=True)
    lines = jnp.sum(lines.reshape(n_t, n_s, window, LANES).astype(F32), axis=0)
    flat = lines.reshape(n_s, -1, own_channels).transpose(1, 0, 2).reshape(-1)
    length = 9 * channels * channels // (n_t * n_s)
    start = space_index * (length - step * LANES * n_s)
    stem_gradient = lax.dynamic_slice_in_dim(flat, start, length, 0)
    return (expected[0, :1], stem_gradient)


def solution(mesh):
    shape = FACTORS[mesh.shape["tm"]] + (2, 2)
    split = Mesh(mesh.devices.reshape(shape), T_AXES + S_AXES)
    both = T_AXES + S_AXES
    in_specs = (
        P(T_AXES, S_AXES, None, None),
        P(S_AXES, None),
        P(S_AXES, None),
        P(T_AXES, None),
        P(),
        P(),
        P(None, S_AXES),
        P(None, S_AXES),
        P(None, S_AXES),
        P(S_AXES, None),
        P(both, None),
        P(),
        P(),
    )
    return jax.shard_map(
        on_device, mesh=split, in_specs=in_specs, out_specs=(P(), P(both)), check_vma=False
    )
```

time: 697 us -> 241 us (0.35)
  waiting for transfers between devices: 373 us -> 89.2 us
  blocking collectives: 172 us -> 8.74 us
  starting transfers between devices: 16.3 us -> 64.3 us
  matrix products: 46.7 us -> 16.6 us
  other arithmetic: 25.3 us -> 7.7 us
  between operations: 16.2 us -> 2 us
    unnamed x4 -> x0, waiting for transfers between devices: 278 us -> none
    psum x1 -> x0, blocking collectives: 96.5 us -> none  [on_device(): lax.psum((pooled_part, rows_part), ('tm', 'space'))]
    all_to_all x1 -> x0, blocking collectives: 62.4 us -> none  [on_device(): lax.all_to_all(grad_embed, 'tm', split_axis=0, concat_axis=1, tiled=True)]
    all_gather x2 -> x0, waiting for transfers between devices: 46.7 us -> none  [the longest x1 26.3 us: on_device(): lax.all_gather(embed_weight, 'space', axis=0, tiled=True)]
    all_to_all x1 -> x7, starting transfers between devices: 16 us -> 61 us  [the longest x1 15.4 us: on_device(): moved = lax.all_to_all(moved, T_AXES, 0, 0, tiled=True)]
    dot_general x18 -> x10, matrix products: 43.6 us -> 16.6 us  [dot(): return lax.dot_general(lhs, rhs, dims, preferred_element_type=F32)]
    all_to_all x1 -> x7, waiting for transfers between devices: 48.8 us -> 75.7 us  [the longest x1 26.2 us: on_device(): moved = lax.all_to_all(moved, T_AXES, 0, 0, tiled=True)]
    convert_element_type x7 -> x3, local copies, waits for them, and re-layouts: 19.8 us -> 0.73 us  [the longest x2 0.71 us: on_device(): lines = local_grad.reshape(n_t, -1, LANES).astype(BF)]
  transfers between devices with their start and end apart: 4 -> 8, of which waited for: 4 -> 7; matrix products, arithmetic and copies ran while one was open for 1% -> 7% of each run, Pallas kernels for 0% -> 0%
where the time goes in v1:
time: 241 us; the launch traced here: 240 us
  waiting for transfers between devices  89.2 us (37%)
  starting transfers between devices  64.3 us (27%)
  local copies, waits for them, and re-layouts  47 us (20%)
  matrix products  16.6 us (7%)
  blocking collectives  8.74 us (4%)
  other arithmetic  7.7 us (3%)
  Pallas kernels  4.05 us (2%)
    all_to_all x1, waiting for transfers between devices, on_device(): moved = lax.all_to_all(moved, T_AXES, 0, 0, tiled=True)  26.2 us
    all_to_all x1, waiting for transfers between devices, on_device(): sent = lax.all_to_all(sent, everyone, 0, 0, tiled=True)  21.7 us
    all_to_all x1, waiting for transfers between devices, on_device(): lines = lax.all_to_all(lines, everyone, 0, 0, tiled=True)  21.5 us
    unnamed x61, local copies, waits for them, and re-layouts  20.2 us
    dot_general x10, matrix products, dot(): return lax.dot_general(lhs, rhs, dims, preferred_element_type=F32)  16.6 us
    all_to_all x1, starting transfers between devices, on_device(): moved = lax.all_to_all(moved, T_AXES, 0, 0, tiled=True)  15.4 us
    all_to_all x3, starting transfers between devices, on_device(): packed = lax.all_to_all(packed, axes, 0, 0, tiled=True)  13.5 us
    ppermute x1, waiting for transfers between devices, on_device(): other = lax.ppermute(pair, 'zl', [(0, 1), (1, 0)])  13.5 us
  transfers between devices with their start and end apart: 8, of which 7 were waited for; matrix products, arithmetic and copies ran while one was open for 7% of the time, Pallas kernels for 0%

profile of v1, /device:TPU:1, one launch (start us, length us, event | category | flops | bytes accessed | tf_op | source)
XLA Modules:
  0.0 239.6 jit_solution(12211107353068401263)
XLA Ops:
  0.6 0.9 fusion.56
  1.8 1.2 copy.117
  3.5 1.1 copy.119
  4.6 10.3 %all-to-all-start = ((bf16[4,544,128]{2,1,0:T(8,128)(2,1)}), bf16[4,544,128]{2,1,0:T(8,128)(2,1)S(1)}, u32[]{:S(2)}, u32[]{:S(2)}) async-start(bf16[4,544,128]{2,1,0:T(8,128)(2,1)} %copy.119), calls=%async_computation | async-start | bytes 1114112 | tf_op jit(solution)/shard_map/all_to_all | solution.py:207
  14.9 2.2 all_gather.7
  17.0 3.3 %collective-permute-start = (bf16[128,2048]{1,0:T(8,128)(2,1)S(1)}, bf16[128,2048]{1,0:T(8,128)(2,1)}, u32[]{:S(2)}, u32[]{:S(2)}) collective-permute-start(bf16[128,2048]{1,0:T(8,128)(2,1)S(1)} %all_gather.7), channel_id=1, source_target_pairs={{0,2},{2,0},{1,3},{3,1},{4,6},{6,4},{5,7},{7,5},{8,10},{10,8},{9,1... | collective-permute-start | bytes 1572872 | tf_op jit(solution)/shard_map/ppermute | solution.py:193
  20.9 13.5 %collective-permute-done = bf16[128,2048]{1,0:T(8,128)(2,1)} collective-permute-done((bf16[128,2048]{1,0:T(8,128)(2,1)S(1)}, bf16[128,2048]{1,0:T(8,128)(2,1)}, u32[]{:S(2)}, u32[]{:S(2)}) %collective-permute-start) | collective-permute-done | bytes 524320 | tf_op jit(solution)/shard_map/ppermute | solution.py:193
  34.4 1.9 broadcast_select_fusion.1
  36.8 1.3 pad_slice_fusion
  38.1 0.8 constant_dynamic-update-slice_fusion.7
  39.9 1.7 constant_dynamic-update-slice_fusion.6
  41.6 1.7 constant_dynamic-update-slice_fusion.5
  43.3 1.7 constant_dynamic-update-slice_fusion.4
  45.0 0.8 bitcast_dynamic-update-slice_fusion
  45.8 1.7 constant_dynamic-update-slice_fusion.3
  47.5 1.7 constant_dynamic-update-slice_fusion.2
  49.2 1.7 constant_dynamic-update-slice_fusion.1
  50.9 0.7 constant_dynamic-update-slice_fusion
  51.6 3.1 %multiply_convert_fusion.4 = (bf16[64,512]{1,0:T(8,128)(2,1)S(1)}, f32[64,512]{1,0:T(8,128)}) fusion(bf16[2304,64]{0,1:T(8,128)(2,1)S(1)} %reshape.150, bf16[512,2304]{1,0:T(8,128)(2,1)} %constant_dynamic-update-slice_fusion), kind=kOutput, calls=%fused_computation.74 | convolution fusion | flops 151289856 | bytes 2850816 | tf_op jit(solution)/shard_map/dot_general | solution.py:25
  54.8 6.6 %all_gather.6 = bf16[256,512]{1,0:T(8,128)(2,1)S(1)} all-gather(bf16[64,512]{1,0:T(8,128)(2,1)S(1)} %get-tuple-element.34), channel_id=1, replica_groups=mesh['zh'=4,'y'=8,'x'=4,'zl'=2,'core'=2] {'zl','core'}, dimensions={0}, use_global_device_ids=true | all-gather | bytes 327680 | tf_op jit(solution)/shard_map/all_gather | solution.py:220
  61.4 1.0 convert_reduce_fusion
  62.4 0.9 convolution_convert_fusion.4
  63.3 1.0 copy-done.19
  64.3 0.9 convolution_convert_fusion.3
  65.6 0.9 convolution_convert_fusion.2
  66.8 1.4 copy.124
  68.4 1.4 fusion.15
  69.8 15.4 %all-to-all-start.1 = ((bf16[128,4,896]{2,1,0:T(4,128)(2,1)}), bf16[128,4,896]{2,1,0:T(4,128)(2,1)}, u32[]{:S(2)}, u32[]{:S(2)}) async-start(bf16[128,4,896]{2,1,0:T(4,128)(2,1)} %fusion.15), calls=%async_computation.1 | async-start | bytes 1835008 | tf_op jit(solution)/shard_map/all_to_all | solution.py:253
  85.9 26.2 %all-to-all-done.1 = bf16[128,4,896]{2,1,0:T(4,128)(2,1)} async-done(((bf16[128,4,896]{2,1,0:T(4,128)(2,1)}), bf16[128,4,896]{2,1,0:T(4,128)(2,1)}, u32[]{:S(2)}, u32[]{:S(2)}) %all-to-all-start.1) | async-done | bytes 917536 | tf_op jit(solution)/shard_map/all_to_all | solution.py:253
  112.1 1.4 slice_bitcast_fusion
  113.6 1.3 attend.1
  115.0 1.0 copy-done.5
  116.0 1.1 fusion.34
  117.0 0.7 broadcast_in_dim.19
  117.7 6.2 %all-to-all-start.2 = ((f32[16,17,128]{2,1,0:T(8,128)}), f32[16,17,128]{2,1,0:T(8,128)S(1)}, u32[]{:S(2)}, u32[]{:S(2)}) async-start(f32[16,17,128]{2,1,0:T(8,128)} %broadcast_in_dim.19), calls=%async_computation.2 | async-start | bytes 393216 | tf_op jit(solution)/shard_map/all_to_all | solution.py:277
  124.0 2.6 %fusion.11 = bf16[256,256]{1,0:T(8,128)(2,1)} fusion(bf16[2048,256]{1,0:T(8,128)(2,1)S(1)} %copy-done, f32[2048]{0:T(1024)S(1)} %convert_element_type.102, bf16[128,2048]{1,0:T(8,128)(2,1)} %get-tuple-element.17, bf16[128,2048]{1,0:T(8,128)(2,1)} %copy-done.9), kind=kOutput, calls=%fused_computation.26 | convolution fusion | flops 271646720 | bytes 2236416 | tf_op jit(solution)/shard_map/dot_general | solution.py:25
  126.6 1.2 fusion.12
  127.8 2.9 %all-to-all-done.2 = f32[16,17,128]{2,1,0:T(8,128)S(1)} async-done(((f32[16,17,128]{2,1,0:T(8,128)}), f32[16,17,128]{2,1,0:T(8,128)S(1)}, u32[]{:S(2)}, u32[]{:S(2)}) %all-to-all-start.2) | async-done | bytes 139296 | tf_op jit(solution)/shard_map/all_to_all | solution.py:277
  131.4 4.0 %all-to-all-start.3 = ((f32[8,20,128]{2,1,0:T(8,128)}), f32[8,20,128]{2,1,0:T(8,128)}, u32[]{:S(2)}, u32[]{:S(2)}) async-start(f32[8,20,128]{2,1,0:T(8,128)} %broadcast_in_dim.20), calls=%async_computation.3 | async-start | bytes 196608 | tf_op jit(solution)/shard_map/all_to_all | solution.py:277
  135.4 2.1 fusion.13
  137.5 0.9 pad_maximum_fusion.4
  138.5 0.9 copy.129
  139.4 3.4 %all-to-all-done.3 = f32[8,20,128]{2,1,0:T(8,128)} async-done(((f32[8,20,128]{2,1,0:T(8,128)}), f32[8,20,128]{2,1,0:T(8,128)}, u32[]{:S(2)}, u32[]{:S(2)}) %all-to-all-start.3) | async-done | bytes 81952 | tf_op jit(solution)/shard_map/all_to_all | solution.py:277
  142.8 0.8 slice.131
  143.6 0.9 slice_reduce_fusion.1
  144.4 0.7 broadcast_in_dim.21
  145.1 3.3 %all-to-all-start.4 = ((f32[4,48,128]{2,1,0:T(8,128)}), f32[4,48,128]{2,1,0:T(8,128)S(1)}, u32[]{:S(2)}, u32[]{:S(2)}) async-start(f32[4,48,128]{2,1,0:T(8,128)} %broadcast_in_dim.21), calls=%async_computation.4 | async-start | bytes 196608 | tf_op jit(solution)/shard_map/all_to_all | solution.py:277
  148.4 2.4 fusion.55
  150.8 2.3 copy.145.back_first_ref
  153.1 2.3 copy.146.back_second_ref
  155.6 1.1 copy-done.2
  156.7 1.1 copy-done.3
  157.9 1.2 copy-done.6
  159.1 2.7 %attend_back.1 = (f32[8,128]{1,0:T(8,128)S(1)}, f32[64,128]{1,0:T(8,128)S(1)}, bf16[2,128,512]{2,1,0:T(8,128)(2,1)S(1)}, f32[2,256,8]{2,1,0:T(8,128)S(1)}) custom-call(s32[1]{0:T(128)S(6)} %copy.166.target_ref, f32[1,2048]{1,0:T(1,128)S(1)} %bitcast.114, f32[8,2048]{1,0:T(8,128)S(1)} %pad.25.rating_ref, bf16[1,2048]{1,0:T(2,128)(2,1)S(1)} %broadcast_in_dim.22.gain_ref, ...), custom_call_target="tpu_custom_call" | custom-call | tf_op jit(solution)/shard_map/attend_back/pallas_call | solution.py:299
  161.8 0.7 copy-done.7
  162.6 1.1 fusion.23
  164.2 1.4 copy.133
  165.6 12.7 %all-to-all-start.5 = ((bf16[512,3,128]{2,1,0:T(4,128)(2,1)}), bf16[512,3,128]{2,1,0:T(4,128)(2,1)S(1)}, u32[]{:S(2)}, u32[]{:S(2)}) async-start(bf16[512,3,128]{2,1,0:T(4,128)(2,1)} %bitcast.39), calls=%async_computation.5 | async-start | bytes 1048576 | tf_op jit(solution)/shard_map/all_to_all | solution.py:330
  178.4 21.7 %all-to-all-done.5 = bf16[512,3,128]{2,1,0:T(4,128)(2,1)S(1)} async-done(((bf16[512,3,128]{2,1,0:T(4,128)(2,1)}), bf16[512,3,128]{2,1,0:T(4,128)(2,1)S(1)}, u32[]{:S(2)}, u32[]{:S(2)}) %all-to-all-start.5) | async-done | bytes 393248 | tf_op jit(solution)/shard_map/all_to_all | solution.py:330
  200.9 3.6 %convolution_convert_fusion = bf16[2304,64]{0,1:T(8,128)(2,1)S(1)} fusion(bf16[512,2304]{1,0:T(8,128)(2,1)} %constant_dynamic-update-slice_fusion, f32[64,512]{1,0:T(8,128)S(1)} %reshape.169, bf16[512,2048]{1,0:T(8,128)(2,1)} %copy-done.8, bf16[64,2048]{1,0:T(8,128)(2,1)S(1)} %copy-done.4, f32[64,512]{1,0:T(8,128)S(1)} %copy-done.13, ...), kind=kOutput, calls=%fused_computation.8 | convolution fusion | flops 286146560 | bytes 5280000 | tf_op jit(solution)/shard_map/dot_general | solution.py:25
  206.3 1.1 copy.141
  207.4 9.0 %all-to-all-start.6 = ((bf16[512,3,128]{2,1,0:T(4,128)(2,1)}), bf16[512,3,128]{2,1,0:T(4,128)(2,1)S(1)}, u32[]{:S(2)}, u32[]{:S(2)}) async-start(bf16[512,3,128]{2,1,0:T(4,128)(2,1)} %copy.141), calls=%async_computation.6 | async-start | bytes 1048576 | tf_op jit(solution)/shard_map/all_to_all | solution.py:346
  217.0 21.5 %all-to-all-done.6 = bf16[512,3,128]{2,1,0:T(4,128)(2,1)S(1)} async-done(((bf16[512,3,128]{2,1,0:T(4,128)(2,1)}), bf16[512,3,128]{2,1,0:T(4,128)(2,1)S(1)}, u32[]{:S(2)}, u32[]{:S(2)}) %all-to-all-start.6) | async-done | bytes 393248 | tf_op jit(solution)/shard_map/all_to_all | solution.py:346
  238.9 0.7 dynamic_slice.3
  (110 shorter events, 8.6 us)
Async XLA Ops:
  0.6 61.7 %copy-start = (bf16[2048,256]{1,0:T(8,128)(2,1)S(1)}, bf16[2048,256]{1,0:T(8,128)(2,1)}, u32[]{:S(2)}) copy-start(bf16[2048,256]{1,0:T(8,128)(2,1)} %param.19) | copy-start | bytes 3145732
  3.3 11.6 %copy-start.4 = (bf16[64,2048]{1,0:T(8,128)(2,1)S(1)}, bf16[64,2048]{1,0:T(8,128)(2,1)}, u32[]{:S(2)}) copy-start(bf16[64,2048]{1,0:T(8,128)(2,1)} %own_embed_ref.1) | copy-start | bytes 786436
  3.4 16.9 %copy-start.16 = (bf16[2,2048]{1,0:T(2,128)(2,1)S(1)}, bf16[2,2048]{1,0:T(2,128)(2,1)}, u32[]{:S(2)}) copy-start(bf16[2,2048]{1,0:T(2,128)(2,1)} %param.16) | copy-start | bytes 24580
  3.4 17.0 %copy-start.17 = (bf16[2048]{0:T(1024)(128)(2,1)S(1)}, bf16[2048]{0:T(1024)(128)(2,1)}, u32[]{:S(2)}) copy-start(bf16[2048]{0:T(1024)(128)(2,1)} %param.17) | copy-start | bytes 12292
  3.4 17.0 %copy-start.22 = (s32[5]{0:T(128)S(1)}, s32[5]{0:T(128)}, u32[]{:S(2)}) copy-start(s32[5]{0:T(128)} %param.24) | copy-start | bytes 64
  3.4 17.0 %copy-start.14 = (bf16[64,2048]{1,0:T(8,128)(2,1)S(1)}, bf16[64,2048]{1,0:T(8,128)(2,1)}, u32[]{:S(2)}) copy-start(bf16[64,2048]{1,0:T(8,128)(2,1)} %param.23) | copy-start | bytes 786436
  4.6 31.7 %all-to-all-start = ((bf16[4,544,128]{2,1,0:T(8,128)(2,1)}), bf16[4,544,128]{2,1,0:T(8,128)(2,1)S(1)}, u32[]{:S(2)}, u32[]{:S(2)}) async-start(bf16[4,544,128]{2,1,0:T(8,128)(2,1)} %copy.119), calls=%async_computation | async-start | bytes 1114112 | tf_op jit(solution)/shard_map/all_to_all | solution.py:207
  17.0 17.4 %collective-permute-start = (bf16[128,2048]{1,0:T(8,128)(2,1)S(1)}, bf16[128,2048]{1,0:T(8,128)(2,1)}, u32[]{:S(2)}, u32[]{:S(2)}) collective-permute-start(bf16[128,2048]{1,0:T(8,128)(2,1)S(1)} %all_gather.7), channel_id=1, source_target_pairs={{0,2},{2,0},{1,3},{3,1},{4,6},{6,4},{5,7},{7,5},{8,10},{10,8},{9,1... | collective-permute-start | bytes 1572872 | tf_op jit(solution)/shard_map/ppermute | solution.py:193
  36.3 25.0 %copy-start.9 = (bf16[128,2048]{1,0:T(8,128)(2,1)}, bf16[128,2048]{1,0:T(8,128)(2,1)S(1)}, u32[]{:S(2)}) copy-start(bf16[128,2048]{1,0:T(8,128)(2,1)S(1)} %get-tuple-element.16) | copy-start | bytes 1572868
  47.5 13.9 %copy-start.11 = (bf16[128,2048]{1,0:T(8,128)(2,1)S(1)}, bf16[128,2048]{1,0:T(8,128)(2,1)}, u32[]{:S(2)}) copy-start(bf16[128,2048]{1,0:T(8,128)(2,1)} %get-tuple-element.17) | copy-start | bytes 1572868
  62.3 3.0 %copy-start.8 = (bf16[512,2048]{1,0:T(8,128)(2,1)}, bf16[512,2048]{1,0:T(8,128)(2,1)S(1)}, u32[]{:S(2)}) copy-start(bf16[512,2048]{1,0:T(8,128)(2,1)S(1)} %get-tuple-element.36) | copy-start | bytes 6291460
  62.4 2.0 copy-start.19
  64.3 1.2 copy-start.21
  68.1 17.1 %copy-start.18 = (bf16[2048]{0:T(1024)(128)(2,1)S(1)}, bf16[2048]{0:T(1024)(128)(2,1)}, u32[]{:S(2)}) copy-start(bf16[2048]{0:T(1024)(128)(2,1)} %param.18) | copy-start | bytes 12292
  69.8 43.8 %copy-start.1 = (bf16[256,2048]{1,0:T(8,128)(2,1)S(1)}, bf16[256,2048]{1,0:T(8,128)(2,1)}, u32[]{:S(2)}) copy-start(bf16[256,2048]{1,0:T(8,128)(2,1)} %out_weight_ref.3) | copy-start | bytes 3145732
  69.8 42.3 %all-to-all-start.1 = ((bf16[128,4,896]{2,1,0:T(4,128)(2,1)}), bf16[128,4,896]{2,1,0:T(4,128)(2,1)}, u32[]{:S(2)}, u32[]{:S(2)}) async-start(bf16[128,4,896]{2,1,0:T(4,128)(2,1)} %fusion.15), calls=%async_computation.1 | async-start | bytes 1835008 | tf_op jit(solution)/shard_map/all_to_all | solution.py:253
  114.9 1.0 copy-start.5
  117.7 12.9 %all-to-all-start.2 = ((f32[16,17,128]{2,1,0:T(8,128)}), f32[16,17,128]{2,1,0:T(8,128)S(1)}, u32[]{:S(2)}, u32[]{:S(2)}) async-start(f32[16,17,128]{2,1,0:T(8,128)} %broadcast_in_dim.19), calls=%async_computation.2 | async-start | bytes 393216 | tf_op jit(solution)/shard_map/all_to_all | solution.py:277
  124.0 2.6 %copy-start.10 = (bf16[128,2048]{1,0:T(8,128)(2,1)S(1)}, bf16[128,2048]{1,0:T(8,128)(2,1)}, u32[]{:S(2)}) copy-start(bf16[128,2048]{1,0:T(8,128)(2,1)} %copy-done.9) | copy-start | bytes 1572868
  124.0 2.6 %copy-start.12 = (bf16[128,2048]{1,0:T(8,128)(2,1)S(1)}, bf16[128,2048]{1,0:T(8,128)(2,1)}, u32[]{:S(2)}) copy-start(bf16[128,2048]{1,0:T(8,128)(2,1)} %get-tuple-element.17) | copy-start | bytes 1572868
  124.0 2.6 %copy-start.20 = (bf16[2048,256]{1,0:T(8,128)(2,1)S(1)}, bf16[2048,256]{1,0:T(8,128)(2,1)}, u32[]{:S(2)}) copy-start(bf16[2048,256]{1,0:T(8,128)(2,1)} %param.20) | copy-start | bytes 3145732
  131.4 11.4 %all-to-all-start.3 = ((f32[8,20,128]{2,1,0:T(8,128)}), f32[8,20,128]{2,1,0:T(8,128)}, u32[]{:S(2)}, u32[]{:S(2)}) async-start(f32[8,20,128]{2,1,0:T(8,128)} %broadcast_in_dim.20), calls=%async_computation.3 | async-start | bytes 196608 | tf_op jit(solution)/shard_map/all_to_all | solution.py:277
  135.4 2.2 copy-start.15
  145.1 10.3 %all-to-all-start.4 = ((f32[4,48,128]{2,1,0:T(8,128)}), f32[4,48,128]{2,1,0:T(8,128)S(1)}, u32[]{:S(2)}, u32[]{:S(2)}) async-start(f32[4,48,128]{2,1,0:T(8,128)} %broadcast_in_dim.21), calls=%async_computation.4 | async-start | bytes 196608 | tf_op jit(solution)/shard_map/all_to_all | solution.py:277
  155.6 1.1 copy-start.2
  156.7 1.1 copy-start.3
  157.9 1.2 copy-start.6
  161.8 0.7 copy-start.7
  164.2 36.7 %copy-start.13 = (f32[64,512]{1,0:T(8,128)S(1)}, f32[64,512]{1,0:T(8,128)}, u32[]{:S(2)}) copy-start(f32[64,512]{1,0:T(8,128)} %get-tuple-element.35) | copy-start | bytes 393220
  165.6 34.6 %all-to-all-start.5 = ((bf16[512,3,128]{2,1,0:T(4,128)(2,1)}), bf16[512,3,128]{2,1,0:T(4,128)(2,1)S(1)}, u32[]{:S(2)}, u32[]{:S(2)}) async-start(bf16[512,3,128]{2,1,0:T(4,128)(2,1)} %bitcast.39), calls=%async_computation.5 | async-start | bytes 1048576 | tf_op jit(solution)/shard_map/all_to_all | solution.py:330
  207.4 31.0 %all-to-all-start.6 = ((bf16[512,3,128]{2,1,0:T(4,128)(2,1)}), bf16[512,3,128]{2,1,0:T(4,128)(2,1)S(1)}, u32[]{:S(2)}, u32[]{:S(2)}) async-start(bf16[512,3,128]{2,1,0:T(4,128)(2,1)} %copy.141), calls=%async_computation.6 | async-start | bytes 1048576 | tf_op jit(solution)/shard_map/all_to_all | solution.py:346

commit v2 on v1

v2 whole, which is shorter than its diff:
```python
import functools
import math

import jax
import jax.numpy as jnp
from jax import lax
from jax.experimental import pallas as pl
from jax.experimental.pallas import tpu as pltpu
from jax.sharding import Mesh, PartitionSpec as P

HEAD = 128
LANES = 128
EPSILON = 1e-05
BF = jnp.bfloat16
F32 = jnp.float32
T_AXES = ("zh", "y", "x")
S_AXES = ("zl", "core")
FACTORS = {128: (4, 8, 4), 8: (2, 2, 2)}
NT = (((1,), (1,)), ((), ()))
TN = (((0,), (0,)), ((), ()))
VMEM_LIMIT = 20 * 1024 * 1024
LINES = 4
N_S = 4
SPACE_OF_BLOCK = (0, 2, 1, 3)


def dot(lhs, rhs, dims=(((1,), (0,)), ((), ()))):
    return lax.dot_general(lhs, rhs, dims, preferred_element_type=F32)


def thirds(row):
    first = row.astype(BF)
    rest = row - first.astype(F32)
    second = rest.astype(BF)
    third = (rest - second.astype(F32)).astype(BF)
    zero = jnp.zeros((5, row.shape[1]), F32)
    parts = [first.astype(F32), second.astype(F32), third.astype(F32), zero]
    return jnp.concatenate(parts, axis=0).astype(BF)


def halves(values):
    first = values.astype(BF)
    return first, (values - first.astype(F32)).astype(BF)


def in_window(lanes, cols, rows, row_off, col_off):
    lane = lax.broadcasted_iota(jnp.int32, (1, lanes), 1) % (rows * cols)
    row = lane // cols + row_off
    col = lane % cols + col_off
    return ((row >= 0) & (row < rows) & (col >= 0) & (col < cols)).astype(F32)


def offsets():
    return [(a, b) for a in (-1, 0, 1) for b in (-1, 0, 1)]


def stem_kernel(cols, rows, packed_ref, act_ref, slope_ref, tokens_ref, weight_ref):
    n_s = packed_ref.shape[0]
    lanes, channels = tokens_ref.shape
    own = act_ref.shape[0]
    frames = lanes // (rows * cols)
    block = lanes // (frames * n_s)
    lane_blocks = channels // LANES
    count = lane_blocks * frames * block
    half = packed_ref.shape[1] - count
    for s in range(n_s):
        for part in range(lane_blocks):
            for frame in range(frames):
                source = (part * frames + frame) * block
                target = (frame * n_s + s) * block
                tokens_ref[target : target + block, part * LANES : (part + 1) * LANES] = packed_ref[
                    s, source : source + block, :
                ]
        pairs = packed_ref[s, count:, :]
        at = 2 * s * half
        weight_ref[at : at + half, :] = pairs[:, :own]
        weight_ref[at + half : at + 2 * half, :] = pairs[:, own:]
    tokens = tokens_ref[...]
    total = jnp.zeros((own, lanes), F32)
    for tap, (row_off, col_off) in enumerate(offsets()):
        weight = weight_ref[tap * channels : (tap + 1) * channels, :]
        part = dot(weight, tokens, (((0,), (1,)), ((), ())))
        shift = row_off * cols + col_off
        if shift:
            part = pltpu.roll(part, (-shift) % lanes, 1)
        total = total + in_window(lanes, cols, rows, row_off, col_off) * part
    root = math.sqrt(2.0 / math.pi)
    square = total * total
    bent = jnp.tanh(root * (total + 0.044715 * (square * total)))
    half_up = 0.5 * (1.0 + bent)
    act_ref[...] = (total * half_up).astype(BF)
    slope_ref[...] = half_up + 0.5 * total * (1.0 - bent * bent) * (
        root * (1.0 + 3 * 0.044715 * square)
    )


def stem_back_kernel(
    cols,
    rows,
    slots,
    frames,
    got_ref,
    back_unit_ref,
    scale_ref,
    direct_ref,
    slope_ref,
    tokens_ref,
    out_ref,
    grad_ref,
    lines_ref,
):
    lanes, channels = tokens_ref.shape
    own = slope_ref.shape[0]
    depth = got_ref.shape[0] // LINES
    turned = [got_ref[pl.ds(i, depth, stride=LINES), :].T for i in range(slots + 1)]
    unit = jnp.concatenate(
        [turned[s][f * own : (f + 1) * own] for f in range(frames) for s in range(slots)], axis=1
    )
    mean = jnp.concatenate(
        [
            turned[slots][s * frames + f : s * frames + f + 1]
            for f in range(frames)
            for s in range(slots)
        ],
        axis=1,
    )
    grad_act = scale_ref[...] * (unit - mean * back_unit_ref[...]) + direct_ref[:, :1]
    grad_pre = (slope_ref[...] * grad_act).astype(BF).astype(F32)
    tokens = tokens_ref[...]
    for tap, (row_off, col_off) in enumerate(offsets()):
        moved = in_window(lanes, cols, rows, row_off, col_off) * grad_pre
        shift = row_off * cols + col_off
        if shift:
            moved = pltpu.roll(moved, shift % lanes, 1)
        part = dot(tokens, moved.astype(BF), (((0,), (1,)), ((), ())))
        grad_ref[tap * channels : (tap + 1) * channels, :] = part
    count = lines_ref.shape[0]
    lines_ref[...] = jnp.concatenate(
        [grad_ref[pl.ds(i, count, stride=2), :] for i in range(2)], axis=1
    )
    step, window = line_window(count, depth)
    out_lines = out_ref.shape[0] // (N_S * depth)
    blank = jnp.zeros((depth, LANES), F32)
    for s in range(N_S):
        for line in range(out_lines):
            value = blank
            if line < window:
                value = lines_ref[pl.ds(step * s + line, depth, stride=count // depth), :]
            out_ref[pl.ds(s * out_lines + line, depth, stride=N_S * out_lines), :] = value


def line_window(count, depth):
    per = count // depth
    return per // N_S, -(-per // N_S)


def split_heads(block, heads):
    inner = heads * HEAD
    for head in range(heads):
        at = head * HEAD
        yield (
            head,
            block[:, at : at + HEAD],
            block[:, inner + at : inner + at + HEAD],
            block[:, 2 * inner + at : 2 * inner + at + HEAD],
        )


def as_lines(row):
    return jnp.concatenate(
        [row[:, i : i + LANES] for i in range(0, row.shape[1], LANES)], axis=0
    )


def as_row(lines):
    return jnp.concatenate([lines[i : i + 1] for i in range(lines.shape[0])], axis=1)


def forward_kernel(
    heads, qkv_ref, out_weight_ref, embed_sum_ref, rating_ref, back_ref, weights_ref, packed_ref
):
    del back_ref
    slots = qkv_ref.shape[0]
    factor = 1.0 / math.sqrt(HEAD)
    sums = [0.0] * heads
    for slot in range(slots):
        for head, query, key, value in split_heads(qkv_ref[slot], heads):
            scores = dot(key, query, NT) * factor
            top = jnp.max(scores, axis=0, keepdims=True)
            raised = jnp.exp(scores - top)
            weights = raised / jnp.sum(raised, axis=0, keepdims=True)
            weights_ref[slot * heads + head] = weights
            mixture = dot(weights.astype(BF), value, TN).astype(BF).astype(F32)
            sums[head] = sums[head] + jnp.sum(mixture, axis=0, keepdims=True)
    mixture_sum = thirds(jnp.concatenate(sums, axis=1))
    mixed = jnp.sum(dot(mixture_sum, out_weight_ref[...]), axis=0, keepdims=True)
    pooled = as_lines(embed_sum_ref[...] + mixed)
    rating = jnp.sum(rating_ref[...].astype(F32), axis=0, keepdims=True)
    blank = jnp.zeros((packed_ref.shape[1] - pooled.shape[0] - 1, LANES), F32)
    packed = jnp.concatenate([pooled, rating, blank], axis=0)
    for i in range(packed_ref.shape[0]):
        packed_ref[i] = packed


def combine_kernel(lines, per, joint, in_ref, out_ref):
    size = in_ref.shape[0]
    pooled = in_ref[0, :lines]
    for i in range(1, size):
        pooled = pooled + in_ref[i, :lines]
    ratings = []
    for i in range(0, size, joint):
        rating = in_ref[i, lines : lines + per]
        for j in range(1, joint):
            rating = rating + in_ref[i + j, lines : lines + per]
        ratings.append(rating)
    parts = [pooled] + ratings
    left = out_ref.shape[1] - lines - per * len(ratings)
    if left:
        parts.append(jnp.zeros((left, LANES), F32))
    packed = jnp.concatenate(parts, axis=0)
    for i in range(out_ref.shape[0]):
        out_ref[i] = packed


def backward_kernel(
    heads,
    tokens,
    ratings,
    target_ref,
    packed_ref,
    gain_ref,
    out_weight_ref,
    own_embed_ref,
    qkv_ref,
    weights_ref,
    back_ref,
    expected_ref,
    direct_ref,
    sent_ref,
):
    lines = gain_ref.shape[0]
    width = lines * LANES
    pooled = packed_ref[0, :lines]
    for i in range(1, packed_ref.shape[0]):
        pooled = pooled + packed_ref[i, :lines]
    turned = jnp.concatenate([packed_ref[i, lines:] for i in range(packed_ref.shape[0])], axis=0)
    pad = LANES - turned.shape[0]
    if pad:
        turned = jnp.concatenate([turned, jnp.zeros((pad, LANES), F32)], axis=0)
    n_t = packed_ref.shape[0] * (packed_ref.shape[1] - lines)
    turned = turned.T[:, :n_t]
    groups = width // n_t
    rows = [turned[r * groups : (r + 1) * groups] for r in range(ratings)]
    if n_t != LANES:
        rows = [as_lines(as_row(row)) for row in rows]

    def total_of(values):
        return jnp.sum(jnp.sum(values, axis=1, keepdims=True), axis=0, keepdims=True)

    pooled_raw = pooled / tokens
    inverse_rms = lax.rsqrt(total_of(pooled_raw * pooled_raw) / width + EPSILON)
    unit = pooled_raw * inverse_rms
    gain = gain_ref[...].astype(F32)
    gained_unit = unit * gain
    logits = [total_of(row * gained_unit) for row in rows]
    top = functools.reduce(jnp.maximum, logits)
    raised = [jnp.exp(logit - top) for logit in logits]
    norm = sum(raised)
    probs = [value / norm for value in raised]
    expected = sum((r + 1.0) * prob for r, prob in enumerate(probs))
    expected_ref[...] = jnp.broadcast_to(expected, expected_ref.shape)
    target = target_ref[0]
    mixed = sum(
        (prob - jnp.where(target == r + 1, 1.0, 0.0)) * rows[r] for r, prob in enumerate(probs)
    )
    gained = gain * mixed
    centre = total_of(gained * unit) / width
    cotangent = inverse_rms * (gained - unit * centre) / math.sqrt(tokens)
    parts = thirds(as_row(cotangent))
    direct = jnp.sum(dot(own_embed_ref[...], parts, NT), axis=1, keepdims=True)
    direct_ref[...] = jnp.broadcast_to(direct, direct_ref.shape)
    grad_heads = jnp.sum(dot(parts, out_weight_ref[...], NT), axis=0, keepdims=True)
    factor = 1.0 / math.sqrt(HEAD)
    slots, frames = qkv_ref.shape[0], qkv_ref.shape[1]
    depth = frames // 2
    back_upper, back_lower = halves(back_ref[...])
    own = back_ref.shape[1] // N_S
    lane = lax.broadcasted_iota(jnp.int32, (1, LANES), 1)
    means = jnp.zeros((depth, LANES), F32)
    for slot in range(slots):
        grads_q, grads_k, grads_v = [], [], []
        total = jnp.zeros((frames, 1), F32)
        for head, query, key, value in split_heads(qkv_ref[slot], heads):
            grad_mixture = grad_heads[:, head * HEAD : (head + 1) * HEAD]
            weights = weights_ref[slot * heads + head]
            wide_value = value.astype(F32)
            grad_weights = jnp.sum(wide_value * grad_mixture, axis=1, keepdims=True)
            centre = jnp.sum(weights * grad_weights, axis=0, keepdims=True)
            upper, lower = halves(weights * (grad_weights - centre) * factor)
            grad_query = dot(upper, key, TN) + dot(lower, key, TN)
            grad_key = dot(upper, query) + dot(lower, query)
            mass = jnp.sum(weights.astype(BF).astype(F32), axis=1, keepdims=True)
            grad_value = mass * grad_mixture
            total = total + jnp.sum(
                grad_query * query.astype(F32)
                + grad_key * key.astype(F32)
                + grad_value * wide_value,
                axis=1,
                keepdims=True,
            )
            grads_q.append(grad_query.astype(BF))
            grads_k.append(grad_key.astype(BF))
            grads_v.append(grad_value.astype(BF))
        grads = jnp.concatenate(grads_q + grads_k + grads_v, axis=1)
        sent = dot(grads, back_upper) + dot(grads, back_lower)
        for block in range(N_S):
            s = SPACE_OF_BLOCK[block]
            both = [
                sent[f * depth : (f + 1) * depth, block * own : (block + 1) * own]
                for f in range(2)
            ]
            sent_ref[pl.ds(s * LINES + slot, depth, stride=N_S * LINES), :] = jnp.concatenate(
                both, axis=1
            )
        for f in range(2):
            column = total[f * depth : (f + 1) * depth] / width
            means = means + jnp.where(lane == slot * 2 + f, 1.0, 0.0) * column
    blank = jnp.zeros((depth, LANES), F32)
    for s in range(N_S):
        sent_ref[pl.ds(s * LINES + slots, depth, stride=N_S * LINES), :] = means
        for line in range(slots + 1, LINES):
            sent_ref[pl.ds(s * LINES + line, depth, stride=N_S * LINES), :] = blank


def on_device(
    patches,
    stem_weight,
    embed_weight,
    frame_embed,
    attention_gain,
    final_gain,
    query_weight,
    key_weight,
    value_weight,
    output_weight,
    unembedding,
    rating_ids,
    target_score,
):
    n_t = lax.axis_size(T_AXES)
    n_s = lax.axis_size(S_AXES)
    everyone = T_AXES + S_AXES
    space_index = lax.axis_index(S_AXES)
    frames_dev, rows_dev, cols, channels = patches.shape
    own_channels = channels // n_s
    count_rows = rows_dev * n_s
    positions = count_rows * cols
    slots = positions // n_t
    width = embed_weight.shape[1]
    inner = query_weight.shape[1]
    heads = inner // HEAD
    all_frames = frames_dev * n_t
    tokens = all_frames * positions
    tokens_dev = frames_dev * positions
    assert frames_dev == 2 and slots == 2

    whole = pl.BlockSpec(memory_space=pltpu.VMEM)
    params = pltpu.CompilerParams(vmem_limit_bytes=VMEM_LIMIT)
    other = lax.ppermute(embed_weight, "zl", [(0, 1), (1, 0)])

    lane_blocks = channels // LANES
    patch_rows = patches.reshape(-1, channels)
    patch_part = jnp.concatenate(
        [patch_rows[:, i * LANES : (i + 1) * LANES] for i in range(lane_blocks)], axis=0
    )
    stem_half = stem_weight.shape[0] // 2
    stem_part = jnp.stack(
        [
            jnp.concatenate(
                [
                    stem_weight[h * stem_half : (h + 1) * stem_half, c : c + own_channels]
                    for h in range(2)
                ],
                axis=1,
            )
            for c in range(0, channels, own_channels)
        ],
        axis=0,
    )
    packed = jnp.concatenate(
        [jnp.broadcast_to(patch_part[None], (n_s,) + patch_part.shape), stem_part], axis=1
    )
    packed = lax.all_to_all(packed, S_AXES, 0, 0, tiled=True)

    act, gelu_slope, patch_tokens = pl.pallas_call(
        functools.partial(stem_kernel, cols, count_rows),
        name="stem",
        out_shape=(
            jax.ShapeDtypeStruct((own_channels, tokens_dev), BF),
            jax.ShapeDtypeStruct((own_channels, tokens_dev), F32),
            jax.ShapeDtypeStruct((tokens_dev, channels), BF),
        ),
        in_specs=[whole],
        out_specs=(whole,) * 3,
        scratch_shapes=[pltpu.VMEM((9 * channels, own_channels), BF)],
        compiler_params=params,
    )(packed)
    act = lax.all_gather(act, ("core", "zl"), axis=0, tiled=True)

    lower = lax.axis_index("zl") == 0
    pair = jnp.concatenate(
        [jnp.where(lower, embed_weight, other), jnp.where(lower, other, embed_weight)], axis=0
    )
    full_embed = lax.all_gather(pair, "core", axis=0, tiled=True)
    gain = attention_gain.astype(F32)
    embedded = dot(act, full_embed, TN).reshape(frames_dev, positions, width)
    embedded = (embedded + frame_embed.astype(F32)[:, None, :]).astype(BF)
    embedded = embedded.reshape(tokens_dev, width)
    wide = embedded.astype(F32)
    scale = lax.rsqrt(jnp.mean(wide * wide, axis=-1, keepdims=True) + EPSILON)
    normed = (wide * scale * gain).astype(BF)
    qkv = jnp.concatenate(
        [dot(normed, w).astype(BF) for w in (query_weight, key_weight, value_weight)], axis=1
    )
    embed_sum = jnp.sum(wide, axis=0, keepdims=True) * (1.0 / n_s)
    scale_row = scale.reshape(1, tokens_dev)
    back_unit = dot(embed_weight, embedded, NT) * scale_row

    vocab_dev = unembedding.shape[0]
    ratings = rating_ids.shape[0]
    first_row = lax.axis_index(everyone) * vocab_dev
    picks = (rating_ids[:, None] - first_row == jnp.arange(vocab_dev)[None, :]).astype(BF)
    rows_part = dot(picks, unembedding).astype(BF)
    groups = width // n_t
    rating_part = rows_part.reshape(ratings * groups, n_t).T
    rating_part = jnp.pad(rating_part, ((0, 0), (0, LANES - ratings * groups)))
    rating_part = jnp.pad(rating_part[:, None, :], ((0, 0), (0, slots - 1), (0, 0)))

    qkv = qkv.reshape(frames_dev, slots, n_t, 3 * inner)
    moved = jnp.concatenate(
        [qkv[f].transpose(1, 0, 2) for f in range(frames_dev)] + [rating_part], axis=2
    )
    moved = lax.all_to_all(moved, T_AXES, 0, 0, tiled=True)
    qkv = jnp.concatenate(
        [
            moved[:, :, f * 3 * inner : (f + 1) * 3 * inner].transpose(1, 0, 2)
            for f in range(frames_dev)
        ],
        axis=1,
    )
    rating_got = moved[:, 0, frames_dev * 3 * inner :]

    scaled = full_embed.astype(F32) * gain
    back = jnp.concatenate(
        [
            sum(dot(w, part, (((0,), (1,)), ((), ()))) for part in halves(scaled))
            for w in (query_weight, key_weight, value_weight)
        ],
        axis=0,
    )

    items = slots * heads
    lines = width // LANES
    first = lax.axis_size(("x",) + S_AXES)
    weights, packed = pl.pallas_call(
        functools.partial(forward_kernel, heads),
        name="attend",
        out_shape=(
            jax.ShapeDtypeStruct((items, all_frames, all_frames), F32),
            jax.ShapeDtypeStruct((first, lines + 8, LANES), F32),
        ),
        in_specs=[whole] * 4 + [pl.BlockSpec(memory_space=pl.ANY)],
        out_specs=(whole, whole),
        compiler_params=params,
    )(qkv, output_weight, embed_sum, rating_got, back)

    packed = lax.all_to_all(packed, ("x",) + S_AXES, 0, 0, tiled=True)
    size_x, size_y, size_z = (lax.axis_size(axis) for axis in ("x", "y", "zh"))
    for axis, before, joint, out_lines, out_size in (
        ("y", 1, n_s, lines + 8, size_y),
        ("zh", size_x, 1, lines + size_x * size_y, size_z),
    ):
        packed = pl.pallas_call(
            functools.partial(combine_kernel, lines, before, joint),
            name="combine_" + axis,
            out_shape=jax.ShapeDtypeStruct((out_size, out_lines, LANES), F32),
            in_specs=[whole],
            out_specs=whole,
            compiler_params=params,
        )(packed)
        packed = lax.all_to_all(packed, axis, 0, 0, tiled=True)

    expected, direct, sent = pl.pallas_call(
        functools.partial(backward_kernel, heads, float(tokens), ratings),
        name="attend_back",
        out_shape=(
            jax.ShapeDtypeStruct((8, LANES), F32),
            jax.ShapeDtypeStruct((own_channels, LANES), F32),
            jax.ShapeDtypeStruct((n_t * n_s * LINES, LANES), F32),
        ),
        in_specs=[pl.BlockSpec(memory_space=pltpu.SMEM)] + [whole] * 7,
        out_specs=(whole,) * 3,
        compiler_params=params,
    )(
        target_score,
        packed,
        final_gain.reshape(lines, LANES),
        output_weight,
        embed_weight,
        qkv,
        weights,
        back,
    )

    sent = sent.astype(BF).reshape(n_t * n_s, LINES, LANES)
    sent = lax.all_to_all(sent, everyone, 0, 0, tiled=True)
    got = jnp.sum(sent.reshape(n_t, n_s, LINES, LANES).astype(F32), axis=1)

    count = 9 * channels * own_channels // LANES
    step, window = line_window(count, n_t)
    out_lines = -(-window // 4) * 4
    sums = pl.pallas_call(
        functools.partial(stem_back_kernel, cols, count_rows, slots, frames_dev),
        name="stem_back",
        out_shape=jax.ShapeDtypeStruct((n_t * n_s * out_lines, LANES), F32),
        in_specs=[whole] * 6,
        out_specs=whole,
        scratch_shapes=[
            pltpu.VMEM((9 * channels, own_channels), F32),
            pltpu.VMEM((count, LANES), F32),
        ],
        compiler_params=params,
    )(got.reshape(n_t * LINES, LANES), back_unit, scale_row, direct, gelu_slope, patch_tokens)
    sums = sums.astype(BF).reshape(n_t * n_s, out_lines, LANES)
    sums = lax.all_to_all(sums, everyone, 0, 0, tiled=True)
    sums = jnp.sum(sums.reshape(n_t, n_s, out_lines, LANES).astype(F32), axis=0)[:, :window]
    flat = sums.reshape(n_s, -1, own_channels).transpose(1, 0, 2).reshape(-1)
    length = 9 * channels * channels // (n_t * n_s)
    start = space_index * (length - step * LANES * n_s)
    stem_gradient = lax.dynamic_slice_in_dim(flat, start, length, 0)
    return (expected[0, :1], stem_gradient)


def solution(mesh):
    shape = FACTORS[mesh.shape["tm"]] + (2, 2)
    split = Mesh(mesh.devices.reshape(shape), T_AXES + S_AXES)
    both = T_AXES + S_AXES
    in_specs = (
        P(T_AXES, S_AXES, None, None),
        P(S_AXES, None),
        P(S_AXES, None),
        P(T_AXES, None),
        P(),
        P(),
        P(None, S_AXES),
        P(None, S_AXES),
        P(None, S_AXES),
        P(S_AXES, None),
        P(both, None),
        P(),
        P(),
    )
    return jax.shard_map(
        on_device, mesh=split, in_specs=in_specs, out_specs=(P(), P(both)), check_vma=False
    )
```

time: 241 us -> 224 us (0.929)
  local copies, waits for them, and re-layouts: 47 us -> 14.8 us
  blocking collectives: 8.74 us -> 34.4 us
  between operations: 2 us -> 15.2 us
  waiting for transfers between devices: 89.2 us -> 76.4 us
  starting transfers between devices: 64.3 us -> 55.8 us
  matrix products: 16.6 us -> 11.8 us
  Pallas kernels: 4.05 us -> 7.59 us
    all_to_all x0 -> x2, blocking collectives: none -> 23.5 us  [the longest x1 12.5 us: on_device(): packed = lax.all_to_all(packed, ('x',) + S_AXES, 0, 0, tiled=True)]
    unnamed x61 -> x40, local copies, waits for them, and re-layouts: 20.2 us -> 6.86 us
    ppermute x1, waiting for transfers between devices: 13.5 us -> 1.63 us  [on_device(): other = lax.ppermute(embed_weight, 'zl', [(0, 1), (1, 0)])]
    all_to_all x4 -> x2, starting transfers between devices: 22.6 us -> 12.4 us  [the longest x1 9.08 us: on_device(): sums = lax.all_to_all(sums, everyone, 0, 0, tiled=True)]
    reshape x13 -> x2, local copies, waits for them, and re-layouts: 7.4 us -> 0.16 us  [on_device(): flat = sums.reshape(n_s, -1, own_channels).transpose(1, 0, 2).reshape(-1)]
    all_to_all x1, waiting for transfers between devices: 0.01 us -> 7.1 us  [on_device(): packed = lax.all_to_all(packed, S_AXES, 0, 0, tiled=True)]
    concatenate x5 -> x0, local copies, waits for them, and re-layouts: 6.47 us -> none  [the longest x1 2.36 us: on_device(): jnp.concatenate([blank, back], axis=2).reshape(3 * inner, sent_width)]
    all_to_all x1, waiting for transfers between devices: 26.2 us -> 20.2 us  [on_device(): moved = lax.all_to_all(moved, T_AXES, 0, 0, tiled=True)]
  transfers between devices with their start and end apart: 8 -> 7, of which waited for: 7 -> 6; matrix products, arithmetic and copies ran while one was open for 7% -> 5% of each run, Pallas kernels for 0% -> 1%
where the time goes in v2:
time: 224 us; the launch traced here: 223 us
  waiting for transfers between devices  76.4 us (34%)
  starting transfers between devices  55.8 us (25%)
  blocking collectives  34.4 us (15%)
  between operations  15.2 us (7%)
  local copies, waits for them, and re-layouts  14.8 us (7%)
  matrix products  11.8 us (5%)
  Pallas kernels  7.59 us (3%)
  other arithmetic  7.05 us (3%)
    all_to_all x1, waiting for transfers between devices, on_device(): sums = lax.all_to_all(sums, everyone, 0, 0, tiled=True)  21.5 us
    all_to_all x1, waiting for transfers between devices, on_device(): moved = lax.all_to_all(moved, T_AXES, 0, 0, tiled=True)  20.2 us
    all_to_all x1, waiting for transfers between devices, on_device(): sent = lax.all_to_all(sent, everyone, 0, 0, tiled=True)  19.6 us
    all_to_all x1, starting transfers between devices, on_device(): moved = lax.all_to_all(moved, T_AXES, 0, 0, tiled=True)  16.9 us
    all_to_all x1, blocking collectives, on_device(): packed = lax.all_to_all(packed, ('x',) + S_AXES, 0, 0, tiled=True)  12.5 us
    dot_general x12, matrix products, dot(): return lax.dot_general(lhs, rhs, dims, preferred_element_type=F32)  11.8 us
    all_to_all x1, starting transfers between devices, on_device(): sent = lax.all_to_all(sent, everyone, 0, 0, tiled=True)  11.5 us
    all_to_all x1, blocking collectives, on_device(): packed = lax.all_to_all(packed, axis, 0, 0, tiled=True)  11 us
  transfers between devices with their start and end apart: 7, of which 6 were waited for; matrix products, arithmetic and copies ran while one was open for 5% of the time, Pallas kernels for 1%

profile of v2, /device:TPU:1, one launch (start us, length us, event | category | flops | bytes accessed | tf_op | source)
XLA Modules:
  0.0 223.0 jit_solution(14425940411701760169)
XLA Ops:
  7.2 4.9 %collective-permute-start = (bf16[64,2048]{1,0:T(8,128)(2,1)}, bf16[64,2048]{1,0:T(8,128)(2,1)S(1)}, u32[]{:S(2)}, u32[]{:S(2)}) collective-permute-start(bf16[64,2048]{1,0:T(8,128)(2,1)} %own_embed_ref.1), channel_id=1, source_target_pairs={{0,2},{2,0},{1,3},{3,1},{4,6},{6,4},{5,7},{7,5},{8,10},{10,8},{9,1... | collective-permute-start | bytes 786440 | tf_op jit(solution)/shard_map/ppermute | solution.py:369
  12.2 0.8 fusion.44
  13.0 1.3 fusion.43
  14.3 0.1 maximum_bitcast_fusion
  14.4 0.1 maximum_bitcast_fusion.2
  14.5 1.6 collective-permute-done
  16.2 0.9 pad_maximum_fusion.3
  17.2 0.8 maximum_maximum_fusion
  18.0 10.0 %all-to-all-start = ((bf16[4,544,128]{2,1,0:T(8,128)(2,1)}), bf16[4,544,128]{2,1,0:T(8,128)(2,1)S(1)}, u32[]{:S(2)}, u32[]{:S(2)}) async-start(bf16[4,544,128]{2,1,0:T(8,128)(2,1)} %maximum_maximum_fusion), calls=%async_computation | async-start | bytes 1114112 | tf_op jit(solution)/shard_map/all_to_all | solution.py:393
  28.1 0.2 convolution_convert_fusion
  28.3 0.7 copy.31
  29.1 7.1 %all-to-all-done.packed_ref = bf16[4,544,128]{2,1,0:T(8,128)(2,1)S(1)} async-done(((bf16[4,544,128]{2,1,0:T(8,128)(2,1)}), bf16[4,544,128]{2,1,0:T(8,128)(2,1)S(1)}, u32[]{:S(2)}, u32[]{:S(2)}) %all-to-all-start) | async-done | bytes 557088 | tf_op jit(solution)/shard_map/all_to_all | solution.py:393
  36.2 1.2 stem.1
  37.4 10.9 %all_gather.6 = bf16[256,512]{1,0:T(8,128)(2,1)S(1)} all-gather(bf16[64,512]{1,0:T(8,128)(2,1)S(1)} %get-tuple-element.10), channel_id=1, replica_groups=mesh['zh'=4,'y'=8,'x'=4,'zl'=2,'core'=2] {'core','zl'}, dimensions={0}, use_global_device_ids=true | all-gather | bytes 327680 | tf_op jit(solution)/shard_map/all_gather | solution.py:408
  48.4 2.8 %convert_reduce_fusion = (f32[2048]{0:T(1024)}, f32[512]{0:T(512)S(1)}, bf16[512,2048]{1,0:T(8,128)(2,1)S(1)}) fusion(f32[2,2048]{1,0:T(2,128)S(1)} %convert_element_type.69, bf16[256,512]{1,0:T(8,128)(2,1)S(1)} %all_gather.6, bf16[256,2048]{1,0:T(8,128)(2,1)} %all-gather.2.cloned.1.call-done), kind=kOutput, calls=%fused_computation | convolution fusion | flops 543159808 | bytes 3434496 | tf_op jit(solution)/shard_map/dot_general | solution.py:28
  51.2 0.9 convolution_convert_fusion.2
  52.1 1.0 copy-done.9
  53.2 0.9 convolution_convert_fusion.1
  54.1 0.3 copy-done.11
  54.4 0.9 convolution_convert_fusion.3
  55.3 0.1 pad_maximum_fusion
  55.4 0.1 fusion.42
  55.5 0.1 squeeze.12
  55.6 0.5 copy.21
  56.1 0.1 squeeze.13
  56.2 1.1 copy.22
  57.3 2.5 %fusion.33 = bf16[128,2,1664]{2,1,0:T(2,128)(2,1)} fusion(bf16[128,1,128]{2,1,0:T(2,128)(2,1)} %copy.31, bf16[128,2,768]{2,1,0:T(2,128)(2,1)} %bitcast.76, bf16[128,2,768]{2,1,0:T(2,128)(2,1)S(1)} %bitcast.75), kind=kLoop, calls=%fused_computation.32 | loop fusion | flops 3407872 | bytes 1671168 | tf_op jit(solution)/shard_map/concatenate | solution.py:440
  59.8 16.9 %all-to-all-start.1 = ((bf16[128,2,1664]{2,1,0:T(2,128)(2,1)}), bf16[128,2,1664]{2,1,0:T(2,128)(2,1)}, u32[]{:S(2)}, u32[]{:S(2)}) async-start(bf16[128,2,1664]{2,1,0:T(2,128)(2,1)} %fusion.33), calls=%async_computation.1 | async-start | bytes 1703936 | tf_op jit(solution)/shard_map/all_to_all | solution.py:443
  76.7 0.6 fusion.35
  77.4 0.6 copy-done.10
  78.0 0.6 fusion.34
  78.6 0.6 copy-done.12
  79.2 0.6 fusion.36
  79.8 0.6 fusion.20
  80.4 0.6 fusion.26
  81.0 0.6 fusion.14
  81.6 0.1 pad_maximum_fusion.2.back_ref
  81.7 20.2 %all-to-all-done.1 = bf16[128,2,1664]{2,1,0:T(2,128)(2,1)} async-done(((bf16[128,2,1664]{2,1,0:T(2,128)(2,1)}), bf16[128,2,1664]{2,1,0:T(2,128)(2,1)}, u32[]{:S(2)}, u32[]{:S(2)}) %all-to-all-start.1) | async-done | bytes 852000 | tf_op jit(solution)/shard_map/all_to_all | solution.py:443
  101.9 0.9 slice.76
  102.8 1.7 fusion.41
  104.7 1.3 attend.1
  106.1 1.0 copy-done.4
  107.1 12.5 %all_to_all.35.in_ref = f32[16,24,128]{2,1,0:T(8,128)S(1)} all-to-all(f32[16,24,128]{2,1,0:T(8,128)S(1)} %get-tuple-element.11), channel_id=1, replica_groups=mesh['zh'=4,'y'=8,'x'=4,'zl'=2,'core'=2] {'x','zl','core'}, dimensions={0} | all-to-all | bytes 393216 | tf_op jit(solution)/shard_map/all_to_all | solution.py:477
  119.6 11.0 %all_to_all.36.in_ref = f32[8,24,128]{2,1,0:T(8,128)S(1)} all-to-all(f32[8,24,128]{2,1,0:T(8,128)S(1)} %combine_y.1), channel_id=1, replica_groups=mesh['zh'=4,'y'=8,'x'=4,'zl'=2,'core'=2] {'y'}, dimensions={0} | all-to-all | bytes 196608 | tf_op jit(solution)/shard_map/all_to_all | solution.py:491
  130.6 0.6 combine_zh.1
  131.2 3.3 %all-to-all-start.4 = ((f32[4,48,128]{2,1,0:T(8,128)}), f32[4,48,128]{2,1,0:T(8,128)S(1)}, u32[]{:S(2)}, u32[]{:S(2)}) async-start(f32[4,48,128]{2,1,0:T(8,128)} %combine_zh.1), calls=%async_computation.4 | async-start | bytes 196608 | tf_op jit(solution)/shard_map/all_to_all | solution.py:491
  135.2 6.4 %all-to-all-done.4.packed_ref = f32[4,48,128]{2,1,0:T(8,128)S(1)} async-done(((f32[4,48,128]{2,1,0:T(8,128)}), f32[4,48,128]{2,1,0:T(8,128)S(1)}, u32[]{:S(2)}, u32[]{:S(2)}) %all-to-all-start.4) | async-done | bytes 98336 | tf_op jit(solution)/shard_map/all_to_all | solution.py:491
  141.6 1.2 copy-done.2
  142.8 1.2 copy-done.5
  144.0 3.0 %attend_back.1 = (f32[8,128]{1,0:T(8,128)S(1)}, f32[64,128]{1,0:T(8,128)S(1)}, f32[2048,128]{1,0:T(8,128)S(1)}) custom-call(s32[1]{0:T(128)S(6)} %copy.38.target_ref, f32[4,48,128]{2,1,0:T(8,128)S(1)} %all-to-all-done.4.packed_ref, bf16[16,128]{1,0:T(8,128)(2,1)S(1)} %bitcast.71, bf16[256,2048]{1,0:T(8,128)(2,1)S(1)} %copy-done.2, ...), custom_call_target="tpu_custom_call" | custom-call | tf_op jit(solution)/shard_map/attend_back/pallas_call | solution.py:493
  147.0 0.9 convert_element_type.82
  147.8 11.5 %all-to-all-start.5 = ((bf16[512,4,128]{2,1,0:T(4,128)(2,1)}), bf16[512,4,128]{2,1,0:T(4,128)(2,1)S(1)}, u32[]{:S(2)}, u32[]{:S(2)}) async-start(bf16[512,4,128]{2,1,0:T(4,128)(2,1)} %bitcast.19), calls=%async_computation.5 | async-start | bytes 1048576 | tf_op jit(solution)/shard_map/all_to_all | solution.py:516
  159.4 2.4 %fusion.29.back_unit_ref = f32[64,512]{1,0:T(8,128)S(1)} fusion(bf16[512,2048]{1,0:T(8,128)(2,1)} %copy-done.8, bf16[64,2048]{1,0:T(8,128)(2,1)S(1)} %copy-done.3, f32[512]{0:T(512)S(1)} %add_rsqrt_fusion), kind=kOutput, calls=%fused_computation.26 | convolution fusion | flops 134250496 | bytes 2492416 | tf_op jit(solution)/shard_map/dot_general | solution.py:28
  161.7 19.6 %all-to-all-done.5 = bf16[512,4,128]{2,1,0:T(4,128)(2,1)S(1)} async-done(((bf16[512,4,128]{2,1,0:T(4,128)(2,1)}), bf16[512,4,128]{2,1,0:T(4,128)(2,1)S(1)}, u32[]{:S(2)}, u32[]{:S(2)}) %all-to-all-start.5) | async-done | bytes 524320 | tf_op jit(solution)/shard_map/all_to_all | solution.py:516
  181.4 0.4 convert_reduce_fusion.2
  181.7 1.4 stem_back.1
  183.1 0.9 convert_element_type.85
  184.0 9.1 %all-to-all-start.6 = ((bf16[512,4,128]{2,1,0:T(4,128)(2,1)}), bf16[512,4,128]{2,1,0:T(4,128)(2,1)S(1)}, u32[]{:S(2)}, u32[]{:S(2)}) async-start(bf16[512,4,128]{2,1,0:T(4,128)(2,1)} %bitcast.24), calls=%async_computation.6 | async-start | bytes 1048576 | tf_op jit(solution)/shard_map/all_to_all | solution.py:535
  193.1 0.5 slice.68
  193.6 21.5 %all-to-all-done.6 = bf16[512,4,128]{2,1,0:T(4,128)(2,1)S(1)} async-done(((bf16[512,4,128]{2,1,0:T(4,128)(2,1)}), bf16[512,4,128]{2,1,0:T(4,128)(2,1)S(1)}, u32[]{:S(2)}, u32[]{:S(2)}) %all-to-all-start.6) | async-done | bytes 524320 | tf_op jit(solution)/shard_map/all_to_all | solution.py:535
  215.1 0.3 convert_reduce_fusion.1
  215.3 0.1 reshape.90
  215.4 0.1 reshape.91
  215.5 0.7 dynamic_slice.3
  (48 shorter events, 0.5 us)
Async XLA Ops:
  7.2 44.0 %copy-start = (bf16[2048,256]{1,0:T(8,128)(2,1)S(1)}, bf16[2048,256]{1,0:T(8,128)(2,1)}, u32[]{:S(2)}) copy-start(bf16[2048,256]{1,0:T(8,128)(2,1)} %param.20) | copy-start | bytes 3145732
  7.2 9.0 %copy-start.3 = (bf16[64,2048]{1,0:T(8,128)(2,1)S(1)}, bf16[64,2048]{1,0:T(8,128)(2,1)}, u32[]{:S(2)}) copy-start(bf16[64,2048]{1,0:T(8,128)(2,1)} %own_embed_ref.1) | copy-start | bytes 786436
  7.2 41.2 %all-gather.2.cloned.1.call-start = ((), (), s32[]{:S(2)}) async-start(), calls=%async_computation.7 | async-start | bytes 1572864 | tf_op jit(solution)/shard_map/all_gather | solution.py:414
  7.2 8.9 %collective-permute-start = (bf16[64,2048]{1,0:T(8,128)(2,1)}, bf16[64,2048]{1,0:T(8,128)(2,1)S(1)}, u32[]{:S(2)}, u32[]{:S(2)}) collective-permute-start(bf16[64,2048]{1,0:T(8,128)(2,1)} %own_embed_ref.1), channel_id=1, source_target_pairs={{0,2},{2,0},{1,3},{3,1},{4,6},{6,4},{5,7},{7,5},{8,10},{10,8},{9,1... | collective-permute-start | bytes 786440 | tf_op jit(solution)/shard_map/ppermute | solution.py:369
  16.2 11.8 %copy-start.16 = (bf16[2048]{0:T(1024)(128)(2,1)S(1)}, bf16[2048]{0:T(1024)(128)(2,1)}, u32[]{:S(2)}) copy-start(bf16[2048]{0:T(1024)(128)(2,1)} %param.17) | copy-start | bytes 12292
  16.2 11.8 %copy-start.15 = (bf16[2,2048]{1,0:T(2,128)(2,1)S(1)}, bf16[2,2048]{1,0:T(2,128)(2,1)}, u32[]{:S(2)}) copy-start(bf16[2,2048]{1,0:T(2,128)(2,1)} %param.16) | copy-start | bytes 24580
  16.2 11.8 %copy-start.17 = (s32[5]{0:T(128)S(1)}, s32[5]{0:T(128)}, u32[]{:S(2)}) copy-start(s32[5]{0:T(128)} %param.24) | copy-start | bytes 64
  16.2 11.8 %copy-start.13 = (bf16[64,2048]{1,0:T(8,128)(2,1)S(1)}, bf16[64,2048]{1,0:T(8,128)(2,1)}, u32[]{:S(2)}) copy-start(bf16[64,2048]{1,0:T(8,128)(2,1)} %param.23) | copy-start | bytes 786436
  18.0 18.2 %all-to-all-start = ((bf16[4,544,128]{2,1,0:T(8,128)(2,1)}), bf16[4,544,128]{2,1,0:T(8,128)(2,1)S(1)}, u32[]{:S(2)}, u32[]{:S(2)}) async-start(bf16[4,544,128]{2,1,0:T(8,128)(2,1)} %maximum_maximum_fusion), calls=%async_computation | async-start | bytes 1114112 | tf_op jit(solution)/shard_map/all_to_all | solution.py:393
  51.2 3.0 %copy-start.8 = (bf16[512,2048]{1,0:T(8,128)(2,1)}, bf16[512,2048]{1,0:T(8,128)(2,1)S(1)}, u32[]{:S(2)}) copy-start(bf16[512,2048]{1,0:T(8,128)(2,1)S(1)} %get-tuple-element.36) | copy-start | bytes 6291460
  51.2 2.0 copy-start.9
  53.2 1.2 copy-start.11
  56.2 20.6 %copy-start.7 = (bf16[256,2048]{1,0:T(8,128)(2,1)S(1)}, bf16[256,2048]{1,0:T(8,128)(2,1)}, u32[]{:S(2)}) copy-start(bf16[256,2048]{1,0:T(8,128)(2,1)} %all-gather.2.cloned.1.call-done) | copy-start | bytes 3145732
  59.8 42.1 %all-to-all-start.1 = ((bf16[128,2,1664]{2,1,0:T(2,128)(2,1)}), bf16[128,2,1664]{2,1,0:T(2,128)(2,1)}, u32[]{:S(2)}, u32[]{:S(2)}) async-start(bf16[128,2,1664]{2,1,0:T(2,128)(2,1)} %fusion.33), calls=%async_computation.1 | async-start | bytes 1703936 | tf_op jit(solution)/shard_map/all_to_all | solution.py:443
  76.7 1.2 copy-start.10
  78.0 1.2 copy-start.12
  81.0 0.7 copy-start.14
  102.8 1.9 copy-start.1
  104.7 36.9 %copy-start.6 = (bf16[2048]{0:T(1024)(128)(2,1)S(1)}, bf16[2048]{0:T(1024)(128)(2,1)}, u32[]{:S(2)}) copy-start(bf16[2048]{0:T(1024)(128)(2,1)} %param.18) | copy-start | bytes 12292
  106.1 1.0 copy-start.4
  131.2 10.3 %all-to-all-start.4 = ((f32[4,48,128]{2,1,0:T(8,128)}), f32[4,48,128]{2,1,0:T(8,128)S(1)}, u32[]{:S(2)}, u32[]{:S(2)}) async-start(f32[4,48,128]{2,1,0:T(8,128)} %combine_zh.1), calls=%async_computation.4 | async-start | bytes 196608 | tf_op jit(solution)/shard_map/all_to_all | solution.py:491
  141.6 1.2 copy-start.2
  142.8 1.2 copy-start.5
  147.8 33.5 %all-to-all-start.5 = ((bf16[512,4,128]{2,1,0:T(4,128)(2,1)}), bf16[512,4,128]{2,1,0:T(4,128)(2,1)S(1)}, u32[]{:S(2)}, u32[]{:S(2)}) async-start(bf16[512,4,128]{2,1,0:T(4,128)(2,1)} %bitcast.19), calls=%async_computation.5 | async-start | bytes 1048576 | tf_op jit(solution)/shard_map/all_to_all | solution.py:516
  184.0 31.1 %all-to-all-start.6 = ((bf16[512,4,128]{2,1,0:T(4,128)(2,1)}), bf16[512,4,128]{2,1,0:T(4,128)(2,1)S(1)}, u32[]{:S(2)}, u32[]{:S(2)}) async-start(bf16[512,4,128]{2,1,0:T(4,128)(2,1)} %bitcast.24), calls=%async_computation.6 | async-start | bytes 1048576 | tf_op jit(solution)/shard_map/all_to_all | solution.py:535
Sparse Core Ops, SparseCore 0:
  17.2 25.4 all-gather.1

commit v3 on v2

--- a/solution.py
+++ b/solution.py
@@ -18,7 +18,7 @@
 FACTORS = {128: (4, 8, 4), 8: (2, 2, 2)}
 NT = (((1,), (1,)), ((), ()))
 TN = (((0,), (0,)), ((), ()))
-VMEM_LIMIT = 20 * 1024 * 1024
+VMEM_LIMIT = 40 * 1024 * 1024
 LINES = 4
 N_S = 4
 SPACE_OF_BLOCK = (0, 2, 1, 3)
@@ -108,6 +108,7 @@
     out_ref,
     grad_ref,
     lines_ref,
+    wide_ref,
 ):
     lanes, channels = tokens_ref.shape
     own = slope_ref.shape[0]
@@ -146,7 +147,8 @@
             value = blank
             if line < window:
                 value = lines_ref[pl.ds(step * s + line, depth, stride=count // depth), :]
-            out_ref[pl.ds(s * out_lines + line, depth, stride=N_S * out_lines), :] = value
+            wide_ref[pl.ds(s * out_lines + line, depth, stride=N_S * out_lines), :] = value
+    out_ref[...] = wide_ref[...].astype(BF)
 
 
 def line_window(count, depth):
@@ -176,26 +178,124 @@
     return jnp.concatenate([lines[i : i + 1] for i in range(lines.shape[0])], axis=1)
 
 
+def pack_kernel(patches_ref, stem_ref, out_ref):
+    count = patches_ref.shape[0]
+    lane_blocks = patches_ref.shape[1] // LANES
+    half = stem_ref.shape[0] // 2
+    own = stem_ref.shape[1] // N_S
+    for s in range(N_S):
+        for i in range(lane_blocks):
+            out_ref[s, i * count : (i + 1) * count, :] = patches_ref[:, i * LANES : (i + 1) * LANES]
+        pair = [stem_ref[h * half : (h + 1) * half, s * own : (s + 1) * own] for h in range(2)]
+        out_ref[s, lane_blocks * count :, :] = jnp.concatenate(pair, axis=1)
+
+
+def chunk_rows(n_t, chunks, chunk, frame):
+    return pl.ds(2 * chunk + frame, n_t, stride=2 * chunks)
+
+
+def embed_kernel(
+    n_t,
+    slots,
+    place_ref,
+    ids_ref,
+    act_ref,
+    pair_ref,
+    across_ref,
+    frame_ref,
+    gain_ref,
+    query_ref,
+    key_ref,
+    value_ref,
+    own_embed_ref,
+    vocab_ref,
+    moved_ref,
+    embed_sum_ref,
+    scale_ref,
+    back_unit_ref,
+    wide_ref,
+):
+    core = place_ref[0]
+    width = frame_ref.shape[1]
+    frames = frame_ref.shape[0]
+    tokens = act_ref.shape[1] // frames
+    inner = query_ref.shape[1]
+    near = pair_ref.shape[0]
+    per = 3 * inner // LANES
+    chunks = slots * per + 1
+    gain = gain_ref[...].astype(F32)
+    here = pl.multiple_of(core * near, near)
+    there = pl.multiple_of((1 - core) * near, near)
+    embed_sum = jnp.zeros((1, width), F32)
+    for frame in range(frames):
+        at = frame * tokens
+        mine = act_ref[pl.ds(here, near), at : at + tokens]
+        other = act_ref[pl.ds(there, near), at : at + tokens]
+        made = dot(mine, pair_ref[...], TN) + dot(other, across_ref[...], TN)
+        embedded = (made + frame_ref[frame : frame + 1, :].astype(F32)).astype(BF)
+        wide = embedded.astype(F32)
+        embed_sum = embed_sum + jnp.sum(wide, axis=0, keepdims=True)
+        scale = lax.rsqrt(jnp.mean(wide * wide, axis=1, keepdims=True) + EPSILON)
+        normed = (wide * scale * gain).astype(BF)
+        scale_row = jnp.broadcast_to(scale, (tokens, LANES)).T[:1]
+        scale_ref[:, at : at + tokens] = scale_row
+        back_unit_ref[:, at : at + tokens] = dot(own_embed_ref[...], embedded, NT) * scale_row
+        for part, weight_ref in enumerate((query_ref, key_ref, value_ref)):
+            made = dot(normed, weight_ref[...])
+            for slot in range(slots):
+                for i in range(inner // LANES):
+                    chunk = slot * per + part * (inner // LANES) + i
+                    wide_ref[chunk_rows(n_t, chunks, chunk, frame), :] = made[
+                        slot * n_t : (slot + 1) * n_t, i * LANES : (i + 1) * LANES
+                    ]
+    embed_sum_ref[...] = embed_sum * (1.0 / N_S)
+    vocab = vocab_ref.shape[0]
+    ratings = ids_ref.shape[0]
+    column = lax.broadcasted_iota(jnp.int32, (1, vocab), 1)
+    picks = [(column == ids_ref[r] - place_ref[1]).astype(F32) for r in range(ratings)]
+    picks.append(jnp.zeros((8 - ratings, vocab), F32))
+    rows = dot(jnp.concatenate(picks, axis=0).astype(BF), vocab_ref[...])
+    groups = width // n_t
+    lines = [
+        rows[r : r + 1, g * n_t : (g + 1) * n_t] for r in range(ratings) for g in range(groups)
+    ]
+    lines.append(jnp.zeros((LANES - ratings * groups, n_t), F32))
+    wide_ref[chunk_rows(n_t, chunks, chunks - 1, 0), :] = jnp.concatenate(lines, axis=0).T
+    wide_ref[chunk_rows(n_t, chunks, chunks - 1, 1), :] = jnp.zeros((n_t, LANES), F32)
+    moved_ref[...] = wide_ref[...].astype(BF)
+
+
+def attention_weights(key, query):
+    scores = dot(key, query, NT) * (1.0 / math.sqrt(HEAD))
+    raised = jnp.exp(scores - jnp.max(scores, axis=0, keepdims=True))
+    return raised / jnp.sum(raised, axis=0, keepdims=True)
+
+
 def forward_kernel(
-    heads, qkv_ref, out_weight_ref, embed_sum_ref, rating_ref, back_ref, weights_ref, packed_ref
+    heads, moved_ref, out_weight_ref, embed_sum_ref, back_ref, qkv_ref, packed_ref, wide_ref
 ):
     del back_ref
-    slots = qkv_ref.shape[0]
-    factor = 1.0 / math.sqrt(HEAD)
+    slots, frames = qkv_ref.shape[0], qkv_ref.shape[1]
+    n_t = frames // 2
+    per = 3 * heads
+    chunks = slots * per + 1
+    wide_ref[...] = moved_ref[...].astype(F32)
     sums = [0.0] * heads
     for slot in range(slots):
+        for chunk in range(per):
+            for frame in range(2):
+                rows = chunk_rows(n_t, chunks, slot * per + chunk, frame)
+                qkv_ref[
+                    slot, frame * n_t : (frame + 1) * n_t, chunk * LANES : (chunk + 1) * LANES
+                ] = wide_ref[rows, :].astype(BF)
         for head, query, key, value in split_heads(qkv_ref[slot], heads):
-            scores = dot(key, query, NT) * factor
-            top = jnp.max(scores, axis=0, keepdims=True)
-            raised = jnp.exp(scores - top)
-            weights = raised / jnp.sum(raised, axis=0, keepdims=True)
-            weights_ref[slot * heads + head] = weights
+            weights = attention_weights(key, query)
             mixture = dot(weights.astype(BF), value, TN).astype(BF).astype(F32)
             sums[head] = sums[head] + jnp.sum(mixture, axis=0, keepdims=True)
     mixture_sum = thirds(jnp.concatenate(sums, axis=1))
     mixed = jnp.sum(dot(mixture_sum, out_weight_ref[...]), axis=0, keepdims=True)
     pooled = as_lines(embed_sum_ref[...] + mixed)
-    rating = jnp.sum(rating_ref[...].astype(F32), axis=0, keepdims=True)
+    rating = jnp.sum(wide_ref[chunk_rows(n_t, chunks, chunks - 1, 0), :], axis=0, keepdims=True)
     blank = jnp.zeros((packed_ref.shape[1] - pooled.shape[0] - 1, LANES), F32)
     packed = jnp.concatenate([pooled, rating, blank], axis=0)
     for i in range(packed_ref.shape[0]):
@@ -232,10 +332,10 @@
     out_weight_ref,
     own_embed_ref,
     qkv_ref,
-    weights_ref,
     back_ref,
     expected_ref,
     direct_ref,
+    out_ref,
     sent_ref,
 ):
     lines = gain_ref.shape[0]
@@ -292,7 +392,7 @@
         total = jnp.zeros((frames, 1), F32)
         for head, query, key, value in split_heads(qkv_ref[slot], heads):
             grad_mixture = grad_heads[:, head * HEAD : (head + 1) * HEAD]
-            weights = weights_ref[slot * heads + head]
+            weights = attention_weights(key, query)
             wide_value = value.astype(F32)
             grad_weights = jnp.sum(wide_value * grad_mixture, axis=1, keepdims=True)
             centre = jnp.sum(weights * grad_weights, axis=0, keepdims=True)
@@ -330,6 +430,7 @@
         sent_ref[pl.ds(s * LINES + slots, depth, stride=N_S * LINES), :] = means
         for line in range(slots + 1, LINES):
             sent_ref[pl.ds(s * LINES + line, depth, stride=N_S * LINES), :] = blank
+    out_ref[...] = sent_ref[...].astype(BF)
 
 
 def on_device(
@@ -368,28 +469,17 @@
     params = pltpu.CompilerParams(vmem_limit_bytes=VMEM_LIMIT)
     other = lax.ppermute(embed_weight, "zl", [(0, 1), (1, 0)])
 
-    lane_blocks = channels // LANES
     patch_rows = patches.reshape(-1, channels)
-    patch_part = jnp.concatenate(
-        [patch_rows[:, i * LANES : (i + 1) * LANES] for i in range(lane_blocks)], axis=0
-    )
     stem_half = stem_weight.shape[0] // 2
-    stem_part = jnp.stack(
-        [
-            jnp.concatenate(
-                [
-                    stem_weight[h * stem_half : (h + 1) * stem_half, c : c + own_channels]
-                    for h in range(2)
-                ],
-                axis=1,
-            )
-            for c in range(0, channels, own_channels)
-        ],
-        axis=0,
-    )
-    packed = jnp.concatenate(
-        [jnp.broadcast_to(patch_part[None], (n_s,) + patch_part.shape), stem_part], axis=1
-    )
+    packed_rows = patch_rows.shape[0] * (channels // LANES) + stem_half
+    packed = pl.pallas_call(
+        pack_kernel,
+        name="pack",
+        out_shape=jax.ShapeDtypeStruct((n_s, packed_rows, LANES), BF),
+        in_specs=[whole] * 2,
+        out_specs=whole,
+        compiler_params=params,
+    )(patch_rows, stem_weight)
     packed = lax.all_to_all(packed, S_AXES, 0, 0, tiled=True)
 
     act, gelu_slope, patch_tokens = pl.pallas_call(
@@ -411,68 +501,80 @@
     pair = jnp.concatenate(
         [jnp.where(lower, embed_weight, other), jnp.where(lower, other, embed_weight)], axis=0
     )
-    full_embed = lax.all_gather(pair, "core", axis=0, tiled=True)
-    gain = attention_gain.astype(F32)
-    embedded = dot(act, full_embed, TN).reshape(frames_dev, positions, width)
-    embedded = (embedded + frame_embed.astype(F32)[:, None, :]).astype(BF)
-    embedded = embedded.reshape(tokens_dev, width)
-    wide = embedded.astype(F32)
-    scale = lax.rsqrt(jnp.mean(wide * wide, axis=-1, keepdims=True) + EPSILON)
-    normed = (wide * scale * gain).astype(BF)
-    qkv = jnp.concatenate(
-        [dot(normed, w).astype(BF) for w in (query_weight, key_weight, value_weight)], axis=1
-    )
-    embed_sum = jnp.sum(wide, axis=0, keepdims=True) * (1.0 / n_s)
-    scale_row = scale.reshape(1, tokens_dev)
-    back_unit = dot(embed_weight, embedded, NT) * scale_row
-
+    across = lax.ppermute(pair, "core", [(0, 1), (1, 0)])
+    core_index = lax.axis_index("core")
     vocab_dev = unembedding.shape[0]
     ratings = rating_ids.shape[0]
-    first_row = lax.axis_index(everyone) * vocab_dev
-    picks = (rating_ids[:, None] - first_row == jnp.arange(vocab_dev)[None, :]).astype(BF)
-    rows_part = dot(picks, unembedding).astype(BF)
-    groups = width // n_t
-    rating_part = rows_part.reshape(ratings * groups, n_t).T
-    rating_part = jnp.pad(rating_part, ((0, 0), (0, LANES - ratings * groups)))
-    rating_part = jnp.pad(rating_part[:, None, :], ((0, 0), (0, slots - 1), (0, 0)))
-
-    qkv = qkv.reshape(frames_dev, slots, n_t, 3 * inner)
-    moved = jnp.concatenate(
-        [qkv[f].transpose(1, 0, 2) for f in range(frames_dev)] + [rating_part], axis=2
-    )
+    place = jnp.stack([core_index, lax.axis_index(everyone) * vocab_dev]).astype(jnp.int32)
+
+    chunks = slots * 3 * inner // LANES + 1
+    scalars = pl.BlockSpec(memory_space=pltpu.SMEM)
+    moved, embed_sum, scale_row, back_unit = pl.pallas_call(
+        functools.partial(embed_kernel, n_t, slots),
+        name="embed",
+        out_shape=(
+            jax.ShapeDtypeStruct((n_t * chunks * 2, LANES), BF),
+            jax.ShapeDtypeStruct((1, width), F32),
+            jax.ShapeDtypeStruct((1, tokens_dev), F32),
+            jax.ShapeDtypeStruct((own_channels, tokens_dev), F32),
+        ),
+        in_specs=[scalars] * 2 + [whole] * 10,
+        out_specs=(whole,) * 4,
+        scratch_shapes=[pltpu.VMEM((n_t * chunks * 2, LANES), F32)],
+        compiler_params=params,
+    )(
+        place,
+        rating_ids,
+        act,
+        pair,
+        across,
+        frame_embed,
+        attention_gain[None, :],
+        query_weight,
+        key_weight,
+        value_weight,
+        embed_weight,
+        unembedding,
+    )
+
+    moved = moved.reshape(n_t * chunks, 2, LANES)
     moved = lax.all_to_all(moved, T_AXES, 0, 0, tiled=True)
-    qkv = jnp.concatenate(
-        [
-            moved[:, :, f * 3 * inner : (f + 1) * 3 * inner].transpose(1, 0, 2)
-            for f in range(frames_dev)
-        ],
+    moved = moved.reshape(n_t * chunks * 2, LANES)
+
+    gain = attention_gain.astype(F32)
+    sides = []
+    for part in (pair, across):
+        upper, lower_half = halves(part.astype(F32) * gain)
+        sides.append(
+            jnp.concatenate(
+                [
+                    dot(w, upper, (((0,), (1,)), ((), ())))
+                    + dot(w, lower_half, (((0,), (1,)), ((), ())))
+                    for w in (query_weight, key_weight, value_weight)
+                ],
+                axis=0,
+            )
+        )
+    first_core = core_index == 0
+    back = jnp.concatenate(
+        [jnp.where(first_core, sides[0], sides[1]), jnp.where(first_core, sides[1], sides[0])],
         axis=1,
     )
-    rating_got = moved[:, 0, frames_dev * 3 * inner :]
-
-    scaled = full_embed.astype(F32) * gain
-    back = jnp.concatenate(
-        [
-            sum(dot(w, part, (((0,), (1,)), ((), ()))) for part in halves(scaled))
-            for w in (query_weight, key_weight, value_weight)
-        ],
-        axis=0,
-    )
-
-    items = slots * heads
+
     lines = width // LANES
     first = lax.axis_size(("x",) + S_AXES)
-    weights, packed = pl.pallas_call(
+    qkv, packed = pl.pallas_call(
         functools.partial(forward_kernel, heads),
         name="attend",
         out_shape=(
-            jax.ShapeDtypeStruct((items, all_frames, all_frames), F32),
+            jax.ShapeDtypeStruct((slots, all_frames, 3 * inner), BF),
             jax.ShapeDtypeStruct((first, lines + 8, LANES), F32),
         ),
-        in_specs=[whole] * 4 + [pl.BlockSpec(memory_space=pl.ANY)],
+        in_specs=[whole] * 3 + [pl.BlockSpec(memory_space=pl.ANY)],
         out_specs=(whole, whole),
+        scratch_shapes=[pltpu.VMEM((n_t * chunks * 2, LANES), F32)],
         compiler_params=params,
-    )(qkv, output_weight, embed_sum, rating_got, back)
+    )(moved, output_weight, embed_sum, back)
 
     packed = lax.all_to_all(packed, ("x",) + S_AXES, 0, 0, tiled=True)
     size_x, size_y, size_z = (lax.axis_size(axis) for axis in ("x", "y", "zh"))
@@ -496,10 +598,11 @@
         out_shape=(
             jax.ShapeDtypeStruct((8, LANES), F32),
             jax.ShapeDtypeStruct((own_channels, LANES), F32),
-            jax.ShapeDtypeStruct((n_t * n_s * LINES, LANES), F32),
+            jax.ShapeDtypeStruct((n_t * n_s * LINES, LANES), BF),
         ),
-        in_specs=[pl.BlockSpec(memory_space=pltpu.SMEM)] + [whole] * 7,
+        in_specs=[scalars] + [whole] * 6,
         out_specs=(whole,) * 3,
+        scratch_shapes=[pltpu.VMEM((n_t * n_s * LINES, LANES), F32)],
         compiler_params=params,
     )(
         target_score,
@@ -508,11 +611,10 @@
         output_weight,
         embed_weight,
         qkv,
-        weights,
         back,
     )
 
-    sent = sent.astype(BF).reshape(n_t * n_s, LINES, LANES)
+    sent = sent.reshape(n_t * n_s, LINES, LANES)
     sent = lax.all_to_all(sent, everyone, 0, 0, tiled=True)
     got = jnp.sum(sent.reshape(n_t, n_s, LINES, LANES).astype(F32), axis=1)
 
@@ -522,16 +624,17 @@
     sums = pl.pallas_call(
         functools.partial(stem_back_kernel, cols, count_rows, slots, frames_dev),
         name="stem_back",
-        out_shape=jax.ShapeDtypeStruct((n_t * n_s * out_lines, LANES), F32),
+        out_shape=jax.ShapeDtypeStruct((n_t * n_s * out_lines, LANES), BF),
         in_specs=[whole] * 6,
         out_specs=whole,
         scratch_shapes=[
             pltpu.VMEM((9 * channels, own_channels), F32),
             pltpu.VMEM((count, LANES), F32),
+            pltpu.VMEM((n_t * n_s * out_lines, LANES), F32),
         ],
         compiler_params=params,
     )(got.reshape(n_t * LINES, LANES), back_unit, scale_row, direct, gelu_slope, patch_tokens)
-    sums = sums.astype(BF).reshape(n_t * n_s, out_lines, LANES)
+    sums = sums.reshape(n_t * n_s, out_lines, LANES)
     sums = lax.all_to_all(sums, everyone, 0, 0, tiled=True)
     sums = jnp.sum(sums.reshape(n_t, n_s, out_lines, LANES).astype(F32), axis=0)[:, :window]
     flat = sums.reshape(n_s, -1, own_channels).transpose(1, 0, 2).reshape(-1)

time: 224 us -> 200 us (0.89)
  blocking collectives: 34.4 us -> 69.3 us
  waiting for transfers between devices: 76.4 us -> 48.8 us
  between operations: 15.2 us -> 1.63 us
  starting transfers between devices: 55.8 us -> 42.9 us
  Pallas kernels: 7.59 us -> 15.8 us
  other arithmetic: 7.05 us -> 1.72 us
  local copies, waits for them, and re-layouts: 14.8 us -> 10.8 us
  matrix products: 11.8 us -> 8.15 us
    all_to_all x0 -> x1, blocking collectives: none -> 33.8 us  [on_device(): sent = lax.all_to_all(sent, everyone, 0, 0, tiled=True)]
    all_to_all x1 -> x0, waiting for transfers between devices: 19.6 us -> none  [on_device(): sent = lax.all_to_all(sent, everyone, 0, 0, tiled=True)]
    all_to_all x1 -> x0, starting transfers between devices: 11.5 us -> none  [on_device(): sent = lax.all_to_all(sent, everyone, 0, 0, tiled=True)]
    all_to_all x1, waiting for transfers between devices: 7.1 us -> 0.01 us  [on_device(): packed = lax.all_to_all(packed, S_AXES, 0, 0, tiled=True)]
    pallas_call x0 -> x2, Pallas kernels: none -> 6.18 us  [the longest x1 5.22 us: on_device(): pl.pallas_call(functools.partial(embed_kernel, n_t, slots), name='embed',...]
    slice x5 -> x0, local copies, waits for them, and re-layouts: 4.74 us -> none  [the longest x1 1.74 us: on_device(): moved[:, :, f * 3 * inner:(f + 1) * 3 * inner].transpose(1, 0, 2)]
    dot_general x12, matrix products: 11.8 us -> 8.15 us  [dot(): return lax.dot_general(lhs, rhs, dims, preferred_element_type=F32)]
    concatenate x6 -> x1, other arithmetic: 3.52 us -> 0.05 us  [on_device(): jnp.concatenate([jnp.where(first_core, sides[0], sides[1]), jnp.where(fir...]
  transfers between devices with their start and end apart: 7 -> 6, of which waited for: 6 -> 3; matrix products, arithmetic and copies ran while one was open for 5% -> 5% of each run, Pallas kernels for 1% -> 1%
where the time goes in v3:
time: 200 us; the launch traced here: 199 us
  blocking collectives  69.3 us (35%)
  waiting for transfers between devices  48.8 us (24%)
  starting transfers between devices  42.9 us (21%)
  Pallas kernels  15.8 us (8%)
  local copies, waits for them, and re-layouts  10.8 us (5%)
  matrix products  8.15 us (4%)
    all_to_all x1, blocking collectives, on_device(): sent = lax.all_to_all(sent, everyone, 0, 0, tiled=True)  33.8 us
    all_to_all x1, waiting for transfers between devices, on_device(): sums = lax.all_to_all(sums, everyone, 0, 0, tiled=True)  21.5 us
    all_to_all x1, waiting for transfers between devices, on_device(): moved = lax.all_to_all(moved, T_AXES, 0, 0, tiled=True)  20.9 us
    all_to_all x1, starting transfers between devices, on_device(): moved = lax.all_to_all(moved, T_AXES, 0, 0, tiled=True)  16.3 us
    all_to_all x1, blocking collectives, on_device(): packed = lax.all_to_all(packed, ('x',) + S_AXES, 0, 0, tiled=True)  13.9 us
    all_to_all x1, blocking collectives, on_device(): packed = lax.all_to_all(packed, axis, 0, 0, tiled=True)  11 us
    all_gather x1, blocking collectives, on_device(): act = lax.all_gather(act, ('core', 'zl'), axis=0, tiled=True)  10.5 us
    unnamed x54, local copies, waits for them, and re-layouts  9.45 us
  transfers between devices with their start and end apart: 6, of which 3 were waited for; matrix products, arithmetic and copies ran while one was open for 5% of the time, Pallas kernels for 1%

profile of v3, /device:TPU:1, one launch (start us, length us, event | category | flops | bytes accessed | tf_op | source)
XLA Modules:
  0.0 199.0 jit_solution(11323520222196096065)
XLA Ops:
  0.6 4.8 %collective-permute-start = (bf16[64,2048]{1,0:T(8,128)(2,1)}, bf16[64,2048]{1,0:T(8,128)(2,1)S(1)}, u32[]{:S(2)}, u32[]{:S(2)}) collective-permute-start(bf16[64,2048]{1,0:T(8,128)(2,1)} %own_embed_ref.3), channel_id=1, source_target_pairs={{0,2},{2,0},{1,3},{3,1},{4,6},{6,4},{5,7},{7,5},{8,10},{10,8},{9,1... | collective-permute-start | bytes 786440 | tf_op jit(solution)/shard_map/ppermute | solution.py:470
  5.5 1.0 copy-done.11
  6.4 0.8 copy-done.19
  7.3 1.0 pack.1
  8.2 7.5 %all-to-all-start = ((bf16[4,544,128]{2,1,0:T(8,128)(2,1)}), bf16[4,544,128]{2,1,0:T(8,128)(2,1)S(1)}, u32[]{:S(2)}, u32[]{:S(2)}) async-start(bf16[4,544,128]{2,1,0:T(8,128)(2,1)} %pack.1), calls=%async_computation | async-start | bytes 1114112 | tf_op jit(solution)/shard_map/all_to_all | solution.py:483
  15.7 0.7 copy-done.26
  16.5 0.1 pad_add_fusion.place_ref
  16.6 0.8 pad_maximum_fusion.1.pair_ref
  17.4 1.9 collective-permute-start.1
  19.4 0.5 fusion.8
  19.9 0.0 copy-start.1
  19.9 1.2 fusion.3
  21.1 0.0 copy-done.1
  21.2 0.5 fusion.10
  21.7 0.0 copy-start.2
  21.7 1.2 fusion.4
  22.9 0.0 copy-done.2
  22.9 0.5 fusion.12
  23.4 1.2 fusion.5
  24.6 1.2 stem.1
  25.9 0.7 copy-done.13
  26.5 0.7 copy-done.15
  27.2 10.5 %all_gather.3.act_ref = bf16[256,512]{1,0:T(8,128)(2,1)S(1)} all-gather(bf16[64,512]{1,0:T(8,128)(2,1)S(1)} %get-tuple-element.14), channel_id=1, replica_groups=mesh['zh'=4,'y'=8,'x'=4,'zl'=2,'core'=2] {'core','zl'}, dimensions={0}, use_global_device_ids=true | all-gather | bytes 327680 | tf_op jit(solution)/shard_map/all_gather | solution.py:498
  37.8 0.0 copy-start.3
  37.8 1.2 copy-done.3
  39.0 5.2 %embed.1 = (bf16[3328,128]{1,0:T(8,128)(2,1)S(1)}, f32[1,2048]{1,0:T(1,128)S(1)}, f32[1,512]{1,0:T(1,128)S(1)}, f32[64,512]{1,0:T(8,128)S(1)}) custom-call(s32[2]{0:T(128)S(1)} %pad_add_fusion.place_ref, s32[5]{0:T(128)S(1)} %copy-done.22, bf16[256,512]{1,0:T(8,128)(2,1)S(1)} %all_gather.3.act_ref, bf16[128,2048]{1,0:T(8,128)(2,1)} %pad_maximum_fusion.1.pair_ref, ...), custom_call_target="tpu_custom_call" | custom-call | tf_op jit(solution)/shard_map/embed/pallas_call | solution.py:512
  44.2 0.6 copy-done.17
  44.9 0.9 copy-done.8
  45.8 16.3 %all-to-all-start.1 = ((bf16[1664,2,128]{2,1,0:T(2,128)(2,1)}), bf16[1664,2,128]{2,1,0:T(2,128)(2,1)S(1)}, u32[]{:S(2)}, u32[]{:S(2)}) async-start(bf16[1664,2,128]{2,1,0:T(2,128)(2,1)} %bitcast.43), calls=%async_computation.1 | async-start | bytes 1703936 | tf_op jit(solution)/shard_map/all_to_all | solution.py:541
  62.1 0.5 fusion.25
  62.6 0.5 fusion.26
  63.1 0.7 copy-done.4
  63.8 0.5 fusion.27
  64.4 0.5 fusion
  64.9 0.5 fusion.1
  65.4 0.5 fusion.2
  65.9 0.4 copy-done.23
  66.3 0.1 copy-done.24
  66.3 0.1 copy-done.25
  66.4 0.1 fusion.24
  66.5 0.1 pad_maximum_fusion.back_ref
  66.5 20.9 %all-to-all-done.1 = bf16[1664,2,128]{2,1,0:T(2,128)(2,1)S(1)} async-done(((bf16[1664,2,128]{2,1,0:T(2,128)(2,1)}), bf16[1664,2,128]{2,1,0:T(2,128)(2,1)S(1)}, u32[]{:S(2)}, u32[]{:S(2)}) %all-to-all-start.1) | async-done | bytes 852000 | tf_op jit(solution)/shard_map/all_to_all | solution.py:541
  87.5 1.5 attend.1
  89.0 0.9 copy-done.9
  89.8 13.9 %all_to_all.35.in_ref = f32[16,24,128]{2,1,0:T(8,128)S(1)} all-to-all(f32[16,24,128]{2,1,0:T(8,128)S(1)} %get-tuple-element.17), channel_id=1, replica_groups=mesh['zh'=4,'y'=8,'x'=4,'zl'=2,'core'=2] {'x','zl','core'}, dimensions={0} | all-to-all | bytes 393216 | tf_op jit(solution)/shard_map/all_to_all | solution.py:579
  103.7 11.0 %all_to_all.36.in_ref = f32[8,24,128]{2,1,0:T(8,128)S(1)} all-to-all(f32[8,24,128]{2,1,0:T(8,128)S(1)} %combine_y.1), channel_id=1, replica_groups=mesh['zh'=4,'y'=8,'x'=4,'zl'=2,'core'=2] {'y'}, dimensions={0} | all-to-all | bytes 196608 | tf_op jit(solution)/shard_map/all_to_all | solution.py:593
  114.8 0.6 combine_zh.1
  115.4 3.3 %all-to-all-start.4 = ((f32[4,48,128]{2,1,0:T(8,128)}), f32[4,48,128]{2,1,0:T(8,128)S(1)}, u32[]{:S(2)}, u32[]{:S(2)}) async-start(f32[4,48,128]{2,1,0:T(8,128)} %combine_zh.1), calls=%async_computation.4 | async-start | bytes 196608 | tf_op jit(solution)/shard_map/all_to_all | solution.py:593
  118.7 0.0 copy-start.21
  119.4 6.3 %all-to-all-done.4.packed_ref = f32[4,48,128]{2,1,0:T(8,128)S(1)} async-done(((f32[4,48,128]{2,1,0:T(8,128)}), f32[4,48,128]{2,1,0:T(8,128)S(1)}, u32[]{:S(2)}, u32[]{:S(2)}) %all-to-all-start.4) | async-done | bytes 98336 | tf_op jit(solution)/shard_map/all_to_all | solution.py:593
  125.8 4.0 %attend_back.1 = (f32[8,128]{1,0:T(8,128)S(1)}, f32[64,128]{1,0:T(8,128)S(1)}, bf16[2048,128]{1,0:T(8,128)(2,1)S(1)}) custom-call(s32[1]{0:T(128)S(6)} %copy.52.target_ref, f32[4,48,128]{2,1,0:T(8,128)S(1)} %all-to-all-done.4.packed_ref, bf16[16,128]{1,0:T(8,128)(2,1)S(1)} %bitcast.46, bf16[256,2048]{1,0:T(8,128)(2,1)S(1)} %copy-done.5, ...), custom_call_target="tpu_custom_call" | custom-call | tf_op jit(solution)/shard_map/attend_back/pallas_call | solution.py:595
  129.8 33.8 %all_to_all.37 = bf16[512,4,128]{2,1,0:T(4,128)(2,1)S(1)} all-to-all(bf16[512,4,128]{2,1,0:T(4,128)(2,1)S(1)} %bitcast.44), channel_id=1, replica_groups=mesh['zh'=4,'y'=8,'x'=4,'zl'=2,'core'=2] {'zh','y','x','zl','core'}, dimensions={0} | all-to-all | bytes 1048576 | tf_op jit(solution)/shard_map/all_to_all | solution.py:618
  163.6 0.4 convert_reduce_fusion.1
  164.0 0.6 copy-done.14
  164.5 0.0 copy-done.16
  164.6 0.1 copy-done.18
  164.6 2.3 %stem_back.1 = bf16[2048,128]{1,0:T(8,128)(2,1)} custom-call(f32[512,128]{1,0:T(8,128)S(1)} %bitcast.42, f32[64,512]{1,0:T(8,128)S(1)} %copy-done.18, f32[1,512]{1,0:T(1,128)S(1)} %get-tuple-element.22.scale_ref, f32[64,128]{1,0:T(8,128)S(1)} %get-tuple-element.23.direct_ref, f32[64,512]{1,0:T(8,128)S(1)} %copy-done.16, bf16[512,256]{1,0:T(8,128)(2,1)S(1)} %copy-done.14), custom_call_target="tpu_custom_call" | custom-call | tf_op jit(solution)/shard_map/stem_back/pallas_call | solution.py:624
  166.9 9.1 %all-to-all-start.6 = ((bf16[512,4,128]{2,1,0:T(4,128)(2,1)}), bf16[512,4,128]{2,1,0:T(4,128)(2,1)S(1)}, u32[]{:S(2)}, u32[]{:S(2)}) async-start(bf16[512,4,128]{2,1,0:T(4,128)(2,1)} %bitcast.16), calls=%async_computation.6 | async-start | bytes 1048576 | tf_op jit(solution)/shard_map/all_to_all | solution.py:638
  175.9 0.5 slice.6
  176.5 21.5 %all-to-all-done.6 = bf16[512,4,128]{2,1,0:T(4,128)(2,1)S(1)} async-done(((bf16[512,4,128]{2,1,0:T(4,128)(2,1)}), bf16[512,4,128]{2,1,0:T(4,128)(2,1)S(1)}, u32[]{:S(2)}, u32[]{:S(2)}) %all-to-all-start.6) | async-done | bytes 524320 | tf_op jit(solution)/shard_map/all_to_all | solution.py:638
  197.9 0.3 convert_reduce_fusion
  198.2 0.1 reshape.45
  198.3 0.1 reshape.46
  198.4 0.7 dynamic_slice.3
  (40 shorter events, 0.2 us)
Async XLA Ops:
  0.6 15.9 %collective-permute-start = (bf16[64,2048]{1,0:T(8,128)(2,1)}, bf16[64,2048]{1,0:T(8,128)(2,1)S(1)}, u32[]{:S(2)}, u32[]{:S(2)}) collective-permute-start(bf16[64,2048]{1,0:T(8,128)(2,1)} %own_embed_ref.3), channel_id=1, source_target_pairs={{0,2},{2,0},{1,3},{3,1},{4,6},{6,4},{5,7},{7,5},{8,10},{10,8},{9,1... | collective-permute-start | bytes 786440 | tf_op jit(solution)/shard_map/ppermute | solution.py:470
  5.5 1.0 copy-start.11
  6.4 0.8 copy-start.19
  8.2 8.3 %copy-start.6 = (bf16[64,2048]{1,0:T(8,128)(2,1)S(1)}, bf16[64,2048]{1,0:T(8,128)(2,1)}, u32[]{:S(2)}) copy-start(bf16[64,2048]{1,0:T(8,128)(2,1)} %own_embed_ref.3) | copy-start | bytes 786436
  8.2 16.4 %all-to-all-start = ((bf16[4,544,128]{2,1,0:T(8,128)(2,1)}), bf16[4,544,128]{2,1,0:T(8,128)(2,1)S(1)}, u32[]{:S(2)}, u32[]{:S(2)}) async-start(bf16[4,544,128]{2,1,0:T(8,128)(2,1)} %pack.1), calls=%async_computation | async-start | bytes 1114112 | tf_op jit(solution)/shard_map/all_to_all | solution.py:483
  15.7 0.7 copy-start.26
  16.5 2.9 %copy-start = (bf16[2048,256]{1,0:T(8,128)(2,1)S(1)}, bf16[2048,256]{1,0:T(8,128)(2,1)}, u32[]{:S(2)}) copy-start(bf16[2048,256]{1,0:T(8,128)(2,1)} %value_ref.1) | copy-start | bytes 3145732
  17.4 20.3 %collective-permute-start.1 = (bf16[128,2048]{1,0:T(8,128)(2,1)}, bf16[128,2048]{1,0:T(8,128)(2,1)S(1)}, u32[]{:S(2)}, u32[]{:S(2)}) collective-permute-start(bf16[128,2048]{1,0:T(8,128)(2,1)} %pad_maximum_fusion.1.pair_ref), channel_id=1, source_target_pairs={{0,1},{1,0},{2,3},{3,2},{4,5},{5,4},{6,7},{7,6},{8,9},{9,8},{10,11... | collective-permute-start | bytes 1572872 | tf_op jit(solution)/shard_map/ppermute | solution.py:504
  19.9 1.2 copy-start.1
  21.7 1.2 copy-start.2
  25.9 0.7 copy-start.13
  26.5 0.7 copy-start.15
  27.2 10.6 %copy-start.12 = (bf16[64,2048]{1,0:T(8,128)(2,1)S(1)}, bf16[64,2048]{1,0:T(8,128)(2,1)}, u32[]{:S(2)}) copy-start(bf16[64,2048]{1,0:T(8,128)(2,1)} %vocab_ref.1) | copy-start | bytes 786436
  27.2 10.6 %copy-start.20 = (bf16[2,2048]{1,0:T(2,128)(2,1)S(1)}, bf16[2,2048]{1,0:T(2,128)(2,1)}, u32[]{:S(2)}) copy-start(bf16[2,2048]{1,0:T(2,128)(2,1)} %frame_ref.1) | copy-start | bytes 24580
  27.2 10.6 %copy-start.22 = (s32[5]{0:T(128)S(1)}, s32[5]{0:T(128)}, u32[]{:S(2)}) copy-start(s32[5]{0:T(128)} %ids_ref.1) | copy-start | bytes 64
  37.8 1.2 copy-start.3
  44.2 0.6 copy-start.17
  44.9 0.9 copy-start.8
  45.8 41.7 %all-to-all-start.1 = ((bf16[1664,2,128]{2,1,0:T(2,128)(2,1)}), bf16[1664,2,128]{2,1,0:T(2,128)(2,1)S(1)}, u32[]{:S(2)}, u32[]{:S(2)}) async-start(bf16[1664,2,128]{2,1,0:T(2,128)(2,1)} %bitcast.43), calls=%async_computation.1 | async-start | bytes 1703936 | tf_op jit(solution)/shard_map/all_to_all | solution.py:541
  62.6 1.2 copy-start.4
  65.4 0.9 copy-start.23
  65.4 1.0 copy-start.24
  65.4 1.0 copy-start.25
  66.5 21.0 %copy-start.5 = (bf16[256,2048]{1,0:T(8,128)(2,1)S(1)}, bf16[256,2048]{1,0:T(8,128)(2,1)}, u32[]{:S(2)}) copy-start(bf16[256,2048]{1,0:T(8,128)(2,1)} %out_weight_ref.3) | copy-start | bytes 3145732
  88.9 0.9 copy-start.9
  89.8 35.9 %copy-start.10 = (bf16[2,256,768]{2,1,0:T(8,128)(2,1)S(1)}, bf16[2,256,768]{2,1,0:T(8,128)(2,1)}, u32[]{:S(2)}) copy-start(bf16[2,256,768]{2,1,0:T(8,128)(2,1)} %copy-done.9) | copy-start | bytes 2359300
  103.7 22.0 %copy-start.7 = (bf16[64,2048]{1,0:T(8,128)(2,1)S(1)}, bf16[64,2048]{1,0:T(8,128)(2,1)}, u32[]{:S(2)}) copy-start(bf16[64,2048]{1,0:T(8,128)(2,1)} %own_embed_ref.3) | copy-start | bytes 786436
  115.4 10.3 %all-to-all-start.4 = ((f32[4,48,128]{2,1,0:T(8,128)}), f32[4,48,128]{2,1,0:T(8,128)S(1)}, u32[]{:S(2)}, u32[]{:S(2)}) async-start(f32[4,48,128]{2,1,0:T(8,128)} %combine_zh.1), calls=%async_computation.4 | async-start | bytes 196608 | tf_op jit(solution)/shard_map/all_to_all | solution.py:593
  118.7 7.0 %copy-start.21 = (bf16[2048]{0:T(1024)(128)(2,1)S(1)}, bf16[2048]{0:T(1024)(128)(2,1)}, u32[]{:S(2)}) copy-start(bf16[2048]{0:T(1024)(128)(2,1)} %param.18) | copy-start | bytes 12292
  163.6 1.0 copy-start.14
  163.6 1.0 copy-start.16
  163.6 1.0 copy-start.18
  166.9 31.0 %all-to-all-start.6 = ((bf16[512,4,128]{2,1,0:T(4,128)(2,1)}), bf16[512,4,128]{2,1,0:T(4,128)(2,1)S(1)}, u32[]{:S(2)}, u32[]{:S(2)}) async-start(bf16[512,4,128]{2,1,0:T(4,128)(2,1)} %bitcast.16), calls=%async_computation.6 | async-start | bytes 1048576 | tf_op jit(solution)/shard_map/all_to_all | solution.py:638

commit v4 on v3

--- a/solution.py
+++ b/solution.py
@@ -109,11 +109,13 @@
     grad_ref,
     lines_ref,
     wide_ref,
+    got_wide_ref,
 ):
     lanes, channels = tokens_ref.shape
     own = slope_ref.shape[0]
     depth = got_ref.shape[0] // LINES
-    turned = [got_ref[pl.ds(i, depth, stride=LINES), :].T for i in range(slots + 1)]
+    got_wide_ref[...] = got_ref[...].astype(F32)
+    turned = [got_wide_ref[pl.ds(i, depth, stride=LINES), :].T for i in range(slots + 1)]
     unit = jnp.concatenate(
         [turned[s][f * own : (f + 1) * own] for f in range(frames) for s in range(slots)], axis=1
     )
@@ -139,21 +141,14 @@
     lines_ref[...] = jnp.concatenate(
         [grad_ref[pl.ds(i, count, stride=2), :] for i in range(2)], axis=1
     )
-    step, window = line_window(count, depth)
-    out_lines = out_ref.shape[0] // (N_S * depth)
+    per, out_lines = count // depth, out_ref.shape[0] // depth
     blank = jnp.zeros((depth, LANES), F32)
-    for s in range(N_S):
-        for line in range(out_lines):
-            value = blank
-            if line < window:
-                value = lines_ref[pl.ds(step * s + line, depth, stride=count // depth), :]
-            wide_ref[pl.ds(s * out_lines + line, depth, stride=N_S * out_lines), :] = value
+    for line in range(out_lines):
+        value = blank
+        if line < per:
+            value = lines_ref[pl.ds(line, depth, stride=per), :]
+        wide_ref[pl.ds(line, depth, stride=out_lines), :] = value
     out_ref[...] = wide_ref[...].astype(BF)
-
-
-def line_window(count, depth):
-    per = count // depth
-    return per // N_S, -(-per // N_S)
 
 
 def split_heads(block, heads):
@@ -224,14 +219,17 @@
     per = 3 * inner // LANES
     chunks = slots * per + 1
     gain = gain_ref[...].astype(F32)
-    here = pl.multiple_of(core * near, near)
-    there = pl.multiple_of((1 - core) * near, near)
+    own = own_embed_ref.shape[0]
+
+    def rows_of(which, at):
+        starts = [pl.multiple_of((zl * 2 + which) * own, own) for zl in range(near // own)]
+        return jnp.concatenate([act_ref[pl.ds(i, own), at : at + tokens] for i in starts], axis=0)
+
     embed_sum = jnp.zeros((1, width), F32)
     for frame in range(frames):
         at = frame * tokens
-        mine = act_ref[pl.ds(here, near), at : at + tokens]
-        other = act_ref[pl.ds(there, near), at : at + tokens]
-        made = dot(mine, pair_ref[...], TN) + dot(other, across_ref[...], TN)
+        made = dot(rows_of(core, at), pair_ref[...], TN)
+        made = made + dot(rows_of(1 - core, at), across_ref[...], TN)
         embedded = (made + frame_ref[frame : frame + 1, :].astype(F32)).astype(BF)
         wide = embedded.astype(F32)
         embed_sum = embed_sum + jnp.sum(wide, axis=0, keepdims=True)
@@ -335,7 +333,6 @@
     back_ref,
     expected_ref,
     direct_ref,
-    out_ref,
     sent_ref,
 ):
     lines = gain_ref.shape[0]
@@ -419,18 +416,33 @@
                 sent[f * depth : (f + 1) * depth, block * own : (block + 1) * own]
                 for f in range(2)
             ]
-            sent_ref[pl.ds(s * LINES + slot, depth, stride=N_S * LINES), :] = jnp.concatenate(
+            sent_ref[s, slot * depth : (slot + 1) * depth, :] = jnp.concatenate(
                 both, axis=1
-            )
+            ).astype(BF)
         for f in range(2):
             column = total[f * depth : (f + 1) * depth] / width
             means = means + jnp.where(lane == slot * 2 + f, 1.0, 0.0) * column
-    blank = jnp.zeros((depth, LANES), F32)
+    turned = means.T[:16]
+    if depth < LANES:
+        turned = jnp.concatenate([turned, jnp.zeros((16, LANES - depth), F32)], axis=1)
+    turned = turned.astype(BF)
     for s in range(N_S):
-        sent_ref[pl.ds(s * LINES + slots, depth, stride=N_S * LINES), :] = means
-        for line in range(slots + 1, LINES):
-            sent_ref[pl.ds(s * LINES + line, depth, stride=N_S * LINES), :] = blank
-    out_ref[...] = sent_ref[...].astype(BF)
+        sent_ref[s, slots * depth :, :] = turned
+
+
+def gather_kernel(slots, in_ref, out_ref, wide_ref):
+    depth = out_ref.shape[0] // LINES
+    total = in_ref[0].astype(F32)
+    for i in range(1, in_ref.shape[0]):
+        total = total + in_ref[i].astype(F32)
+    for slot in range(slots):
+        wide_ref[pl.ds(slot, depth, stride=LINES), :] = total[slot * depth : (slot + 1) * depth]
+    means = total[slots * depth :]
+    blank = jnp.zeros((LANES - means.shape[0], LANES), F32)
+    means = jnp.concatenate([means, blank], axis=0)
+    wide_ref[pl.ds(slots, depth, stride=LINES), :] = means.T[:depth]
+    wide_ref[pl.ds(slots + 1, depth, stride=LINES), :] = jnp.zeros((depth, LANES), F32)
+    out_ref[...] = wide_ref[...].astype(BF)
 
 
 def on_device(
@@ -495,7 +507,7 @@
         scratch_shapes=[pltpu.VMEM((9 * channels, own_channels), BF)],
         compiler_params=params,
     )(packed)
-    act = lax.all_gather(act, ("core", "zl"), axis=0, tiled=True)
+    act = lax.all_gather(act, S_AXES, axis=0, tiled=True)
 
     lower = lax.axis_index("zl") == 0
     pair = jnp.concatenate(
@@ -598,11 +610,10 @@
         out_shape=(
             jax.ShapeDtypeStruct((8, LANES), F32),
             jax.ShapeDtypeStruct((own_channels, LANES), F32),
-            jax.ShapeDtypeStruct((n_t * n_s * LINES, LANES), BF),
+            jax.ShapeDtypeStruct((n_s, slots * n_t + 16, LANES), BF),
         ),
         in_specs=[scalars] + [whole] * 6,
         out_specs=(whole,) * 3,
-        scratch_shapes=[pltpu.VMEM((n_t * n_s * LINES, LANES), F32)],
         compiler_params=params,
     )(
         target_score,
@@ -614,33 +625,44 @@
         back,
     )
 
-    sent = sent.reshape(n_t * n_s, LINES, LANES)
-    sent = lax.all_to_all(sent, everyone, 0, 0, tiled=True)
-    got = jnp.sum(sent.reshape(n_t, n_s, LINES, LANES).astype(F32), axis=1)
+    sent = lax.all_to_all(sent, S_AXES, 0, 0, tiled=True)
+    sent = pl.pallas_call(
+        functools.partial(gather_kernel, slots),
+        name="gather",
+        out_shape=jax.ShapeDtypeStruct((n_t * LINES, LANES), BF),
+        in_specs=[whole],
+        out_specs=whole,
+        scratch_shapes=[pltpu.VMEM((n_t * LINES, LANES), F32)],
+        compiler_params=params,
+    )(sent)
+    sent = lax.all_to_all(
+        sent.reshape(n_t * LINES // 2, 2, LANES), T_AXES, 0, 0, tiled=True
+    ).reshape(n_t * LINES, LANES)
 
     count = 9 * channels * own_channels // LANES
-    step, window = line_window(count, n_t)
-    out_lines = -(-window // 4) * 4
+    per = count // n_t
+    out_lines = per + per % 2
     sums = pl.pallas_call(
         functools.partial(stem_back_kernel, cols, count_rows, slots, frames_dev),
         name="stem_back",
-        out_shape=jax.ShapeDtypeStruct((n_t * n_s * out_lines, LANES), BF),
+        out_shape=jax.ShapeDtypeStruct((n_t * out_lines, LANES), BF),
         in_specs=[whole] * 6,
         out_specs=whole,
         scratch_shapes=[
             pltpu.VMEM((9 * channels, own_channels), F32),
             pltpu.VMEM((count, LANES), F32),
-            pltpu.VMEM((n_t * n_s * out_lines, LANES), F32),
+            pltpu.VMEM((n_t * out_lines, LANES), F32),
+            pltpu.VMEM((n_t * LINES, LANES), F32),
         ],
         compiler_params=params,
-    )(got.reshape(n_t * LINES, LANES), back_unit, scale_row, direct, gelu_slope, patch_tokens)
-    sums = sums.reshape(n_t * n_s, out_lines, LANES)
-    sums = lax.all_to_all(sums, everyone, 0, 0, tiled=True)
-    sums = jnp.sum(sums.reshape(n_t, n_s, out_lines, LANES).astype(F32), axis=0)[:, :window]
-    flat = sums.reshape(n_s, -1, own_channels).transpose(1, 0, 2).reshape(-1)
-    length = 9 * channels * channels // (n_t * n_s)
-    start = space_index * (length - step * LANES * n_s)
-    stem_gradient = lax.dynamic_slice_in_dim(flat, start, length, 0)
+    )(sent, back_unit, scale_row, direct, gelu_slope, patch_tokens)
+    sums = sums.reshape(n_t * out_lines // 2, 2, LANES)
+    sums = lax.all_to_all(sums, T_AXES, 0, 0, tiled=True)
+    sums = jnp.sum(sums.reshape(n_t, out_lines // 2, 2, LANES).astype(F32), axis=0)
+    sums = lax.all_gather(sums, S_AXES, axis=0, tiled=False).reshape(n_s, out_lines, LANES)
+    flat = sums[:, :per].reshape(n_s, -1, own_channels).transpose(1, 0, 2).reshape(-1)
+    length = flat.shape[0] // n_s
+    stem_gradient = lax.dynamic_slice_in_dim(flat, space_index * length, length, 0)
     return (expected[0, :1], stem_gradient)
 
 

time: 200 us -> 189 us (0.945)
  waiting for transfers between devices: 48.8 us -> 40.9 us
  starting transfers between devices: 42.9 us -> 40.2 us
    all_to_all x1, waiting for transfers between devices: 21.5 us -> 13.2 us  [on_device(): sums = lax.all_to_all(sums, T_AXES, 0, 0, tiled=True)]
    all_gather x1 -> x2, blocking collectives: 10.5 us -> 15.3 us  [the longest x1 8.97 us: on_device(): lax.all_gather(sums, S_AXES, axis=0, tiled=False)]
    all_to_all x1 -> x2, blocking collectives: 33.8 us -> 30.1 us  [the longest x1 18.7 us: on_device(): lax.all_to_all(sent.reshape(n_t * LINES // 2, 2, LANES), T_AXES, 0, 0, ti...]
    all_to_all x1, starting transfers between devices: 9.05 us -> 6.37 us  [on_device(): sums = lax.all_to_all(sums, T_AXES, 0, 0, tiled=True)]
where the time goes in v4:
time: 189 us; the launch traced here: 188 us
  blocking collectives  69.7 us (37%)
  waiting for transfers between devices  40.9 us (22%)
  starting transfers between devices  40.2 us (21%)
  Pallas kernels  15.3 us (8%)
  local copies, waits for them, and re-layouts  10.2 us (5%)
  matrix products  8.18 us (4%)
    all_to_all x1, waiting for transfers between devices, on_device(): moved = lax.all_to_all(moved, T_AXES, 0, 0, tiled=True)  21.3 us
    all_to_all x1, blocking collectives, on_device(): lax.all_to_all(sent.reshape(n_t * LINES // 2, 2, LANES), T_AXES, 0, 0, ti...  18.7 us
    all_to_all x1, starting transfers between devices, on_device(): moved = lax.all_to_all(moved, T_AXES, 0, 0, tiled=True)  16.3 us
    all_to_all x1, blocking collectives, on_device(): packed = lax.all_to_all(packed, ('x',) + S_AXES, 0, 0, tiled=True)  13.4 us
    all_to_all x1, waiting for transfers between devices, on_device(): sums = lax.all_to_all(sums, T_AXES, 0, 0, tiled=True)  13.2 us
    all_to_all x1, blocking collectives, on_device(): sent = lax.all_to_all(sent, S_AXES, 0, 0, tiled=True)  11.3 us
    all_to_all x1, blocking collectives, on_device(): packed = lax.all_to_all(packed, axis, 0, 0, tiled=True)  11 us
    all_gather x1, blocking collectives, on_device(): lax.all_gather(sums, S_AXES, axis=0, tiled=False)  8.97 us
  transfers between devices with their start and end apart: 6, of which 3 were waited for; matrix products, arithmetic and copies ran while one was open for 5% of the time, Pallas kernels for 1%

profile of v4, /device:TPU:1, one launch (start us, length us, event | category | flops | bytes accessed | tf_op | source)
XLA Modules:
  0.0 187.6 jit_solution(3496096295580067417)
XLA Ops:
  0.6 4.8 %collective-permute-start = (bf16[64,2048]{1,0:T(8,128)(2,1)}, bf16[64,2048]{1,0:T(8,128)(2,1)S(1)}, u32[]{:S(2)}, u32[]{:S(2)}) collective-permute-start(bf16[64,2048]{1,0:T(8,128)(2,1)} %own_embed_ref.3), channel_id=1, source_target_pairs={{0,2},{2,0},{1,3},{3,1},{4,6},{6,4},{5,7},{7,5},{8,10},{10,8},{9,1... | collective-permute-start | bytes 786440 | tf_op jit(solution)/shard_map/ppermute | solution.py:482
  5.5 1.0 copy-done.11
  6.4 0.8 copy-done.19
  7.3 1.0 pack.1
  8.2 7.5 %all-to-all-start = ((bf16[4,544,128]{2,1,0:T(8,128)(2,1)}), bf16[4,544,128]{2,1,0:T(8,128)(2,1)S(1)}, u32[]{:S(2)}, u32[]{:S(2)}) async-start(bf16[4,544,128]{2,1,0:T(8,128)(2,1)} %pack.1), calls=%async_computation | async-start | bytes 1114112 | tf_op jit(solution)/shard_map/all_to_all | solution.py:495
  15.7 0.7 copy-done.26
  16.5 0.1 pad_add_fusion.place_ref
  16.6 0.9 pad_maximum_fusion.1.pair_ref
  17.5 1.9 %collective-permute-start.1 = (bf16[128,2048]{1,0:T(8,128)(2,1)}, bf16[128,2048]{1,0:T(8,128)(2,1)S(1)}, u32[]{:S(2)}, u32[]{:S(2)}) collective-permute-start(bf16[128,2048]{1,0:T(8,128)(2,1)} %pad_maximum_fusion.1.pair_ref), channel_id=1, source_target_pairs={{0,1},{1,0},{2,3},{3,2},{4,5},{5,4},{6,7},{7,6},{8,9},{9,8},{10,11... | collective-permute-start | bytes 1572872 | tf_op jit(solution)/shard_map/ppermute | solution.py:516
  19.4 0.5 fusion.8
  19.9 0.0 copy-start.1
  20.0 1.2 fusion.3
  21.2 0.0 copy-done.1
  21.2 0.5 fusion.10
  21.7 0.0 copy-start.2
  21.7 1.2 fusion.4
  22.9 0.0 copy-done.2
  22.9 0.5 fusion.12
  23.5 1.2 fusion.5
  24.6 1.2 stem.1
  25.9 0.7 copy-done.13
  26.6 0.6 copy-done.15
  27.2 6.3 %all_gather.9.act_ref = bf16[256,512]{1,0:T(8,128)(2,1)S(1)} all-gather(bf16[64,512]{1,0:T(8,128)(2,1)S(1)} %get-tuple-element.14), channel_id=1, replica_groups=mesh['zh'=4,'y'=8,'x'=4,'zl'=2,'core'=2] {'zl','core'}, dimensions={0}, use_global_device_ids=true | all-gather | bytes 327680 | tf_op jit(solution)/shard_map/all_gather | solution.py:510
  33.6 0.0 copy-start.3
  33.6 1.2 copy-done.3
  34.8 5.2 %embed.1 = (bf16[3328,128]{1,0:T(8,128)(2,1)S(1)}, f32[1,2048]{1,0:T(1,128)S(1)}, f32[1,512]{1,0:T(1,128)S(1)}, f32[64,512]{1,0:T(8,128)S(1)}) custom-call(s32[2]{0:T(128)S(1)} %pad_add_fusion.place_ref, s32[5]{0:T(128)S(1)} %copy-done.22, bf16[256,512]{1,0:T(8,128)(2,1)S(1)} %all_gather.9.act_ref, bf16[128,2048]{1,0:T(8,128)(2,1)} %pad_maximum_fusion.1.pair_ref, ...), custom_call_target="tpu_custom_call" | custom-call | tf_op jit(solution)/shard_map/embed/pallas_call | solution.py:524
  40.0 0.6 copy-done.17
  40.7 0.9 copy-done.8
  41.6 16.3 %all-to-all-start.1 = ((bf16[1664,2,128]{2,1,0:T(2,128)(2,1)}), bf16[1664,2,128]{2,1,0:T(2,128)(2,1)S(1)}, u32[]{:S(2)}, u32[]{:S(2)}) async-start(bf16[1664,2,128]{2,1,0:T(2,128)(2,1)} %bitcast.39), calls=%async_computation.1 | async-start | bytes 1703936 | tf_op jit(solution)/shard_map/all_to_all | solution.py:553
  57.9 0.5 fusion.25
  58.4 0.5 fusion.26
  59.0 0.7 copy-done.4
  59.6 0.5 fusion.27
  60.2 0.5 fusion
  60.7 0.5 fusion.1
  61.2 0.5 fusion.2
  61.7 0.4 copy-done.23
  62.1 0.1 copy-done.24
  62.1 0.1 copy-done.25
  62.2 0.1 fusion.24
  62.3 0.1 pad_maximum_fusion.back_ref
  62.3 21.3 %all-to-all-done.1 = bf16[1664,2,128]{2,1,0:T(2,128)(2,1)S(1)} async-done(((bf16[1664,2,128]{2,1,0:T(2,128)(2,1)}), bf16[1664,2,128]{2,1,0:T(2,128)(2,1)S(1)}, u32[]{:S(2)}, u32[]{:S(2)}) %all-to-all-start.1) | async-done | bytes 852000 | tf_op jit(solution)/shard_map/all_to_all | solution.py:553
  83.7 1.5 attend.1
  85.1 0.9 copy-done.9
  86.0 13.4 %all_to_all.40.in_ref = f32[16,24,128]{2,1,0:T(8,128)S(1)} all-to-all(f32[16,24,128]{2,1,0:T(8,128)S(1)} %get-tuple-element.17), channel_id=1, replica_groups=mesh['zh'=4,'y'=8,'x'=4,'zl'=2,'core'=2] {'x','zl','core'}, dimensions={0} | all-to-all | bytes 393216 | tf_op jit(solution)/shard_map/all_to_all | solution.py:591
  99.4 0.0 copy-start.7
  99.5 11.0 %all_to_all.41.in_ref = f32[8,24,128]{2,1,0:T(8,128)S(1)} all-to-all(f32[8,24,128]{2,1,0:T(8,128)S(1)} %combine_y.1), channel_id=1, replica_groups=mesh['zh'=4,'y'=8,'x'=4,'zl'=2,'core'=2] {'y'}, dimensions={0} | all-to-all | bytes 196608 | tf_op jit(solution)/shard_map/all_to_all | solution.py:605
  110.5 0.6 combine_zh.1
  111.1 3.3 %all-to-all-start.4 = ((f32[4,48,128]{2,1,0:T(8,128)}), f32[4,48,128]{2,1,0:T(8,128)S(1)}, u32[]{:S(2)}, u32[]{:S(2)}) async-start(f32[4,48,128]{2,1,0:T(8,128)} %combine_zh.1), calls=%async_computation.4 | async-start | bytes 196608 | tf_op jit(solution)/shard_map/all_to_all | solution.py:605
  114.4 0.0 copy-start.21
  115.1 6.3 %all-to-all-done.4.packed_ref = f32[4,48,128]{2,1,0:T(8,128)S(1)} async-done(((f32[4,48,128]{2,1,0:T(8,128)}), f32[4,48,128]{2,1,0:T(8,128)S(1)}, u32[]{:S(2)}, u32[]{:S(2)}) %all-to-all-start.4) | async-done | bytes 98336 | tf_op jit(solution)/shard_map/all_to_all | solution.py:605
  121.4 3.7 %attend_back.1 = (f32[8,128]{1,0:T(8,128)S(1)}, f32[64,128]{1,0:T(8,128)S(1)}, bf16[4,272,128]{2,1,0:T(8,128)(2,1)S(1)}) custom-call(s32[1]{0:T(128)S(6)} %copy.65.target_ref, f32[4,48,128]{2,1,0:T(8,128)S(1)} %all-to-all-done.4.packed_ref, bf16[16,128]{1,0:T(8,128)(2,1)S(1)} %bitcast.43, bf16[256,2048]{1,0:T(8,128)(2,1)S(1)} %copy-done.5, ...), custom_call_target="tpu_custom_call" | custom-call | tf_op jit(solution)/shard_map/attend_back/pallas_call | solution.py:607
  125.1 11.3 %all_to_all.42.in_ref = bf16[4,272,128]{2,1,0:T(8,128)(2,1)S(1)} all-to-all(bf16[4,272,128]{2,1,0:T(8,128)(2,1)S(1)} %get-tuple-element.20), channel_id=1, replica_groups=mesh['zh'=4,'y'=8,'x'=4,'zl'=2,'core'=2] {'zl','core'}, dimensions={0} | all-to-all | bytes 557056 | tf_op jit(solution)/shard_map/all_to_all | solution.py:628
  136.4 0.1 gather.1
  136.6 18.7 %all_to_all.43 = bf16[256,2,128]{2,1,0:T(2,128)(2,1)S(1)} all-to-all(bf16[256,2,128]{2,1,0:T(2,128)(2,1)S(1)} %bitcast.40), channel_id=1, replica_groups=mesh['zh'=4,'y'=8,'x'=4,'zl'=2,'core'=2] {'zh','y','x'}, dimensions={0} | all-to-all | bytes 262144 | tf_op jit(solution)/shard_map/all_to_all | solution.py:638
  155.3 2.0 %stem_back.1 = bf16[1280,128]{1,0:T(8,128)(2,1)} custom-call(bf16[512,128]{1,0:T(8,128)(2,1)S(1)} %bitcast.41, f32[64,512]{1,0:T(8,128)S(1)} %copy-done.18, f32[1,512]{1,0:T(1,128)S(1)} %get-tuple-element.22.scale_ref, f32[64,128]{1,0:T(8,128)S(1)} %get-tuple-element.23.direct_ref, f32[64,512]{1,0:T(8,128)S(1)} %copy-done.16, bf16[512,256]{1,0:T(8,128)(2,1)S(1)} %copy-done.14), custom_call_target="tpu_custom_call" | custom-call | tf_op jit(solution)/shard_map/stem_back/pallas_call | solution.py:645
  157.3 6.4 %all-to-all-start.7 = ((bf16[640,2,128]{2,1,0:T(2,128)(2,1)}), bf16[640,2,128]{2,1,0:T(2,128)(2,1)S(1)}, u32[]{:S(2)}, u32[]{:S(2)}) async-start(bf16[640,2,128]{2,1,0:T(2,128)(2,1)} %bitcast.15), calls=%async_computation.7 | async-start | bytes 655360 | tf_op jit(solution)/shard_map/all_to_all | solution.py:660
  163.7 0.5 slice.6
  164.2 13.2 %all-to-all-done.7 = bf16[640,2,128]{2,1,0:T(2,128)(2,1)S(1)} async-done(((bf16[640,2,128]{2,1,0:T(2,128)(2,1)}), bf16[640,2,128]{2,1,0:T(2,128)(2,1)S(1)}, u32[]{:S(2)}, u32[]{:S(2)}) %all-to-all-start.7) | async-done | bytes 327712 | tf_op jit(solution)/shard_map/all_to_all | solution.py:660
  177.5 0.3 convert_reduce_fusion
  177.8 9.0 %all-gather = f32[20,2,128]{2,1,0:T(2,128)S(1)} all-gather(f32[5,2,128]{2,1,0:T(2,128)S(1)} %convert_reduce_fusion), channel_id=2, replica_groups=mesh['zh'=4,'y'=8,'x'=4,'zl'=2,'core'=2] {'zl','core'}, dimensions={0}, use_global_device_ids=true | all-gather | bytes 25600 | tf_op jit(solution)/shard_map/all_gather | solution.py:662
  186.8 0.1 reshape.46
  186.9 0.1 reshape.47
  187.0 0.7 dynamic_slice.3
  (43 shorter events, 0.2 us)
Async XLA Ops:
  0.6 15.9 %collective-permute-start = (bf16[64,2048]{1,0:T(8,128)(2,1)}, bf16[64,2048]{1,0:T(8,128)(2,1)S(1)}, u32[]{:S(2)}, u32[]{:S(2)}) collective-permute-start(bf16[64,2048]{1,0:T(8,128)(2,1)} %own_embed_ref.3), channel_id=1, source_target_pairs={{0,2},{2,0},{1,3},{3,1},{4,6},{6,4},{5,7},{7,5},{8,10},{10,8},{9,1... | collective-permute-start | bytes 786440 | tf_op jit(solution)/shard_map/ppermute | solution.py:482
  5.5 1.0 copy-start.11
  6.4 0.8 copy-start.19
  8.2 8.3 %copy-start.6 = (bf16[64,2048]{1,0:T(8,128)(2,1)S(1)}, bf16[64,2048]{1,0:T(8,128)(2,1)}, u32[]{:S(2)}) copy-start(bf16[64,2048]{1,0:T(8,128)(2,1)} %own_embed_ref.3) | copy-start | bytes 786436
  8.2 16.4 %all-to-all-start = ((bf16[4,544,128]{2,1,0:T(8,128)(2,1)}), bf16[4,544,128]{2,1,0:T(8,128)(2,1)S(1)}, u32[]{:S(2)}, u32[]{:S(2)}) async-start(bf16[4,544,128]{2,1,0:T(8,128)(2,1)} %pack.1), calls=%async_computation | async-start | bytes 1114112 | tf_op jit(solution)/shard_map/all_to_all | solution.py:495
  15.7 0.7 copy-start.26
  16.5 2.9 %copy-start = (bf16[2048,256]{1,0:T(8,128)(2,1)S(1)}, bf16[2048,256]{1,0:T(8,128)(2,1)}, u32[]{:S(2)}) copy-start(bf16[2048,256]{1,0:T(8,128)(2,1)} %value_ref.1) | copy-start | bytes 3145732
  17.5 16.1 %collective-permute-start.1 = (bf16[128,2048]{1,0:T(8,128)(2,1)}, bf16[128,2048]{1,0:T(8,128)(2,1)S(1)}, u32[]{:S(2)}, u32[]{:S(2)}) collective-permute-start(bf16[128,2048]{1,0:T(8,128)(2,1)} %pad_maximum_fusion.1.pair_ref), channel_id=1, source_target_pairs={{0,1},{1,0},{2,3},{3,2},{4,5},{5,4},{6,7},{7,6},{8,9},{9,8},{10,11... | collective-permute-start | bytes 1572872 | tf_op jit(solution)/shard_map/ppermute | solution.py:516
  19.9 1.2 copy-start.1
  21.7 1.2 copy-start.2
  25.9 0.7 copy-start.13
  26.6 0.6 copy-start.15
  27.2 6.3 %copy-start.12 = (bf16[64,2048]{1,0:T(8,128)(2,1)S(1)}, bf16[64,2048]{1,0:T(8,128)(2,1)}, u32[]{:S(2)}) copy-start(bf16[64,2048]{1,0:T(8,128)(2,1)} %vocab_ref.1) | copy-start | bytes 786436
  27.2 6.3 %copy-start.20 = (bf16[2,2048]{1,0:T(2,128)(2,1)S(1)}, bf16[2,2048]{1,0:T(2,128)(2,1)}, u32[]{:S(2)}) copy-start(bf16[2,2048]{1,0:T(2,128)(2,1)} %frame_ref.1) | copy-start | bytes 24580
  27.2 6.3 %copy-start.22 = (s32[5]{0:T(128)S(1)}, s32[5]{0:T(128)}, u32[]{:S(2)}) copy-start(s32[5]{0:T(128)} %ids_ref.1) | copy-start | bytes 64
  33.6 1.2 copy-start.3
  40.0 0.6 copy-start.17
  40.7 0.9 copy-start.8
  41.6 42.1 %all-to-all-start.1 = ((bf16[1664,2,128]{2,1,0:T(2,128)(2,1)}), bf16[1664,2,128]{2,1,0:T(2,128)(2,1)S(1)}, u32[]{:S(2)}, u32[]{:S(2)}) async-start(bf16[1664,2,128]{2,1,0:T(2,128)(2,1)} %bitcast.39), calls=%async_computation.1 | async-start | bytes 1703936 | tf_op jit(solution)/shard_map/all_to_all | solution.py:553
  58.4 1.2 copy-start.4
  61.2 0.9 copy-start.23
  61.2 1.0 copy-start.24
  61.2 1.0 copy-start.25
  62.3 21.4 %copy-start.5 = (bf16[256,2048]{1,0:T(8,128)(2,1)S(1)}, bf16[256,2048]{1,0:T(8,128)(2,1)}, u32[]{:S(2)}) copy-start(bf16[256,2048]{1,0:T(8,128)(2,1)} %out_weight_ref.3) | copy-start | bytes 3145732
  85.1 0.9 copy-start.9
  86.0 35.4 %copy-start.10 = (bf16[2,256,768]{2,1,0:T(8,128)(2,1)S(1)}, bf16[2,256,768]{2,1,0:T(8,128)(2,1)}, u32[]{:S(2)}) copy-start(bf16[2,256,768]{2,1,0:T(8,128)(2,1)} %copy-done.9) | copy-start | bytes 2359300
  99.4 22.0 %copy-start.7 = (bf16[64,2048]{1,0:T(8,128)(2,1)S(1)}, bf16[64,2048]{1,0:T(8,128)(2,1)}, u32[]{:S(2)}) copy-start(bf16[64,2048]{1,0:T(8,128)(2,1)} %own_embed_ref.3) | copy-start | bytes 786436
  111.1 10.3 %all-to-all-start.4 = ((f32[4,48,128]{2,1,0:T(8,128)}), f32[4,48,128]{2,1,0:T(8,128)S(1)}, u32[]{:S(2)}, u32[]{:S(2)}) async-start(f32[4,48,128]{2,1,0:T(8,128)} %combine_zh.1), calls=%async_computation.4 | async-start | bytes 196608 | tf_op jit(solution)/shard_map/all_to_all | solution.py:605
  114.4 7.0 %copy-start.21 = (bf16[2048]{0:T(1024)(128)(2,1)S(1)}, bf16[2048]{0:T(1024)(128)(2,1)}, u32[]{:S(2)}) copy-start(bf16[2048]{0:T(1024)(128)(2,1)} %param.18) | copy-start | bytes 12292
  136.4 18.9 %copy-start.14 = (bf16[512,256]{1,0:T(8,128)(2,1)S(1)}, bf16[512,256]{1,0:T(8,128)(2,1)}, u32[]{:S(2)}) copy-start(bf16[512,256]{1,0:T(8,128)(2,1)} %copy-done.13) | copy-start | bytes 786436
  136.6 18.7 %copy-start.16 = (f32[64,512]{1,0:T(8,128)S(1)}, f32[64,512]{1,0:T(8,128)}, u32[]{:S(2)}) copy-start(f32[64,512]{1,0:T(8,128)} %copy-done.15) | copy-start | bytes 393220
  136.6 18.7 %copy-start.18 = (f32[64,512]{1,0:T(8,128)S(1)}, f32[64,512]{1,0:T(8,128)}, u32[]{:S(2)}) copy-start(f32[64,512]{1,0:T(8,128)} %copy-done.17) | copy-start | bytes 393220
  157.3 20.1 %all-to-all-start.7 = ((bf16[640,2,128]{2,1,0:T(2,128)(2,1)}), bf16[640,2,128]{2,1,0:T(2,128)(2,1)S(1)}, u32[]{:S(2)}, u32[]{:S(2)}) async-start(bf16[640,2,128]{2,1,0:T(2,128)(2,1)} %bitcast.15), calls=%async_computation.7 | async-start | bytes 655360 | tf_op jit(solution)/shard_map/all_to_all | solution.py:660

commit v5 on v4

--- a/solution.py
+++ b/solution.py
@@ -20,12 +20,17 @@
 TN = (((0,), (0,)), ((), ()))
 VMEM_LIMIT = 40 * 1024 * 1024
 LINES = 4
+FAR = pltpu.HBM
 N_S = 4
 SPACE_OF_BLOCK = (0, 2, 1, 3)
 
 
 def dot(lhs, rhs, dims=(((1,), (0,)), ((), ()))):
     return lax.dot_general(lhs, rhs, dims, preferred_element_type=F32)
+
+
+def kept(array):
+    return pltpu.with_memory_space_constraint(array, FAR)
 
 
 def thirds(row):
@@ -54,7 +59,18 @@
     return [(a, b) for a in (-1, 0, 1) for b in (-1, 0, 1)]
 
 
-def stem_kernel(cols, rows, packed_ref, act_ref, slope_ref, tokens_ref, weight_ref):
+def stem_kernel(
+    cols,
+    rows,
+    packed_ref,
+    act_ref,
+    slope_far,
+    tokens_far,
+    slope_ref,
+    tokens_ref,
+    weight_ref,
+    done,
+):
     n_s = packed_ref.shape[0]
     lanes, channels = tokens_ref.shape
     own = act_ref.shape[0]
@@ -75,6 +91,8 @@
         at = 2 * s * half
         weight_ref[at : at + half, :] = pairs[:, :own]
         weight_ref[at + half : at + 2 * half, :] = pairs[:, own:]
+    tokens_store = pltpu.make_async_copy(tokens_ref, tokens_far, done.at[0])
+    tokens_store.start()
     tokens = tokens_ref[...]
     total = jnp.zeros((own, lanes), F32)
     for tap, (row_off, col_off) in enumerate(offsets()):
@@ -88,10 +106,14 @@
     square = total * total
     bent = jnp.tanh(root * (total + 0.044715 * (square * total)))
     half_up = 0.5 * (1.0 + bent)
-    act_ref[...] = (total * half_up).astype(BF)
     slope_ref[...] = half_up + 0.5 * total * (1.0 - bent * bent) * (
         root * (1.0 + 3 * 0.044715 * square)
     )
+    slope_store = pltpu.make_async_copy(slope_ref, slope_far, done.at[1])
+    slope_store.start()
+    act_ref[...] = (total * half_up).astype(BF)
+    tokens_store.wait()
+    slope_store.wait()
 
 
 def stem_back_kernel(
@@ -173,7 +195,15 @@
     return jnp.concatenate([lines[i : i + 1] for i in range(lines.shape[0])], axis=1)
 
 
-def pack_kernel(patches_ref, stem_ref, out_ref):
+def pack_kernel(patches_far, stem_far, out_ref, patches_ref, stem_ref, done):
+    fetches = [
+        pltpu.make_async_copy(patches_far, patches_ref, done.at[0]),
+        pltpu.make_async_copy(stem_far, stem_ref, done.at[1]),
+    ]
+    for fetch in fetches:
+        fetch.start()
+    for fetch in fetches:
+        fetch.wait()
     count = patches_ref.shape[0]
     lane_blocks = patches_ref.shape[1] // LANES
     half = stem_ref.shape[0] // 2
@@ -199,17 +229,30 @@
     across_ref,
     frame_ref,
     gain_ref,
-    query_ref,
-    key_ref,
-    value_ref,
+    query_far,
+    key_far,
+    value_far,
     own_embed_ref,
     vocab_ref,
     moved_ref,
     embed_sum_ref,
     scale_ref,
+    back_unit_far,
+    wide_ref,
+    query_ref,
+    key_ref,
+    value_ref,
     back_unit_ref,
-    wide_ref,
+    done,
 ):
+    fetches = [
+        pltpu.make_async_copy(source, target, done.at[i])
+        for i, (source, target) in enumerate(
+            ((query_far, query_ref), (key_far, key_ref), (value_far, value_ref))
+        )
+    ]
+    for fetch in fetches:
+        fetch.start()
     core = place_ref[0]
     width = frame_ref.shape[1]
     frames = frame_ref.shape[0]
@@ -239,6 +282,8 @@
         scale_ref[:, at : at + tokens] = scale_row
         back_unit_ref[:, at : at + tokens] = dot(own_embed_ref[...], embedded, NT) * scale_row
         for part, weight_ref in enumerate((query_ref, key_ref, value_ref)):
+            if frame == 0:
+                fetches[part].wait()
             made = dot(normed, weight_ref[...])
             for slot in range(slots):
                 for i in range(inner // LANES):
@@ -246,6 +291,8 @@
                     wide_ref[chunk_rows(n_t, chunks, chunk, frame), :] = made[
                         slot * n_t : (slot + 1) * n_t, i * LANES : (i + 1) * LANES
                     ]
+    store = pltpu.make_async_copy(back_unit_ref, back_unit_far, done.at[3])
+    store.start()
     embed_sum_ref[...] = embed_sum * (1.0 / N_S)
     vocab = vocab_ref.shape[0]
     ratings = ids_ref.shape[0]
@@ -261,6 +308,7 @@
     wide_ref[chunk_rows(n_t, chunks, chunks - 1, 0), :] = jnp.concatenate(lines, axis=0).T
     wide_ref[chunk_rows(n_t, chunks, chunks - 1, 1), :] = jnp.zeros((n_t, LANES), F32)
     moved_ref[...] = wide_ref[...].astype(BF)
+    store.wait()
 
 
 def attention_weights(key, query):
@@ -270,9 +318,19 @@
 
 
 def forward_kernel(
-    heads, moved_ref, out_weight_ref, embed_sum_ref, back_ref, qkv_ref, packed_ref, wide_ref
+    heads,
+    moved_ref,
+    out_weight_ref,
+    embed_sum_ref,
+    back_ref,
+    qkv_far,
+    packed_ref,
+    wide_ref,
+    qkv_ref,
+    done,
 ):
     del back_ref
+    stores = []
     slots, frames = qkv_ref.shape[0], qkv_ref.shape[1]
     n_t = frames // 2
     per = 3 * heads
@@ -286,6 +344,9 @@
                 qkv_ref[
                     slot, frame * n_t : (frame + 1) * n_t, chunk * LANES : (chunk + 1) * LANES
                 ] = wide_ref[rows, :].astype(BF)
+        store = pltpu.make_async_copy(qkv_ref.at[slot], qkv_far.at[slot], done.at[slot])
+        store.start()
+        stores.append(store)
         for head, query, key, value in split_heads(qkv_ref[slot], heads):
             weights = attention_weights(key, query)
             mixture = dot(weights.astype(BF), value, TN).astype(BF).astype(F32)
@@ -298,6 +359,8 @@
     packed = jnp.concatenate([pooled, rating, blank], axis=0)
     for i in range(packed_ref.shape[0]):
         packed_ref[i] = packed
+    for store in stores:
+        store.wait()
 
 
 def combine_kernel(lines, per, joint, in_ref, out_ref):
@@ -478,6 +541,7 @@
     assert frames_dev == 2 and slots == 2
 
     whole = pl.BlockSpec(memory_space=pltpu.VMEM)
+    far = pl.BlockSpec(memory_space=FAR)
     params = pltpu.CompilerParams(vmem_limit_bytes=VMEM_LIMIT)
     other = lax.ppermute(embed_weight, "zl", [(0, 1), (1, 0)])
 
@@ -488,10 +552,15 @@
         pack_kernel,
         name="pack",
         out_shape=jax.ShapeDtypeStruct((n_s, packed_rows, LANES), BF),
-        in_specs=[whole] * 2,
+        in_specs=[far] * 2,
         out_specs=whole,
+        scratch_shapes=[
+            pltpu.VMEM(patch_rows.shape, BF),
+            pltpu.VMEM(stem_weight.shape, BF),
+            pltpu.SemaphoreType.DMA((2,)),
+        ],
         compiler_params=params,
-    )(patch_rows, stem_weight)
+    )(kept(patch_rows), kept(stem_weight))
     packed = lax.all_to_all(packed, S_AXES, 0, 0, tiled=True)
 
     act, gelu_slope, patch_tokens = pl.pallas_call(
@@ -499,12 +568,17 @@
         name="stem",
         out_shape=(
             jax.ShapeDtypeStruct((own_channels, tokens_dev), BF),
-            jax.ShapeDtypeStruct((own_channels, tokens_dev), F32),
-            jax.ShapeDtypeStruct((tokens_dev, channels), BF),
+            pltpu.HBM((own_channels, tokens_dev), F32),
+            pltpu.HBM((tokens_dev, channels), BF),
         ),
         in_specs=[whole],
-        out_specs=(whole,) * 3,
-        scratch_shapes=[pltpu.VMEM((9 * channels, own_channels), BF)],
+        out_specs=(whole, far, far),
+        scratch_shapes=[
+            pltpu.VMEM((own_channels, tokens_dev), F32),
+            pltpu.VMEM((tokens_dev, channels), BF),
+            pltpu.VMEM((9 * channels, own_channels), BF),
+            pltpu.SemaphoreType.DMA((2,)),
+        ],
         compiler_params=params,
     )(packed)
     act = lax.all_gather(act, S_AXES, axis=0, tiled=True)
@@ -528,11 +602,13 @@
             jax.ShapeDtypeStruct((n_t * chunks * 2, LANES), BF),
             jax.ShapeDtypeStruct((1, width), F32),
             jax.ShapeDtypeStruct((1, tokens_dev), F32),
-            jax.ShapeDtypeStruct((own_channels, tokens_dev), F32),
+            pltpu.HBM((own_channels, tokens_dev), F32),
         ),
-        in_specs=[scalars] * 2 + [whole] * 10,
-        out_specs=(whole,) * 4,
-        scratch_shapes=[pltpu.VMEM((n_t * chunks * 2, LANES), F32)],
+        in_specs=[scalars] * 2 + [whole] * 5 + [far] * 3 + [whole] * 2,
+        out_specs=(whole,) * 3 + (far,),
+        scratch_shapes=[pltpu.VMEM((n_t * chunks * 2, LANES), F32)]
+        + [pltpu.VMEM((width, inner), BF)] * 3
+        + [pltpu.VMEM((own_channels, tokens_dev), F32), pltpu.SemaphoreType.DMA((4,))],
         compiler_params=params,
     )(
         place,
@@ -542,9 +618,9 @@
         across,
         frame_embed,
         attention_gain[None, :],
-        query_weight,
-        key_weight,
-        value_weight,
+        kept(query_weight),
+        kept(key_weight),
+        kept(value_weight),
         embed_weight,
         unembedding,
     )
@@ -579,12 +655,16 @@
         functools.partial(forward_kernel, heads),
         name="attend",
         out_shape=(
-            jax.ShapeDtypeStruct((slots, all_frames, 3 * inner), BF),
+            pltpu.HBM((slots, all_frames, 3 * inner), BF),
             jax.ShapeDtypeStruct((first, lines + 8, LANES), F32),
         ),
         in_specs=[whole] * 3 + [pl.BlockSpec(memory_space=pl.ANY)],
-        out_specs=(whole, whole),
-        scratch_shapes=[pltpu.VMEM((n_t * chunks * 2, LANES), F32)],
+        out_specs=(far, whole),
+        scratch_shapes=[
+            pltpu.VMEM((n_t * chunks * 2, LANES), F32),
+            pltpu.VMEM((slots, all_frames, 3 * inner), BF),
+            pltpu.SemaphoreType.DMA((slots,)),
+        ],
         compiler_params=params,
     )(moved, output_weight, embed_sum, back)
 

time: 189 us -> 185 us (0.979)
  local copies, waits for them, and re-layouts: 10.2 us -> 5.78 us
  Pallas kernels: 15.3 us -> 18.4 us
    unnamed x54 -> x36, local copies, waits for them, and re-layouts: 8.79 us -> 4.4 us
  transfers between devices with their start and end apart: 6 -> 6, of which waited for: 3 -> 4; matrix products, arithmetic and copies ran while one was open for 5% -> 5% of each run, Pallas kernels for 1% -> 2%
where the time goes in v5:
time: 185 us; the launch traced here: 184 us
  blocking collectives  69.5 us (38%)
  starting transfers between devices  40.5 us (22%)
  waiting for transfers between devices  39.7 us (21%)
  Pallas kernels  18.4 us (10%)
  matrix products  7.6 us (4%)
  local copies, waits for them, and re-layouts  5.78 us (3%)
    all_to_all x1, waiting for transfers between devices, on_device(): moved = lax.all_to_all(moved, T_AXES, 0, 0, tiled=True)  19.7 us
    all_to_all x1, blocking collectives, on_device(): lax.all_to_all(sent.reshape(n_t * LINES // 2, 2, LANES), T_AXES, 0, 0, ti...  18.7 us
    all_to_all x1, starting transfers between devices, on_device(): moved = lax.all_to_all(moved, T_AXES, 0, 0, tiled=True)  16.3 us
    all_to_all x1, waiting for transfers between devices, on_device(): sums = lax.all_to_all(sums, T_AXES, 0, 0, tiled=True)  13.2 us
    all_to_all x1, blocking collectives, on_device(): packed = lax.all_to_all(packed, ('x',) + S_AXES, 0, 0, tiled=True)  12.5 us
    all_to_all x1, blocking collectives, on_device(): sent = lax.all_to_all(sent, S_AXES, 0, 0, tiled=True)  11.3 us
    all_to_all x1, blocking collectives, on_device(): packed = lax.all_to_all(packed, axis, 0, 0, tiled=True)  11.2 us
    all_gather x1, blocking collectives, on_device(): lax.all_gather(sums, S_AXES, axis=0, tiled=False)  9 us
  transfers between devices with their start and end apart: 6, of which 4 were waited for; matrix products, arithmetic and copies ran while one was open for 5% of the time, Pallas kernels for 2%

profile of v5, /device:TPU:1, one launch (start us, length us, event | category | flops | bytes accessed | tf_op | source)
XLA Modules:
  0.0 183.7 jit_solution(12377618473349517793)
XLA Ops:
  0.6 4.8 %collective-permute-start = (bf16[64,2048]{1,0:T(8,128)(2,1)}, bf16[64,2048]{1,0:T(8,128)(2,1)S(1)}, u32[]{:S(2)}, u32[]{:S(2)}) collective-permute-start(bf16[64,2048]{1,0:T(8,128)(2,1)} %own_embed_ref.3), channel_id=1, source_target_pairs={{0,2},{2,0},{1,3},{3,1},{4,6},{6,4},{5,7},{7,5},{8,10},{10,8},{9,1... | collective-permute-start | bytes 786440 | tf_op jit(solution)/shard_map/ppermute | solution.py:546
  5.5 2.0 %pack.1 = bf16[4,544,128]{2,1,0:T(8,128)(2,1)} custom-call(bf16[128,256]{1,0:T(8,128)(2,1)} %bitcast.46, bf16[576,256]{1,0:T(8,128)(2,1)} %stem_far.1), custom_call_target="tpu_custom_call" | custom-call | tf_op jit(solution)/shard_map/pack/pallas_call | solution.py:551
  7.5 0.0 copy-start.1
  7.5 7.5 %all-to-all-start = ((bf16[4,544,128]{2,1,0:T(8,128)(2,1)}), bf16[4,544,128]{2,1,0:T(8,128)(2,1)S(1)}, u32[]{:S(2)}, u32[]{:S(2)}) async-start(bf16[4,544,128]{2,1,0:T(8,128)(2,1)} %pack.1), calls=%async_computation | async-start | bytes 1114112 | tf_op jit(solution)/shard_map/all_to_all | solution.py:564
  15.0 0.7 copy-done.17
  15.7 0.1 pad_add_fusion.place_ref
  15.8 0.0 collective-permute-done
  15.8 0.1 broadcast_select_fusion.1
  15.9 2.2 %collective-permute-start.1 = (bf16[128,2048]{1,0:T(8,128)(2,1)S(1)}, bf16[128,2048]{1,0:T(8,128)(2,1)S(1)}, u32[]{:S(2)}, u32[]{:S(2)}) collective-permute-start(bf16[128,2048]{1,0:T(8,128)(2,1)S(1)} %pad_maximum_fusion.1.pair_ref), channel_id=1, source_target_pairs={{0,1},{1,0},{2,3},{3,2},{4,5},{5,4},{6,7},{7,6},{8,9},{9,8},{10,11... | collective-permute-start | bytes 1572872 | tf_op jit(solution)/shard_map/ppermute | solution.py:590
  18.1 0.0 copy-done.11
  18.1 0.5 fusion.8
  18.7 0.0 copy-start.13
  18.7 0.5 fusion.3
  19.2 0.7 copy-done.13
  19.9 0.5 fusion.10
  20.4 0.0 copy-start.15
  20.4 0.5 fusion.4
  21.0 0.7 copy-done.15
  21.6 0.5 fusion.12
  22.2 0.5 fusion.5
  22.7 0.5 all-to-all-done.packed_ref
  23.2 1.9 %stem.1 = (bf16[64,512]{1,0:T(8,128)(2,1)S(1)}, f32[64,512]{1,0:T(8,128)}, bf16[512,256]{1,0:T(8,128)(2,1)}) custom-call(bf16[4,544,128]{2,1,0:T(8,128)(2,1)S(1)} %all-to-all-done.packed_ref), custom_call_target="tpu_custom_call" | custom-call | tf_op jit(solution)/shard_map/stem/pallas_call | solution.py:566
  25.1 0.0 copy-start.4
  25.1 0.0 copy-start.8
  25.1 0.0 copy-start.10
  25.1 6.7 %all_gather.9.act_ref = bf16[256,512]{1,0:T(8,128)(2,1)S(1)} all-gather(bf16[64,512]{1,0:T(8,128)(2,1)S(1)} %get-tuple-element.14), channel_id=1, replica_groups=mesh['zh'=4,'y'=8,'x'=4,'zl'=2,'core'=2] {'zl','core'}, dimensions={0}, use_global_device_ids=true | all-gather | bytes 327680 | tf_op jit(solution)/shard_map/all_gather | solution.py:584
  31.8 0.0 collective-permute-done.1.across_ref
  31.8 6.4 %embed.1 = (bf16[3328,128]{1,0:T(8,128)(2,1)S(1)}, f32[1,2048]{1,0:T(1,128)S(1)}, f32[1,512]{1,0:T(1,128)S(1)}, f32[64,512]{1,0:T(8,128)}) custom-call(s32[2]{0:T(128)S(1)} %pad_add_fusion.place_ref, s32[5]{0:T(128)S(1)} %copy-done.10, bf16[256,512]{1,0:T(8,128)(2,1)S(1)} %all_gather.9.act_ref, bf16[128,2048]{1,0:T(8,128)(2,1)S(1)} %pad_maximum_fusion.1.pair_ref, ...), custom_call_target="tpu_custom_call" | custom-call | tf_op jit(solution)/shard_map/embed/pallas_call | solution.py:598
  38.2 0.9 copy-done.2
  39.1 16.3 %all-to-all-start.1 = ((bf16[1664,2,128]{2,1,0:T(2,128)(2,1)}), bf16[1664,2,128]{2,1,0:T(2,128)(2,1)S(1)}, u32[]{:S(2)}, u32[]{:S(2)}) async-start(bf16[1664,2,128]{2,1,0:T(2,128)(2,1)} %bitcast.39), calls=%async_computation.1 | async-start | bytes 1703936 | tf_op jit(solution)/shard_map/all_to_all | solution.py:629
  55.4 0.0 copy-start.14
  55.4 1.8 %fusion.25 = f32[128,256]{0,1:T(8,128)S(1)} fusion(bf16[2048,256]{1,0:T(8,128)(2,1)} %value_far.1, bf16[128,2048]{1,0:T(8,128)(2,1)S(1)} %collective-permute-done.1.across_ref, f32[2048]{0:T(1024)S(1)} %convert_element_type.34), kind=kOutput, calls=%fused_computation.36 | convolution fusion | flops 135790592 | bytes 1712128 | tf_op jit(solution)/shard_map/dot_general | solution.py:29
  57.3 0.0 copy-start.16
  57.3 0.5 fusion.26
  57.8 0.7 copy-done.16
  58.5 0.5 fusion.27
  59.0 0.7 copy-done.12
  59.7 0.5 fusion
  60.2 0.5 fusion.1
  60.7 0.5 fusion.2
  61.3 0.1 fusion.24
  61.3 0.0 copy-start
  61.3 0.1 pad_maximum_fusion.back_ref
  61.4 19.7 %all-to-all-done.1 = bf16[1664,2,128]{2,1,0:T(2,128)(2,1)S(1)} async-done(((bf16[1664,2,128]{2,1,0:T(2,128)(2,1)}), bf16[1664,2,128]{2,1,0:T(2,128)(2,1)S(1)}, u32[]{:S(2)}, u32[]{:S(2)}) %all-to-all-start.1) | async-done | bytes 852000 | tf_op jit(solution)/shard_map/all_to_all | solution.py:629
  81.1 1.7 attend.1
  82.8 12.5 %all_to_all.40.in_ref = f32[16,24,128]{2,1,0:T(8,128)S(1)} all-to-all(f32[16,24,128]{2,1,0:T(8,128)S(1)} %get-tuple-element.17), channel_id=1, replica_groups=mesh['zh'=4,'y'=8,'x'=4,'zl'=2,'core'=2] {'x','zl','core'}, dimensions={0} | all-to-all | bytes 393216 | tf_op jit(solution)/shard_map/all_to_all | solution.py:671
  95.4 11.2 %all_to_all.41.in_ref = f32[8,24,128]{2,1,0:T(8,128)S(1)} all-to-all(f32[8,24,128]{2,1,0:T(8,128)S(1)} %combine_y.1), channel_id=1, replica_groups=mesh['zh'=4,'y'=8,'x'=4,'zl'=2,'core'=2] {'y'}, dimensions={0} | all-to-all | bytes 196608 | tf_op jit(solution)/shard_map/all_to_all | solution.py:685
  106.6 0.6 combine_zh.1
  107.2 3.3 %all-to-all-start.4 = ((f32[4,48,128]{2,1,0:T(8,128)}), f32[4,48,128]{2,1,0:T(8,128)S(1)}, u32[]{:S(2)}, u32[]{:S(2)}) async-start(f32[4,48,128]{2,1,0:T(8,128)} %combine_zh.1), calls=%async_computation.4 | async-start | bytes 196608 | tf_op jit(solution)/shard_map/all_to_all | solution.py:685
  110.5 0.0 copy-start.9
  111.2 6.3 %all-to-all-done.4.packed_ref = f32[4,48,128]{2,1,0:T(8,128)S(1)} async-done(((f32[4,48,128]{2,1,0:T(8,128)}), f32[4,48,128]{2,1,0:T(8,128)S(1)}, u32[]{:S(2)}, u32[]{:S(2)}) %all-to-all-start.4) | async-done | bytes 98336 | tf_op jit(solution)/shard_map/all_to_all | solution.py:685
  117.5 3.7 %attend_back.1 = (f32[8,128]{1,0:T(8,128)S(1)}, f32[64,128]{1,0:T(8,128)S(1)}, bf16[4,272,128]{2,1,0:T(8,128)(2,1)S(1)}) custom-call(s32[1]{0:T(128)S(6)} %copy.65.target_ref, f32[4,48,128]{2,1,0:T(8,128)S(1)} %all-to-all-done.4.packed_ref, bf16[16,128]{1,0:T(8,128)(2,1)S(1)} %bitcast.42, bf16[256,2048]{1,0:T(8,128)(2,1)S(1)} %copy-done, ...), custom_call_target="tpu_custom_call" | custom-call | tf_op jit(solution)/shard_map/attend_back/pallas_call | solution.py:687
  121.2 11.3 %all_to_all.42.in_ref = bf16[4,272,128]{2,1,0:T(8,128)(2,1)S(1)} all-to-all(bf16[4,272,128]{2,1,0:T(8,128)(2,1)S(1)} %get-tuple-element.20), channel_id=1, replica_groups=mesh['zh'=4,'y'=8,'x'=4,'zl'=2,'core'=2] {'zl','core'}, dimensions={0} | all-to-all | bytes 557056 | tf_op jit(solution)/shard_map/all_to_all | solution.py:708
  132.5 0.1 gather.1
  132.7 18.7 %all_to_all.43 = bf16[256,2,128]{2,1,0:T(2,128)(2,1)S(1)} all-to-all(bf16[256,2,128]{2,1,0:T(2,128)(2,1)S(1)} %bitcast.40), channel_id=1, replica_groups=mesh['zh'=4,'y'=8,'x'=4,'zl'=2,'core'=2] {'zh','y','x'}, dimensions={0} | all-to-all | bytes 262144 | tf_op jit(solution)/shard_map/all_to_all | solution.py:718
  151.4 2.0 %stem_back.1 = bf16[1280,128]{1,0:T(8,128)(2,1)} custom-call(bf16[512,128]{1,0:T(8,128)(2,1)S(1)} %bitcast.41, f32[64,512]{1,0:T(8,128)S(1)} %copy-done.7, f32[1,512]{1,0:T(1,128)S(1)} %get-tuple-element.22.scale_ref, f32[64,128]{1,0:T(8,128)S(1)} %get-tuple-element.23.direct_ref, f32[64,512]{1,0:T(8,128)S(1)} %copy-done.6, bf16[512,256]{1,0:T(8,128)(2,1)S(1)} %copy-done.5), custom_call_target="tpu_custom_call" | custom-call | tf_op jit(solution)/shard_map/stem_back/pallas_call | solution.py:725
  153.4 6.4 %all-to-all-start.7 = ((bf16[640,2,128]{2,1,0:T(2,128)(2,1)}), bf16[640,2,128]{2,1,0:T(2,128)(2,1)S(1)}, u32[]{:S(2)}, u32[]{:S(2)}) async-start(bf16[640,2,128]{2,1,0:T(2,128)(2,1)} %bitcast.15), calls=%async_computation.7 | async-start | bytes 655360 | tf_op jit(solution)/shard_map/all_to_all | solution.py:740
  159.8 0.5 slice.6
  160.3 13.2 %all-to-all-done.7 = bf16[640,2,128]{2,1,0:T(2,128)(2,1)S(1)} async-done(((bf16[640,2,128]{2,1,0:T(2,128)(2,1)}), bf16[640,2,128]{2,1,0:T(2,128)(2,1)S(1)}, u32[]{:S(2)}, u32[]{:S(2)}) %all-to-all-start.7) | async-done | bytes 327712 | tf_op jit(solution)/shard_map/all_to_all | solution.py:740
  173.6 0.3 convert_reduce_fusion
  173.9 9.0 %all-gather = f32[20,2,128]{2,1,0:T(2,128)S(1)} all-gather(f32[5,2,128]{2,1,0:T(2,128)S(1)} %convert_reduce_fusion), channel_id=2, replica_groups=mesh['zh'=4,'y'=8,'x'=4,'zl'=2,'core'=2] {'zl','core'}, dimensions={0}, use_global_device_ids=true | all-gather | bytes 25600 | tf_op jit(solution)/shard_map/all_gather | solution.py:742
  182.9 0.1 reshape.46
  183.0 0.1 reshape.47
  183.1 0.7 dynamic_slice.3
  (25 shorter events, 0.1 us)
Async XLA Ops:
  0.6 15.2 %collective-permute-start = (bf16[64,2048]{1,0:T(8,128)(2,1)}, bf16[64,2048]{1,0:T(8,128)(2,1)S(1)}, u32[]{:S(2)}, u32[]{:S(2)}) collective-permute-start(bf16[64,2048]{1,0:T(8,128)(2,1)} %own_embed_ref.3), channel_id=1, source_target_pairs={{0,2},{2,0},{1,3},{3,1},{4,6},{6,4},{5,7},{7,5},{8,10},{10,8},{9,1... | collective-permute-start | bytes 786440 | tf_op jit(solution)/shard_map/ppermute | solution.py:546
  7.5 8.3 %copy-start.1 = (bf16[64,2048]{1,0:T(8,128)(2,1)S(1)}, bf16[64,2048]{1,0:T(8,128)(2,1)}, u32[]{:S(2)}) copy-start(bf16[64,2048]{1,0:T(8,128)(2,1)} %own_embed_ref.3) | copy-start | bytes 786436
  7.5 15.7 %all-to-all-start = ((bf16[4,544,128]{2,1,0:T(8,128)(2,1)}), bf16[4,544,128]{2,1,0:T(8,128)(2,1)S(1)}, u32[]{:S(2)}, u32[]{:S(2)}) async-start(bf16[4,544,128]{2,1,0:T(8,128)(2,1)} %pack.1), calls=%async_computation | async-start | bytes 1114112 | tf_op jit(solution)/shard_map/all_to_all | solution.py:564
  15.0 0.7 copy-start.17
  15.8 2.3 %copy-start.11 = (bf16[2048,256]{1,0:T(8,128)(2,1)S(1)}, bf16[2048,256]{1,0:T(8,128)(2,1)}, u32[]{:S(2)}) copy-start(bf16[2048,256]{1,0:T(8,128)(2,1)} %value_far.1) | copy-start | bytes 3145732
  15.9 15.9 %collective-permute-start.1 = (bf16[128,2048]{1,0:T(8,128)(2,1)S(1)}, bf16[128,2048]{1,0:T(8,128)(2,1)S(1)}, u32[]{:S(2)}, u32[]{:S(2)}) collective-permute-start(bf16[128,2048]{1,0:T(8,128)(2,1)S(1)} %pad_maximum_fusion.1.pair_ref), channel_id=1, source_target_pairs={{0,1},{1,0},{2,3},{3,2},{4,5},{5,4},{6,7},{7,6},{8,9},{9,8},{10,11... | collective-permute-start | bytes 1572872 | tf_op jit(solution)/shard_map/ppermute | solution.py:590
  18.7 1.2 copy-start.13
  20.4 1.2 copy-start.15
  25.1 6.8 %copy-start.4 = (bf16[64,2048]{1,0:T(8,128)(2,1)S(1)}, bf16[64,2048]{1,0:T(8,128)(2,1)}, u32[]{:S(2)}) copy-start(bf16[64,2048]{1,0:T(8,128)(2,1)} %vocab_ref.1) | copy-start | bytes 786436
  25.1 6.8 %copy-start.8 = (bf16[2,2048]{1,0:T(2,128)(2,1)S(1)}, bf16[2,2048]{1,0:T(2,128)(2,1)}, u32[]{:S(2)}) copy-start(bf16[2,2048]{1,0:T(2,128)(2,1)} %frame_ref.1) | copy-start | bytes 24580
  25.1 6.7 %copy-start.10 = (s32[5]{0:T(128)S(1)}, s32[5]{0:T(128)}, u32[]{:S(2)}) copy-start(s32[5]{0:T(128)} %ids_ref.1) | copy-start | bytes 64
  38.2 0.9 copy-start.2
  39.1 41.9 %all-to-all-start.1 = ((bf16[1664,2,128]{2,1,0:T(2,128)(2,1)}), bf16[1664,2,128]{2,1,0:T(2,128)(2,1)S(1)}, u32[]{:S(2)}, u32[]{:S(2)}) async-start(bf16[1664,2,128]{2,1,0:T(2,128)(2,1)} %bitcast.39), calls=%async_computation.1 | async-start | bytes 1703936 | tf_op jit(solution)/shard_map/all_to_all | solution.py:629
  55.4 1.9 %copy-start.14 = (bf16[2048,256]{1,0:T(8,128)(2,1)S(1)}, bf16[2048,256]{1,0:T(8,128)(2,1)}, u32[]{:S(2)}) copy-start(bf16[2048,256]{1,0:T(8,128)(2,1)} %key_far.1) | copy-start | bytes 3145732
  57.3 1.2 copy-start.16
  58.5 1.2 copy-start.12
  61.3 19.7 %copy-start = (bf16[256,2048]{1,0:T(8,128)(2,1)S(1)}, bf16[256,2048]{1,0:T(8,128)(2,1)}, u32[]{:S(2)}) copy-start(bf16[256,2048]{1,0:T(8,128)(2,1)} %out_weight_ref.3) | copy-start | bytes 3145732
  82.8 34.7 %copy-start.3 = (bf16[2,256,768]{2,1,0:T(8,128)(2,1)S(1)}, bf16[2,256,768]{2,1,0:T(8,128)(2,1)}, u32[]{:S(2)}) copy-start(bf16[2,256,768]{2,1,0:T(8,128)(2,1)} %get-tuple-element.18.qkv_ref) | copy-start | bytes 2359300
  107.2 10.3 %all-to-all-start.4 = ((f32[4,48,128]{2,1,0:T(8,128)}), f32[4,48,128]{2,1,0:T(8,128)S(1)}, u32[]{:S(2)}, u32[]{:S(2)}) async-start(f32[4,48,128]{2,1,0:T(8,128)} %combine_zh.1), calls=%async_computation.4 | async-start | bytes 196608 | tf_op jit(solution)/shard_map/all_to_all | solution.py:685
  110.5 7.0 %copy-start.9 = (bf16[2048]{0:T(1024)(128)(2,1)S(1)}, bf16[2048]{0:T(1024)(128)(2,1)}, u32[]{:S(2)}) copy-start(bf16[2048]{0:T(1024)(128)(2,1)} %param.18) | copy-start | bytes 12292
  132.5 18.9 %copy-start.5 = (bf16[512,256]{1,0:T(8,128)(2,1)S(1)}, bf16[512,256]{1,0:T(8,128)(2,1)}, u32[]{:S(2)}) copy-start(bf16[512,256]{1,0:T(8,128)(2,1)} %get-tuple-element.25.tokens_ref) | copy-start | bytes 786436
  132.7 18.7 %copy-start.6 = (f32[64,512]{1,0:T(8,128)S(1)}, f32[64,512]{1,0:T(8,128)}, u32[]{:S(2)}) copy-start(f32[64,512]{1,0:T(8,128)} %get-tuple-element.24.slope_ref) | copy-start | bytes 393220
  132.7 18.7 %copy-start.7 = (f32[64,512]{1,0:T(8,128)S(1)}, f32[64,512]{1,0:T(8,128)}, u32[]{:S(2)}) copy-start(f32[64,512]{1,0:T(8,128)} %get-tuple-element.21.back_unit_ref) | copy-start | bytes 393220
  153.4 20.1 %all-to-all-start.7 = ((bf16[640,2,128]{2,1,0:T(2,128)(2,1)}), bf16[640,2,128]{2,1,0:T(2,128)(2,1)S(1)}, u32[]{:S(2)}, u32[]{:S(2)}) async-start(bf16[640,2,128]{2,1,0:T(2,128)(2,1)} %bitcast.15), calls=%async_computation.7 | async-start | bytes 655360 | tf_op jit(solution)/shard_map/all_to_all | solution.py:740

commit v6 on v5

--- a/solution.py
+++ b/solution.py
@@ -21,6 +21,7 @@
 VMEM_LIMIT = 40 * 1024 * 1024
 LINES = 4
 FAR = pltpu.HBM
+STORES = 4
 N_S = 4
 SPACE_OF_BLOCK = (0, 2, 1, 3)
 
@@ -157,7 +158,7 @@
         shift = row_off * cols + col_off
         if shift:
             moved = pltpu.roll(moved, shift % lanes, 1)
-        part = dot(tokens, moved.astype(BF), (((0,), (1,)), ((), ())))
+        part = dot(moved.astype(BF), tokens).T
         grad_ref[tap * channels : (tap + 1) * channels, :] = part
     count = lines_ref.shape[0]
     lines_ref[...] = jnp.concatenate(
@@ -234,11 +235,12 @@
     value_far,
     own_embed_ref,
     vocab_ref,
-    moved_ref,
+    moved_far,
     embed_sum_ref,
     scale_ref,
     back_unit_far,
     wide_ref,
+    moved_ref,
     query_ref,
     key_ref,
     value_ref,
@@ -269,6 +271,7 @@
         return jnp.concatenate([act_ref[pl.ds(i, own), at : at + tokens] for i in starts], axis=0)
 
     embed_sum = jnp.zeros((1, width), F32)
+    normed = []
     for frame in range(frames):
         at = frame * tokens
         made = dot(rows_of(core, at), pair_ref[...], TN)
@@ -277,23 +280,23 @@
         wide = embedded.astype(F32)
         embed_sum = embed_sum + jnp.sum(wide, axis=0, keepdims=True)
         scale = lax.rsqrt(jnp.mean(wide * wide, axis=1, keepdims=True) + EPSILON)
-        normed = (wide * scale * gain).astype(BF)
+        normed.append((wide * scale * gain).astype(BF))
         scale_row = jnp.broadcast_to(scale, (tokens, LANES)).T[:1]
         scale_ref[:, at : at + tokens] = scale_row
         back_unit_ref[:, at : at + tokens] = dot(own_embed_ref[...], embedded, NT) * scale_row
-        for part, weight_ref in enumerate((query_ref, key_ref, value_ref)):
-            if frame == 0:
-                fetches[part].wait()
-            made = dot(normed, weight_ref[...])
+    store = pltpu.make_async_copy(back_unit_ref, back_unit_far, done.at[3])
+    store.start()
+    embed_sum_ref[...] = embed_sum * (1.0 / N_S)
+    for part, weight_ref in enumerate((query_ref, key_ref, value_ref)):
+        fetches[part].wait()
+        for frame in range(frames):
+            made = dot(normed[frame], weight_ref[...])
             for slot in range(slots):
                 for i in range(inner // LANES):
                     chunk = slot * per + part * (inner // LANES) + i
                     wide_ref[chunk_rows(n_t, chunks, chunk, frame), :] = made[
                         slot * n_t : (slot + 1) * n_t, i * LANES : (i + 1) * LANES
                     ]
-    store = pltpu.make_async_copy(back_unit_ref, back_unit_far, done.at[3])
-    store.start()
-    embed_sum_ref[...] = embed_sum * (1.0 / N_S)
     vocab = vocab_ref.shape[0]
     ratings = ids_ref.shape[0]
     column = lax.broadcasted_iota(jnp.int32, (1, vocab), 1)
@@ -307,8 +310,17 @@
     lines.append(jnp.zeros((LANES - ratings * groups, n_t), F32))
     wide_ref[chunk_rows(n_t, chunks, chunks - 1, 0), :] = jnp.concatenate(lines, axis=0).T
     wide_ref[chunk_rows(n_t, chunks, chunks - 1, 1), :] = jnp.zeros((n_t, LANES), F32)
-    moved_ref[...] = wide_ref[...].astype(BF)
-    store.wait()
+    stores = [store]
+    block = moved_ref.shape[0] // STORES
+    for i in range(STORES):
+        rows = pl.ds(i * block, block)
+        moved_ref[rows, :] = wide_ref[rows, :].astype(BF)
+        stores.append(
+            pltpu.make_async_copy(moved_ref.at[rows], moved_far.at[rows], done.at[4 + i])
+        )
+        stores[-1].start()
+    for store in stores:
+        store.wait()
 
 
 def attention_weights(key, query):
@@ -599,16 +611,16 @@
         functools.partial(embed_kernel, n_t, slots),
         name="embed",
         out_shape=(
-            jax.ShapeDtypeStruct((n_t * chunks * 2, LANES), BF),
+            pltpu.HBM((n_t * chunks * 2, LANES), BF),
             jax.ShapeDtypeStruct((1, width), F32),
             jax.ShapeDtypeStruct((1, tokens_dev), F32),
             pltpu.HBM((own_channels, tokens_dev), F32),
         ),
         in_specs=[scalars] * 2 + [whole] * 5 + [far] * 3 + [whole] * 2,
-        out_specs=(whole,) * 3 + (far,),
-        scratch_shapes=[pltpu.VMEM((n_t * chunks * 2, LANES), F32)]
+        out_specs=(far, whole, whole, far),
+        scratch_shapes=[pltpu.VMEM((n_t * chunks * 2, LANES), kind) for kind in (F32, BF)]
         + [pltpu.VMEM((width, inner), BF)] * 3
-        + [pltpu.VMEM((own_channels, tokens_dev), F32), pltpu.SemaphoreType.DMA((4,))],
+        + [pltpu.VMEM((own_channels, tokens_dev), F32), pltpu.SemaphoreType.DMA((4 + STORES,))],
         compiler_params=params,
     )(
         place,

time: 185 us -> 184 us (level)
    unnamed x36 -> x34, local copies, waits for them, and re-layouts: 4.4 us -> 3.5 us
  transfers between devices with their start and end apart: 6 -> 6, of which waited for: 4 -> 4; matrix products, arithmetic and copies ran while one was open for 5% -> 4% of each run, Pallas kernels for 2% -> 2%
where the time goes in v6:
time: 184 us; the launch traced here: 183 us
  blocking collectives  69.5 us (38%)
  waiting for transfers between devices  41.1 us (22%)
  starting transfers between devices  40.6 us (22%)
  Pallas kernels  18.1 us (10%)
  matrix products  6.24 us (3%)
  local copies, waits for them, and re-layouts  4.88 us (3%)
    all_to_all x1, waiting for transfers between devices, on_device(): moved = lax.all_to_all(moved, T_AXES, 0, 0, tiled=True)  21 us
    all_to_all x1, blocking collectives, on_device(): lax.all_to_all(sent.reshape(n_t * LINES // 2, 2, LANES), T_AXES, 0, 0, ti...  18.7 us
    all_to_all x1, starting transfers between devices, on_device(): moved = lax.all_to_all(moved, T_AXES, 0, 0, tiled=True)  16.4 us
    all_to_all x1, waiting for transfers between devices, on_device(): sums = lax.all_to_all(sums, T_AXES, 0, 0, tiled=True)  13.3 us
    all_to_all x1, blocking collectives, on_device(): packed = lax.all_to_all(packed, ('x',) + S_AXES, 0, 0, tiled=True)  12.6 us
    all_to_all x1, blocking collectives, on_device(): sent = lax.all_to_all(sent, S_AXES, 0, 0, tiled=True)  11.3 us
    all_to_all x1, blocking collectives, on_device(): packed = lax.all_to_all(packed, axis, 0, 0, tiled=True)  11.2 us
    all_gather x1, blocking collectives, on_device(): lax.all_gather(sums, S_AXES, axis=0, tiled=False)  8.95 us
  transfers between devices with their start and end apart: 6, of which 4 were waited for; matrix products, arithmetic and copies ran while one was open for 4% of the time, Pallas kernels for 2%

profile of v6, /device:TPU:1, one launch (start us, length us, event | category | flops | bytes accessed | tf_op | source)
XLA Modules:
  0.0 182.6 jit_solution(5952008864015382238)
XLA Ops:
  0.6 4.8 %collective-permute-start = (bf16[64,2048]{1,0:T(8,128)(2,1)}, bf16[64,2048]{1,0:T(8,128)(2,1)S(1)}, u32[]{:S(2)}, u32[]{:S(2)}) collective-permute-start(bf16[64,2048]{1,0:T(8,128)(2,1)} %own_embed_ref.3), channel_id=1, source_target_pairs={{0,2},{2,0},{1,3},{3,1},{4,6},{6,4},{5,7},{7,5},{8,10},{10,8},{9,1... | collective-permute-start | bytes 786440 | tf_op jit(solution)/shard_map/ppermute | solution.py:558
  5.5 2.0 %pack.1 = bf16[4,544,128]{2,1,0:T(8,128)(2,1)} custom-call(bf16[128,256]{1,0:T(8,128)(2,1)} %bitcast.46, bf16[576,256]{1,0:T(8,128)(2,1)} %stem_far.1), custom_call_target="tpu_custom_call" | custom-call | tf_op jit(solution)/shard_map/pack/pallas_call | solution.py:563
  7.5 0.0 copy-start.1
  7.5 7.5 %all-to-all-start = ((bf16[4,544,128]{2,1,0:T(8,128)(2,1)}), bf16[4,544,128]{2,1,0:T(8,128)(2,1)S(1)}, u32[]{:S(2)}, u32[]{:S(2)}) async-start(bf16[4,544,128]{2,1,0:T(8,128)(2,1)} %pack.1), calls=%async_computation | async-start | bytes 1114112 | tf_op jit(solution)/shard_map/all_to_all | solution.py:576
  15.0 0.7 copy-done.16
  15.7 0.1 pad_add_fusion.place_ref
  15.8 0.0 collective-permute-done
  15.8 0.0 copy-done.1
  15.9 2.2 %collective-permute-start.1 = (bf16[128,2048]{1,0:T(8,128)(2,1)S(1)}, bf16[128,2048]{1,0:T(8,128)(2,1)S(1)}, u32[]{:S(2)}, u32[]{:S(2)}) collective-permute-start(bf16[128,2048]{1,0:T(8,128)(2,1)S(1)} %pad_maximum_fusion.1.pair_ref), channel_id=1, source_target_pairs={{0,1},{1,0},{2,3},{3,2},{4,5},{5,4},{6,7},{7,6},{8,9},{9,8},{10,11... | collective-permute-start | bytes 1572872 | tf_op jit(solution)/shard_map/ppermute | solution.py:602
  18.1 0.5 fusion.8
  18.6 0.0 copy-start.12
  18.6 0.5 fusion.3
  19.2 0.7 copy-done.12
  19.9 0.5 fusion.10
  20.4 0.0 copy-start.14
  20.4 0.5 fusion.4
  21.0 0.7 copy-done.14
  21.6 0.5 fusion.12
  22.2 0.5 fusion.5
  22.7 0.5 all-to-all-done.packed_ref
  23.2 1.9 %stem.1 = (bf16[64,512]{1,0:T(8,128)(2,1)S(1)}, f32[64,512]{1,0:T(8,128)}, bf16[512,256]{1,0:T(8,128)(2,1)}) custom-call(bf16[4,544,128]{2,1,0:T(8,128)(2,1)S(1)} %all-to-all-done.packed_ref), custom_call_target="tpu_custom_call" | custom-call | tf_op jit(solution)/shard_map/stem/pallas_call | solution.py:578
  25.1 0.0 copy-start.3
  25.1 0.0 copy-start.7
  25.1 0.0 copy-start.9
  25.1 6.7 %all_gather.9.act_ref = bf16[256,512]{1,0:T(8,128)(2,1)S(1)} all-gather(bf16[64,512]{1,0:T(8,128)(2,1)S(1)} %get-tuple-element.14), channel_id=1, replica_groups=mesh['zh'=4,'y'=8,'x'=4,'zl'=2,'core'=2] {'zl','core'}, dimensions={0}, use_global_device_ids=true | all-gather | bytes 327680 | tf_op jit(solution)/shard_map/all_gather | solution.py:596
  31.8 0.0 collective-permute-done.1.across_ref
  31.8 0.0 copy-done.9
  31.8 6.2 %embed.1 = (bf16[3328,128]{1,0:T(8,128)(2,1)}, f32[1,2048]{1,0:T(1,128)S(1)}, f32[1,512]{1,0:T(1,128)S(1)}, f32[64,512]{1,0:T(8,128)}) custom-call(s32[2]{0:T(128)S(1)} %pad_add_fusion.place_ref, s32[5]{0:T(128)S(1)} %copy-done.9, bf16[256,512]{1,0:T(8,128)(2,1)S(1)} %all_gather.9.act_ref, bf16[128,2048]{1,0:T(8,128)(2,1)S(1)} %pad_maximum_fusion.1.pair_ref, ...), custom_call_target="tpu_custom_call" | custom-call | tf_op jit(solution)/shard_map/embed/pallas_call | solution.py:610
  38.1 0.0 copy-start.11
  38.1 16.4 %all-to-all-start.1 = ((bf16[1664,2,128]{2,1,0:T(2,128)(2,1)}), bf16[1664,2,128]{2,1,0:T(2,128)(2,1)S(1)}, u32[]{:S(2)}, u32[]{:S(2)}) async-start(bf16[1664,2,128]{2,1,0:T(2,128)(2,1)} %bitcast.43), calls=%async_computation.1 | async-start | bytes 1703936 | tf_op jit(solution)/shard_map/all_to_all | solution.py:641
  54.5 0.0 copy-done.11
  54.5 0.0 copy-start.13
  54.5 0.5 fusion.25
  55.0 0.7 copy-done.13
  55.7 0.5 fusion.26
  56.3 0.7 copy-done.15
  57.0 0.5 fusion.27
  57.5 0.5 fusion
  58.0 0.5 fusion.1
  58.5 0.5 fusion.2
  59.0 0.1 fusion.24
  59.1 0.0 copy-start
  59.1 0.1 pad_maximum_fusion.back_ref
  59.1 21.0 %all-to-all-done.1 = bf16[1664,2,128]{2,1,0:T(2,128)(2,1)S(1)} async-done(((bf16[1664,2,128]{2,1,0:T(2,128)(2,1)}), bf16[1664,2,128]{2,1,0:T(2,128)(2,1)S(1)}, u32[]{:S(2)}, u32[]{:S(2)}) %all-to-all-start.1) | async-done | bytes 852000 | tf_op jit(solution)/shard_map/all_to_all | solution.py:641
  80.1 1.7 attend.1
  81.9 12.6 %all_to_all.40.in_ref = f32[16,24,128]{2,1,0:T(8,128)S(1)} all-to-all(f32[16,24,128]{2,1,0:T(8,128)S(1)} %get-tuple-element.17), channel_id=1, replica_groups=mesh['zh'=4,'y'=8,'x'=4,'zl'=2,'core'=2] {'x','zl','core'}, dimensions={0} | all-to-all | bytes 393216 | tf_op jit(solution)/shard_map/all_to_all | solution.py:683
  94.5 11.2 %all_to_all.41.in_ref = f32[8,24,128]{2,1,0:T(8,128)S(1)} all-to-all(f32[8,24,128]{2,1,0:T(8,128)S(1)} %combine_y.1), channel_id=1, replica_groups=mesh['zh'=4,'y'=8,'x'=4,'zl'=2,'core'=2] {'y'}, dimensions={0} | all-to-all | bytes 196608 | tf_op jit(solution)/shard_map/all_to_all | solution.py:697
  105.7 0.6 combine_zh.1
  106.3 3.3 %all-to-all-start.4 = ((f32[4,48,128]{2,1,0:T(8,128)}), f32[4,48,128]{2,1,0:T(8,128)S(1)}, u32[]{:S(2)}, u32[]{:S(2)}) async-start(f32[4,48,128]{2,1,0:T(8,128)} %combine_zh.1), calls=%async_computation.4 | async-start | bytes 196608 | tf_op jit(solution)/shard_map/all_to_all | solution.py:697
  109.6 0.0 copy-start.8
  110.3 6.3 %all-to-all-done.4.packed_ref = f32[4,48,128]{2,1,0:T(8,128)S(1)} async-done(((f32[4,48,128]{2,1,0:T(8,128)}), f32[4,48,128]{2,1,0:T(8,128)S(1)}, u32[]{:S(2)}, u32[]{:S(2)}) %all-to-all-start.4) | async-done | bytes 98336 | tf_op jit(solution)/shard_map/all_to_all | solution.py:697
  116.6 3.7 %attend_back.1 = (f32[8,128]{1,0:T(8,128)S(1)}, f32[64,128]{1,0:T(8,128)S(1)}, bf16[4,272,128]{2,1,0:T(8,128)(2,1)S(1)}) custom-call(s32[1]{0:T(128)S(6)} %copy.65.target_ref, f32[4,48,128]{2,1,0:T(8,128)S(1)} %all-to-all-done.4.packed_ref, bf16[16,128]{1,0:T(8,128)(2,1)S(1)} %bitcast.41, bf16[256,2048]{1,0:T(8,128)(2,1)S(1)} %copy-done, ...), custom_call_target="tpu_custom_call" | custom-call | tf_op jit(solution)/shard_map/attend_back/pallas_call | solution.py:699
  120.3 11.3 %all_to_all.42.in_ref = bf16[4,272,128]{2,1,0:T(8,128)(2,1)S(1)} all-to-all(bf16[4,272,128]{2,1,0:T(8,128)(2,1)S(1)} %get-tuple-element.20), channel_id=1, replica_groups=mesh['zh'=4,'y'=8,'x'=4,'zl'=2,'core'=2] {'zl','core'}, dimensions={0} | all-to-all | bytes 557056 | tf_op jit(solution)/shard_map/all_to_all | solution.py:720
  131.6 0.1 gather.1
  131.8 18.7 %all_to_all.43 = bf16[256,2,128]{2,1,0:T(2,128)(2,1)S(1)} all-to-all(bf16[256,2,128]{2,1,0:T(2,128)(2,1)S(1)} %bitcast.39), channel_id=1, replica_groups=mesh['zh'=4,'y'=8,'x'=4,'zl'=2,'core'=2] {'zh','y','x'}, dimensions={0} | all-to-all | bytes 262144 | tf_op jit(solution)/shard_map/all_to_all | solution.py:730
  150.5 1.8 stem_back.1
  152.3 6.4 %all-to-all-start.7 = ((bf16[640,2,128]{2,1,0:T(2,128)(2,1)}), bf16[640,2,128]{2,1,0:T(2,128)(2,1)S(1)}, u32[]{:S(2)}, u32[]{:S(2)}) async-start(bf16[640,2,128]{2,1,0:T(2,128)(2,1)} %bitcast.15), calls=%async_computation.7 | async-start | bytes 655360 | tf_op jit(solution)/shard_map/all_to_all | solution.py:752
  158.7 0.5 slice.6
  159.2 13.3 %all-to-all-done.7 = bf16[640,2,128]{2,1,0:T(2,128)(2,1)S(1)} async-done(((bf16[640,2,128]{2,1,0:T(2,128)(2,1)}), bf16[640,2,128]{2,1,0:T(2,128)(2,1)S(1)}, u32[]{:S(2)}, u32[]{:S(2)}) %all-to-all-start.7) | async-done | bytes 327712 | tf_op jit(solution)/shard_map/all_to_all | solution.py:752
  172.5 0.3 convert_reduce_fusion
  172.8 9.0 %all-gather = f32[20,2,128]{2,1,0:T(2,128)S(1)} all-gather(f32[5,2,128]{2,1,0:T(2,128)S(1)} %convert_reduce_fusion), channel_id=2, replica_groups=mesh['zh'=4,'y'=8,'x'=4,'zl'=2,'core'=2] {'zl','core'}, dimensions={0}, use_global_device_ids=true | all-gather | bytes 25600 | tf_op jit(solution)/shard_map/all_gather | solution.py:754
  181.8 0.1 reshape.46
  181.9 0.1 reshape.47
  182.0 0.7 dynamic_slice.3
  (23 shorter events, 0.2 us)
Async XLA Ops:
  0.6 15.2 %collective-permute-start = (bf16[64,2048]{1,0:T(8,128)(2,1)}, bf16[64,2048]{1,0:T(8,128)(2,1)S(1)}, u32[]{:S(2)}, u32[]{:S(2)}) collective-permute-start(bf16[64,2048]{1,0:T(8,128)(2,1)} %own_embed_ref.3), channel_id=1, source_target_pairs={{0,2},{2,0},{1,3},{3,1},{4,6},{6,4},{5,7},{7,5},{8,10},{10,8},{9,1... | collective-permute-start | bytes 786440 | tf_op jit(solution)/shard_map/ppermute | solution.py:558
  7.5 8.3 %copy-start.1 = (bf16[64,2048]{1,0:T(8,128)(2,1)S(1)}, bf16[64,2048]{1,0:T(8,128)(2,1)}, u32[]{:S(2)}) copy-start(bf16[64,2048]{1,0:T(8,128)(2,1)} %own_embed_ref.3) | copy-start | bytes 786436
  7.5 15.7 %all-to-all-start = ((bf16[4,544,128]{2,1,0:T(8,128)(2,1)}), bf16[4,544,128]{2,1,0:T(8,128)(2,1)S(1)}, u32[]{:S(2)}, u32[]{:S(2)}) async-start(bf16[4,544,128]{2,1,0:T(8,128)(2,1)} %pack.1), calls=%async_computation | async-start | bytes 1114112 | tf_op jit(solution)/shard_map/all_to_all | solution.py:576
  15.0 0.7 copy-start.16
  15.8 2.3 %copy-start.10 = (bf16[2048,256]{1,0:T(8,128)(2,1)S(1)}, bf16[2048,256]{1,0:T(8,128)(2,1)}, u32[]{:S(2)}) copy-start(bf16[2048,256]{1,0:T(8,128)(2,1)} %value_far.1) | copy-start | bytes 3145732
  15.9 15.9 %collective-permute-start.1 = (bf16[128,2048]{1,0:T(8,128)(2,1)S(1)}, bf16[128,2048]{1,0:T(8,128)(2,1)S(1)}, u32[]{:S(2)}, u32[]{:S(2)}) collective-permute-start(bf16[128,2048]{1,0:T(8,128)(2,1)S(1)} %pad_maximum_fusion.1.pair_ref), channel_id=1, source_target_pairs={{0,1},{1,0},{2,3},{3,2},{4,5},{5,4},{6,7},{7,6},{8,9},{9,8},{10,11... | collective-permute-start | bytes 1572872 | tf_op jit(solution)/shard_map/ppermute | solution.py:602
  18.6 1.2 copy-start.12
  20.4 1.2 copy-start.14
  25.1 6.8 %copy-start.3 = (bf16[64,2048]{1,0:T(8,128)(2,1)S(1)}, bf16[64,2048]{1,0:T(8,128)(2,1)}, u32[]{:S(2)}) copy-start(bf16[64,2048]{1,0:T(8,128)(2,1)} %vocab_ref.1) | copy-start | bytes 786436
  25.1 6.7 %copy-start.7 = (bf16[2,2048]{1,0:T(2,128)(2,1)S(1)}, bf16[2,2048]{1,0:T(2,128)(2,1)}, u32[]{:S(2)}) copy-start(bf16[2,2048]{1,0:T(2,128)(2,1)} %frame_ref.1) | copy-start | bytes 24580
  25.1 6.7 %copy-start.9 = (s32[5]{0:T(128)S(1)}, s32[5]{0:T(128)}, u32[]{:S(2)}) copy-start(s32[5]{0:T(128)} %ids_ref.1) | copy-start | bytes 64
  38.1 16.4 %copy-start.11 = (bf16[2048,256]{1,0:T(8,128)(2,1)S(1)}, bf16[2048,256]{1,0:T(8,128)(2,1)}, u32[]{:S(2)}) copy-start(bf16[2048,256]{1,0:T(8,128)(2,1)} %value_far.1) | copy-start | bytes 3145732
  38.1 42.1 %all-to-all-start.1 = ((bf16[1664,2,128]{2,1,0:T(2,128)(2,1)}), bf16[1664,2,128]{2,1,0:T(2,128)(2,1)S(1)}, u32[]{:S(2)}, u32[]{:S(2)}) async-start(bf16[1664,2,128]{2,1,0:T(2,128)(2,1)} %bitcast.43), calls=%async_computation.1 | async-start | bytes 1703936 | tf_op jit(solution)/shard_map/all_to_all | solution.py:641
  54.5 1.2 copy-start.13
  55.7 1.2 copy-start.15
  59.1 21.1 %copy-start = (bf16[256,2048]{1,0:T(8,128)(2,1)S(1)}, bf16[256,2048]{1,0:T(8,128)(2,1)}, u32[]{:S(2)}) copy-start(bf16[256,2048]{1,0:T(8,128)(2,1)} %out_weight_ref.3) | copy-start | bytes 3145732
  81.9 34.8 %copy-start.2 = (bf16[2,256,768]{2,1,0:T(8,128)(2,1)S(1)}, bf16[2,256,768]{2,1,0:T(8,128)(2,1)}, u32[]{:S(2)}) copy-start(bf16[2,256,768]{2,1,0:T(8,128)(2,1)} %get-tuple-element.18.qkv_ref) | copy-start | bytes 2359300
  106.3 10.3 %all-to-all-start.4 = ((f32[4,48,128]{2,1,0:T(8,128)}), f32[4,48,128]{2,1,0:T(8,128)S(1)}, u32[]{:S(2)}, u32[]{:S(2)}) async-start(f32[4,48,128]{2,1,0:T(8,128)} %combine_zh.1), calls=%async_computation.4 | async-start | bytes 196608 | tf_op jit(solution)/shard_map/all_to_all | solution.py:697
  109.6 7.0 %copy-start.8 = (bf16[2048]{0:T(1024)(128)(2,1)S(1)}, bf16[2048]{0:T(1024)(128)(2,1)}, u32[]{:S(2)}) copy-start(bf16[2048]{0:T(1024)(128)(2,1)} %param.18) | copy-start | bytes 12292
  131.6 18.9 %copy-start.4 = (bf16[512,256]{1,0:T(8,128)(2,1)S(1)}, bf16[512,256]{1,0:T(8,128)(2,1)}, u32[]{:S(2)}) copy-start(bf16[512,256]{1,0:T(8,128)(2,1)} %get-tuple-element.25.tokens_ref) | copy-start | bytes 786436
  131.8 18.7 %copy-start.5 = (f32[64,512]{1,0:T(8,128)S(1)}, f32[64,512]{1,0:T(8,128)}, u32[]{:S(2)}) copy-start(f32[64,512]{1,0:T(8,128)} %get-tuple-element.24.slope_ref) | copy-start | bytes 393220
  131.8 18.7 %copy-start.6 = (f32[64,512]{1,0:T(8,128)S(1)}, f32[64,512]{1,0:T(8,128)}, u32[]{:S(2)}) copy-start(f32[64,512]{1,0:T(8,128)} %get-tuple-element.21.back_unit_ref) | copy-start | bytes 393220
  152.3 20.1 %all-to-all-start.7 = ((bf16[640,2,128]{2,1,0:T(2,128)(2,1)}), bf16[640,2,128]{2,1,0:T(2,128)(2,1)S(1)}, u32[]{:S(2)}, u32[]{:S(2)}) async-start(bf16[640,2,128]{2,1,0:T(2,128)(2,1)} %bitcast.15), calls=%async_computation.7 | async-start | bytes 655360 | tf_op jit(solution)/shard_map/all_to_all | solution.py:752

commit v7 on v6

--- a/solution.py
+++ b/solution.py
@@ -555,7 +555,6 @@
     whole = pl.BlockSpec(memory_space=pltpu.VMEM)
     far = pl.BlockSpec(memory_space=FAR)
     params = pltpu.CompilerParams(vmem_limit_bytes=VMEM_LIMIT)
-    other = lax.ppermute(embed_weight, "zl", [(0, 1), (1, 0)])
 
     patch_rows = patches.reshape(-1, channels)
     stem_half = stem_weight.shape[0] // 2
@@ -573,7 +572,9 @@
         ],
         compiler_params=params,
     )(kept(patch_rows), kept(stem_weight))
+    packed, sent_embed = lax.optimization_barrier((packed, embed_weight))
     packed = lax.all_to_all(packed, S_AXES, 0, 0, tiled=True)
+    other = lax.ppermute(sent_embed, "zl", [(0, 1), (1, 0)])
 
     act, gelu_slope, patch_tokens = pl.pallas_call(
         functools.partial(stem_kernel, cols, count_rows),

time: 184 us -> 186 us (1.011)
  starting transfers between devices: 40.6 us -> 43.2 us
  transfers between devices with their start and end apart: 6 -> 6, of which waited for: 4 -> 3; matrix products, arithmetic and copies ran while one was open for 4% -> 4% of each run, Pallas kernels for 2% -> 1%
where the time goes in v7:
time: 186 us; the launch traced here: 185 us
  blocking collectives  69.3 us (37%)
  starting transfers between devices  43.2 us (23%)
  waiting for transfers between devices  40.8 us (22%)
  Pallas kernels  18.1 us (10%)
  matrix products  6.24 us (3%)
  local copies, waits for them, and re-layouts  4.88 us (3%)
    all_to_all x1, waiting for transfers between devices, on_device(): moved = lax.all_to_all(moved, T_AXES, 0, 0, tiled=True)  21.1 us
    all_to_all x1, blocking collectives, on_device(): lax.all_to_all(sent.reshape(n_t * LINES // 2, 2, LANES), T_AXES, 0, 0, ti...  18.7 us
    all_to_all x1, starting transfers between devices, on_device(): moved = lax.all_to_all(moved, T_AXES, 0, 0, tiled=True)  17.4 us
    all_to_all x1, blocking collectives, on_device(): packed = lax.all_to_all(packed, ('x',) + S_AXES, 0, 0, tiled=True)  13.4 us
    all_to_all x1, waiting for transfers between devices, on_device(): sums = lax.all_to_all(sums, T_AXES, 0, 0, tiled=True)  13.3 us
    all_to_all x1, blocking collectives, on_device(): sent = lax.all_to_all(sent, S_AXES, 0, 0, tiled=True)  11.3 us
    all_to_all x1, blocking collectives, on_device(): packed = lax.all_to_all(packed, axis, 0, 0, tiled=True)  10.9 us
    all_gather x1, blocking collectives, on_device(): lax.all_gather(sums, S_AXES, axis=0, tiled=False)  8.96 us
  transfers between devices with their start and end apart: 6, of which 3 were waited for; matrix products, arithmetic and copies ran while one was open for 4% of the time, Pallas kernels for 1%

profile of v7, /device:TPU:1, one launch (start us, length us, event | category | flops | bytes accessed | tf_op | source)
XLA Modules:
  0.0 184.8 jit_solution(1934560631242153963)
XLA Ops:
  0.6 0.0 copy-start.1
  0.6 2.0 %pack.1 = bf16[4,544,128]{2,1,0:T(8,128)(2,1)} custom-call(bf16[128,256]{1,0:T(8,128)(2,1)} %bitcast.46, bf16[576,256]{1,0:T(8,128)(2,1)} %stem_far.1), custom_call_target="tpu_custom_call" | custom-call | tf_op jit(solution)/shard_map/pack/pallas_call | solution.py:562
  2.7 4.8 %collective-permute-start = (bf16[64,2048]{1,0:T(8,128)(2,1)S(1)}, bf16[64,2048]{1,0:T(8,128)(2,1)S(1)}, u32[]{:S(2)}, u32[]{:S(2)}) collective-permute-start(bf16[64,2048]{1,0:T(8,128)(2,1)S(1)} %copy-done.1), channel_id=1, source_target_pairs={{0,2},{2,0},{1,3},{3,1},{4,6},{6,4},{5,7},{7,5},{8,10},{10,8},{9,1... | collective-permute-start | bytes 786440 | tf_op jit(solution)/shard_map/ppermute | solution.py:577
  7.5 7.4 %all-to-all-start = ((bf16[4,544,128]{2,1,0:T(8,128)(2,1)}), bf16[4,544,128]{2,1,0:T(8,128)(2,1)S(1)}, u32[]{:S(2)}, u32[]{:S(2)}) async-start(bf16[4,544,128]{2,1,0:T(8,128)(2,1)} %pack.1), calls=%async_computation | async-start | bytes 1114112 | tf_op jit(solution)/shard_map/all_to_all | solution.py:576
  14.9 0.7 copy-done.16
  15.6 0.1 pad_add_fusion.place_ref
  15.7 0.0 collective-permute-done
  15.8 4.0 %collective-permute-start.1 = (bf16[128,2048]{1,0:T(8,128)(2,1)S(1)}, bf16[128,2048]{1,0:T(8,128)(2,1)S(1)}, u32[]{:S(2)}, u32[]{:S(2)}) collective-permute-start(bf16[128,2048]{1,0:T(8,128)(2,1)S(1)} %pad_maximum_fusion.1.pair_ref), channel_id=1, source_target_pairs={{0,1},{1,0},{2,3},{3,2},{4,5},{5,4},{6,7},{7,6},{8,9},{9,8},{10,11... | collective-permute-start | bytes 1572872 | tf_op jit(solution)/shard_map/ppermute | solution.py:603
  19.8 0.5 fusion.8
  20.4 0.0 copy-start.12
  20.4 0.5 fusion.3
  20.9 0.7 copy-done.12
  21.6 0.5 fusion.10
  22.1 0.0 copy-start.14
  22.1 0.5 fusion.4
  22.7 0.7 copy-done.14
  23.4 0.5 fusion.12
  23.9 0.5 fusion.5
  24.4 0.0 all-to-all-done.packed_ref
  24.4 1.9 %stem.1 = (bf16[64,512]{1,0:T(8,128)(2,1)S(1)}, f32[64,512]{1,0:T(8,128)}, bf16[512,256]{1,0:T(8,128)(2,1)}) custom-call(bf16[4,544,128]{2,1,0:T(8,128)(2,1)S(1)} %all-to-all-done.packed_ref), custom_call_target="tpu_custom_call" | custom-call | tf_op jit(solution)/shard_map/stem/pallas_call | solution.py:579
  26.3 0.0 copy-start.3
  26.3 0.0 copy-start.7
  26.3 0.0 copy-start.9
  26.3 6.0 %all_gather.9.act_ref = bf16[256,512]{1,0:T(8,128)(2,1)S(1)} all-gather(bf16[64,512]{1,0:T(8,128)(2,1)S(1)} %get-tuple-element.17), channel_id=1, replica_groups=mesh['zh'=4,'y'=8,'x'=4,'zl'=2,'core'=2] {'zl','core'}, dimensions={0}, use_global_device_ids=true | all-gather | bytes 327680 | tf_op jit(solution)/shard_map/all_gather | solution.py:597
  32.3 0.0 collective-permute-done.1.across_ref
  32.3 0.0 copy-done.7
  32.3 6.2 %embed.1 = (bf16[3328,128]{1,0:T(8,128)(2,1)}, f32[1,2048]{1,0:T(1,128)S(1)}, f32[1,512]{1,0:T(1,128)S(1)}, f32[64,512]{1,0:T(8,128)}) custom-call(s32[2]{0:T(128)S(1)} %pad_add_fusion.place_ref, s32[5]{0:T(128)S(1)} %copy-done.9, bf16[256,512]{1,0:T(8,128)(2,1)S(1)} %all_gather.9.act_ref, bf16[128,2048]{1,0:T(8,128)(2,1)S(1)} %pad_maximum_fusion.1.pair_ref, ...), custom_call_target="tpu_custom_call" | custom-call | tf_op jit(solution)/shard_map/embed/pallas_call | solution.py:611
  38.6 0.0 copy-start.11
  38.6 17.4 %all-to-all-start.1 = ((bf16[1664,2,128]{2,1,0:T(2,128)(2,1)}), bf16[1664,2,128]{2,1,0:T(2,128)(2,1)S(1)}, u32[]{:S(2)}, u32[]{:S(2)}) async-start(bf16[1664,2,128]{2,1,0:T(2,128)(2,1)} %bitcast.43), calls=%async_computation.1 | async-start | bytes 1703936 | tf_op jit(solution)/shard_map/all_to_all | solution.py:642
  55.9 0.0 copy-start.13
  56.0 0.5 fusion.25
  56.5 0.7 copy-done.13
  57.2 0.5 fusion.26
  57.7 0.7 copy-done.15
  58.4 0.5 fusion.27
  58.9 0.5 fusion
  59.4 0.5 fusion.1
  59.9 0.5 fusion.2
  60.4 0.1 fusion.24
  60.5 0.0 copy-start
  60.5 0.1 pad_maximum_fusion.back_ref
  60.6 21.1 %all-to-all-done.1 = bf16[1664,2,128]{2,1,0:T(2,128)(2,1)S(1)} async-done(((bf16[1664,2,128]{2,1,0:T(2,128)(2,1)}), bf16[1664,2,128]{2,1,0:T(2,128)(2,1)S(1)}, u32[]{:S(2)}, u32[]{:S(2)}) %all-to-all-start.1) | async-done | bytes 852000 | tf_op jit(solution)/shard_map/all_to_all | solution.py:642
  81.7 1.7 attend.1
  83.5 13.4 %all_to_all.40.in_ref = f32[16,24,128]{2,1,0:T(8,128)S(1)} all-to-all(f32[16,24,128]{2,1,0:T(8,128)S(1)} %get-tuple-element.21), channel_id=1, replica_groups=mesh['zh'=4,'y'=8,'x'=4,'zl'=2,'core'=2] {'x','zl','core'}, dimensions={0} | all-to-all | bytes 393216 | tf_op jit(solution)/shard_map/all_to_all | solution.py:684
  96.9 10.9 %all_to_all.41.in_ref = f32[8,24,128]{2,1,0:T(8,128)S(1)} all-to-all(f32[8,24,128]{2,1,0:T(8,128)S(1)} %combine_y.1), channel_id=1, replica_groups=mesh['zh'=4,'y'=8,'x'=4,'zl'=2,'core'=2] {'y'}, dimensions={0} | all-to-all | bytes 196608 | tf_op jit(solution)/shard_map/all_to_all | solution.py:698
  107.9 0.6 combine_zh.1
  108.5 3.3 %all-to-all-start.4 = ((f32[4,48,128]{2,1,0:T(8,128)}), f32[4,48,128]{2,1,0:T(8,128)S(1)}, u32[]{:S(2)}, u32[]{:S(2)}) async-start(f32[4,48,128]{2,1,0:T(8,128)} %combine_zh.1), calls=%async_computation.4 | async-start | bytes 196608 | tf_op jit(solution)/shard_map/all_to_all | solution.py:698
  111.8 0.0 copy-start.8
  112.5 6.3 %all-to-all-done.4.packed_ref = f32[4,48,128]{2,1,0:T(8,128)S(1)} async-done(((f32[4,48,128]{2,1,0:T(8,128)}), f32[4,48,128]{2,1,0:T(8,128)S(1)}, u32[]{:S(2)}, u32[]{:S(2)}) %all-to-all-start.4) | async-done | bytes 98336 | tf_op jit(solution)/shard_map/all_to_all | solution.py:698
  118.8 0.0 copy-done.2
  118.8 3.7 %attend_back.1 = (f32[8,128]{1,0:T(8,128)S(1)}, f32[64,128]{1,0:T(8,128)S(1)}, bf16[4,272,128]{2,1,0:T(8,128)(2,1)S(1)}) custom-call(s32[1]{0:T(128)S(6)} %copy.65.target_ref, f32[4,48,128]{2,1,0:T(8,128)S(1)} %all-to-all-done.4.packed_ref, bf16[16,128]{1,0:T(8,128)(2,1)S(1)} %bitcast.41, bf16[256,2048]{1,0:T(8,128)(2,1)S(1)} %copy-done, ...), custom_call_target="tpu_custom_call" | custom-call | tf_op jit(solution)/shard_map/attend_back/pallas_call | solution.py:700
  122.5 11.3 %all_to_all.42.in_ref = bf16[4,272,128]{2,1,0:T(8,128)(2,1)S(1)} all-to-all(bf16[4,272,128]{2,1,0:T(8,128)(2,1)S(1)} %get-tuple-element.24), channel_id=1, replica_groups=mesh['zh'=4,'y'=8,'x'=4,'zl'=2,'core'=2] {'zl','core'}, dimensions={0} | all-to-all | bytes 557056 | tf_op jit(solution)/shard_map/all_to_all | solution.py:721
  133.8 0.1 gather.1
  134.0 18.7 %all_to_all.43 = bf16[256,2,128]{2,1,0:T(2,128)(2,1)S(1)} all-to-all(bf16[256,2,128]{2,1,0:T(2,128)(2,1)S(1)} %bitcast.39), channel_id=1, replica_groups=mesh['zh'=4,'y'=8,'x'=4,'zl'=2,'core'=2] {'zh','y','x'}, dimensions={0} | all-to-all | bytes 262144 | tf_op jit(solution)/shard_map/all_to_all | solution.py:731
  152.7 0.0 copy-done.6
  152.7 1.8 stem_back.1
  154.5 6.4 %all-to-all-start.7 = ((bf16[640,2,128]{2,1,0:T(2,128)(2,1)}), bf16[640,2,128]{2,1,0:T(2,128)(2,1)S(1)}, u32[]{:S(2)}, u32[]{:S(2)}) async-start(bf16[640,2,128]{2,1,0:T(2,128)(2,1)} %bitcast.15), calls=%async_computation.7 | async-start | bytes 655360 | tf_op jit(solution)/shard_map/all_to_all | solution.py:753
  160.9 0.5 slice.6
  161.4 13.3 %all-to-all-done.7 = bf16[640,2,128]{2,1,0:T(2,128)(2,1)S(1)} async-done(((bf16[640,2,128]{2,1,0:T(2,128)(2,1)}), bf16[640,2,128]{2,1,0:T(2,128)(2,1)S(1)}, u32[]{:S(2)}, u32[]{:S(2)}) %all-to-all-start.7) | async-done | bytes 327712 | tf_op jit(solution)/shard_map/all_to_all | solution.py:753
  174.7 0.3 convert_reduce_fusion
  175.0 9.0 %all-gather = f32[20,2,128]{2,1,0:T(2,128)S(1)} all-gather(f32[5,2,128]{2,1,0:T(2,128)S(1)} %convert_reduce_fusion), channel_id=2, replica_groups=mesh['zh'=4,'y'=8,'x'=4,'zl'=2,'core'=2] {'zl','core'}, dimensions={0}, use_global_device_ids=true | all-gather | bytes 25600 | tf_op jit(solution)/shard_map/all_gather | solution.py:755
  184.0 0.1 reshape.46
  184.1 0.1 reshape.47
  184.1 0.7 dynamic_slice.3
  (23 shorter events, 0.2 us)
Async XLA Ops:
  0.6 2.1 %copy-start.1 = (bf16[64,2048]{1,0:T(8,128)(2,1)S(1)}, bf16[64,2048]{1,0:T(8,128)(2,1)}, u32[]{:S(2)}) copy-start(bf16[64,2048]{1,0:T(8,128)(2,1)} %own_embed_ref.3) | copy-start | bytes 786436
  2.7 13.0 %collective-permute-start = (bf16[64,2048]{1,0:T(8,128)(2,1)S(1)}, bf16[64,2048]{1,0:T(8,128)(2,1)S(1)}, u32[]{:S(2)}, u32[]{:S(2)}) collective-permute-start(bf16[64,2048]{1,0:T(8,128)(2,1)S(1)} %copy-done.1), channel_id=1, source_target_pairs={{0,2},{2,0},{1,3},{3,1},{4,6},{6,4},{5,7},{7,5},{8,10},{10,8},{9,1... | collective-permute-start | bytes 786440 | tf_op jit(solution)/shard_map/ppermute | solution.py:577
  7.5 16.9 %all-to-all-start = ((bf16[4,544,128]{2,1,0:T(8,128)(2,1)}), bf16[4,544,128]{2,1,0:T(8,128)(2,1)S(1)}, u32[]{:S(2)}, u32[]{:S(2)}) async-start(bf16[4,544,128]{2,1,0:T(8,128)(2,1)} %pack.1), calls=%async_computation | async-start | bytes 1114112 | tf_op jit(solution)/shard_map/all_to_all | solution.py:576
  14.9 0.7 copy-start.16
  15.7 4.1 %copy-start.10 = (bf16[2048,256]{1,0:T(8,128)(2,1)S(1)}, bf16[2048,256]{1,0:T(8,128)(2,1)}, u32[]{:S(2)}) copy-start(bf16[2048,256]{1,0:T(8,128)(2,1)} %value_far.1) | copy-start | bytes 3145732
  15.8 16.5 %collective-permute-start.1 = (bf16[128,2048]{1,0:T(8,128)(2,1)S(1)}, bf16[128,2048]{1,0:T(8,128)(2,1)S(1)}, u32[]{:S(2)}, u32[]{:S(2)}) collective-permute-start(bf16[128,2048]{1,0:T(8,128)(2,1)S(1)} %pad_maximum_fusion.1.pair_ref), channel_id=1, source_target_pairs={{0,1},{1,0},{2,3},{3,2},{4,5},{5,4},{6,7},{7,6},{8,9},{9,8},{10,11... | collective-permute-start | bytes 1572872 | tf_op jit(solution)/shard_map/ppermute | solution.py:603
  20.4 1.2 copy-start.12
  22.1 1.2 copy-start.14
  26.3 6.0 %copy-start.3 = (bf16[64,2048]{1,0:T(8,128)(2,1)S(1)}, bf16[64,2048]{1,0:T(8,128)(2,1)}, u32[]{:S(2)}) copy-start(bf16[64,2048]{1,0:T(8,128)(2,1)} %vocab_ref.1) | copy-start | bytes 786436
  26.3 6.0 %copy-start.7 = (bf16[2,2048]{1,0:T(2,128)(2,1)S(1)}, bf16[2,2048]{1,0:T(2,128)(2,1)}, u32[]{:S(2)}) copy-start(bf16[2,2048]{1,0:T(2,128)(2,1)} %frame_ref.1) | copy-start | bytes 24580
  26.3 6.0 %copy-start.9 = (s32[5]{0:T(128)S(1)}, s32[5]{0:T(128)}, u32[]{:S(2)}) copy-start(s32[5]{0:T(128)} %ids_ref.1) | copy-start | bytes 64
  38.6 17.4 %copy-start.11 = (bf16[2048,256]{1,0:T(8,128)(2,1)S(1)}, bf16[2048,256]{1,0:T(8,128)(2,1)}, u32[]{:S(2)}) copy-start(bf16[2048,256]{1,0:T(8,128)(2,1)} %value_far.1) | copy-start | bytes 3145732
  38.6 43.1 %all-to-all-start.1 = ((bf16[1664,2,128]{2,1,0:T(2,128)(2,1)}), bf16[1664,2,128]{2,1,0:T(2,128)(2,1)S(1)}, u32[]{:S(2)}, u32[]{:S(2)}) async-start(bf16[1664,2,128]{2,1,0:T(2,128)(2,1)} %bitcast.43), calls=%async_computation.1 | async-start | bytes 1703936 | tf_op jit(solution)/shard_map/all_to_all | solution.py:642
  55.9 1.2 copy-start.13
  57.2 1.2 copy-start.15
  60.5 21.2 %copy-start = (bf16[256,2048]{1,0:T(8,128)(2,1)S(1)}, bf16[256,2048]{1,0:T(8,128)(2,1)}, u32[]{:S(2)}) copy-start(bf16[256,2048]{1,0:T(8,128)(2,1)} %out_weight_ref.3) | copy-start | bytes 3145732
  83.5 35.4 %copy-start.2 = (bf16[2,256,768]{2,1,0:T(8,128)(2,1)S(1)}, bf16[2,256,768]{2,1,0:T(8,128)(2,1)}, u32[]{:S(2)}) copy-start(bf16[2,256,768]{2,1,0:T(8,128)(2,1)} %get-tuple-element.22.qkv_ref) | copy-start | bytes 2359300
  108.5 10.3 %all-to-all-start.4 = ((f32[4,48,128]{2,1,0:T(8,128)}), f32[4,48,128]{2,1,0:T(8,128)S(1)}, u32[]{:S(2)}, u32[]{:S(2)}) async-start(f32[4,48,128]{2,1,0:T(8,128)} %combine_zh.1), calls=%async_computation.4 | async-start | bytes 196608 | tf_op jit(solution)/shard_map/all_to_all | solution.py:698
  111.8 7.0 %copy-start.8 = (bf16[2048]{0:T(1024)(128)(2,1)S(1)}, bf16[2048]{0:T(1024)(128)(2,1)}, u32[]{:S(2)}) copy-start(bf16[2048]{0:T(1024)(128)(2,1)} %param.18) | copy-start | bytes 12292
  133.8 18.9 %copy-start.4 = (bf16[512,256]{1,0:T(8,128)(2,1)S(1)}, bf16[512,256]{1,0:T(8,128)(2,1)}, u32[]{:S(2)}) copy-start(bf16[512,256]{1,0:T(8,128)(2,1)} %get-tuple-element.29.tokens_ref) | copy-start | bytes 786436
  134.0 18.7 %copy-start.5 = (f32[64,512]{1,0:T(8,128)S(1)}, f32[64,512]{1,0:T(8,128)}, u32[]{:S(2)}) copy-start(f32[64,512]{1,0:T(8,128)} %get-tuple-element.28.slope_ref) | copy-start | bytes 393220
  134.0 18.7 %copy-start.6 = (f32[64,512]{1,0:T(8,128)S(1)}, f32[64,512]{1,0:T(8,128)}, u32[]{:S(2)}) copy-start(f32[64,512]{1,0:T(8,128)} %get-tuple-element.25.back_unit_ref) | copy-start | bytes 393220
  154.5 20.1 %all-to-all-start.7 = ((bf16[640,2,128]{2,1,0:T(2,128)(2,1)}), bf16[640,2,128]{2,1,0:T(2,128)(2,1)S(1)}, u32[]{:S(2)}, u32[]{:S(2)}) async-start(bf16[640,2,128]{2,1,0:T(2,128)(2,1)} %bitcast.15), calls=%async_computation.7 | async-start | bytes 655360 | tf_op jit(solution)/shard_map/all_to_all | solution.py:753
